TPU v7x, 128 devices: a whole 4x4x4 slice. The times are simulated.
128 devices in a mesh: shard: 16 (over y, z_hi, core), ctx: 8 (over x, z_lo).
Axes of the slice: x: 4, y: 4, z: 4 (z_hi: 2, z_lo: 2; z = z_hi * 2 + z_lo), core: 2. Of those that a mesh axis runs over, the one named last changes fastest.
Arguments:
- tokens: bfloat16 [16, 1024, 1024], P('shard', 'ctx'), may hold values from -6 to 6
- positions: int32 [16, 1024], P('shard', 'ctx'), may hold values from 0 to 3069, as said below
- attn_gain: bfloat16 [1024], P('shard'), may hold values from 0.099609375 to 1.8984375
- query_weight: bfloat16 [1024, 2048], P('shard'), may hold values from -0.1875 to 0.1875
- key_matrix: bfloat16 [1024, 1024], P('shard'), may hold values from -0.1875 to 0.1875
- value_matrix: bfloat16 [1024, 1024], P('shard'), may hold values from -0.1875 to 0.1875
- query_gain: bfloat16 [128], P('shard'), may hold values from 0.099609375 to 1.8984375
- key_gain: bfloat16 [128], P('shard'), may hold values from 0.099609375 to 1.8984375
- out_weight: bfloat16 [2048, 1024], P('shard'), may hold values from -0.5 to 0.5
- mlp_gain: bfloat16 [1024], P('shard'), may hold values from 0.099609375 to 1.8984375
- gate_weight: bfloat16 [1024, 3072], P('shard'), may hold values from -0.1875 to 0.1875
- up_weight: bfloat16 [1024, 3072], P('shard'), may hold values from -0.1875 to 0.1875
- down_weight: bfloat16 [3072, 1024], P('shard'), may hold values from -0.109375 to 0.109375
- cotangent: bfloat16 [16, 1024, 1024], P('shard', 'ctx'), may hold values from -6 to 6
Outputs:
- output: bfloat16 [16, 1024, 1024], P('shard', 'ctx')
- input_grad: float32 [16, 1024, 1024], P('shard', 'ctx')
- attn_gain_grad: float32 [1024], P('shard')
- query_weight_grad: float32 [1024, 2048], P('shard')
- key_weight_grad: float32 [1024, 1024], P('shard')
- value_weight_grad: float32 [1024, 1024], P('shard')
- query_gain_grad: float32 [128], P('shard')
- key_gain_grad: float32 [128], P('shard')
- out_weight_grad: float32 [2048, 1024], P('shard')
- mlp_gain_grad: float32 [1024], P('shard')
- gate_weight_grad: float32 [1024, 3072], P('shard')
- up_weight_grad: float32 [1024, 3072], P('shard')
- down_weight_grad: float32 [3072, 1024], P('shard')
Inputs may be any that keep to these rules, and one draw needn't show every extreme that they name: Each row of positions starts at 0 and rises by 1, 2 or 3 from one token to the next; the last row rises by 3 throughout and ends at 3069.
All inputs are finite; a program needn't handle non-finite values.
Results may differ from a plain program's by a relative error of at most 0.025.
Values may be sent and summed in bfloat16 or wider, within the bound.
A program may use at most 192 MiB of HBM per device.

v0:
```python
import jax
import jax.numpy as jnp
from jax import lax
from jax.sharding import PartitionSpec as P

QUERY_HEADS = 16
SHARED_KV_GROUPS = 8
PER_HEAD_DIM = 128


EPSILON = 1e-06
ROPE_BASE = 1000000.0
BLOCKED_SCORE = -1e30


def rms_parts(values):
    inverse = lax.rsqrt(jnp.mean(values * values, -1, keepdims=True) + EPSILON)
    return (values * inverse, inverse)


def rms_back(grad_normed, normed_input, inverse):
    return inverse * (
        grad_normed - normed_input * jnp.mean(grad_normed * normed_input, -1, keepdims=True)
    )


def rotary_tables(positions_row):
    half_dim = PER_HEAD_DIM // 2
    freq = jnp.power(ROPE_BASE, -jnp.arange(half_dim, dtype=jnp.float32) * (2.0 / PER_HEAD_DIM))
    angle = positions_row.astype(jnp.float32)[:, None] * freq[None, :]
    cos_half = jnp.cos(angle)
    sin_half = jnp.sin(angle)
    return (jnp.concatenate([cos_half, cos_half], -1), jnp.concatenate([sin_half, sin_half], -1))


def rotate(values, cosine_table, sine_table):
    half_dim = values.shape[-1] // 2
    turned = jnp.concatenate([-values[..., half_dim:], values[..., :half_dim]], -1)
    return values * cosine_table[:, None, :] + turned * sine_table[:, None, :]


def rotate_reverse(grads, cosine_table, sine_table):
    half_dim = grads.shape[-1] // 2
    turned_in = grads * sine_table[:, None, :]
    return grads * cosine_table[:, None, :] + jnp.concatenate(
        [turned_in[..., half_dim:], -turned_in[..., :half_dim]], -1
    )


def shards(
    tokens,
    positions,
    attn_gain,
    query_weight,
    key_matrix,
    value_matrix,
    query_gain,
    key_gain,
    out_weight,
    mlp_gain,
    gate_weight,
    up_weight,
    down_weight,
    cotangent,
):
    gathered = (
        lax.all_gather(attn_gain, "shard", axis=0, tiled=True),
        lax.all_gather(query_weight, "shard", axis=0, tiled=True),
        lax.all_gather(key_matrix, "shard", axis=0, tiled=True),
        lax.all_gather(value_matrix, "shard", axis=0, tiled=True),
        lax.all_gather(query_gain, "shard", axis=0, tiled=True),
        lax.all_gather(key_gain, "shard", axis=0, tiled=True),
        lax.all_gather(out_weight, "shard", axis=0, tiled=True),
        lax.all_gather(mlp_gain, "shard", axis=0, tiled=True),
        lax.all_gather(gate_weight, "shard", axis=0, tiled=True),
        lax.all_gather(up_weight, "shard", axis=0, tiled=True),
        lax.all_gather(down_weight, "shard", axis=0, tiled=True),
    )
    (
        mixer_norm_scale,
        weight_query,
        weight_key,
        weight_value,
        gain_query,
        gain_key,
        weight_out,
        gain_mlp,
        weight_gate,
        weight_up,
        weight_down,
    ) = gathered
    inputs = tokens[0].astype(jnp.float32)
    length_steps = inputs.shape[0]
    query_groups = QUERY_HEADS // SHARED_KV_GROUPS
    scale = PER_HEAD_DIM ** (-0.5)
    cosine_table, sine_table = rotary_tables(positions[0])
    normed_one, inverse_one = rms_parts(inputs)
    hidden_one = (normed_one * mixer_norm_scale.astype(jnp.float32)).astype(jnp.bfloat16)
    query_raw = jnp.dot(hidden_one, weight_query, preferred_element_type=jnp.float32).reshape(
        length_steps, QUERY_HEADS, PER_HEAD_DIM
    )
    query_normed, query_inverse = rms_parts(query_raw)
    query_half_float = rotate(
        query_normed * gain_query.astype(jnp.float32), cosine_table, sine_table
    )
    query_half_float = query_half_float.astype(jnp.bfloat16).reshape(
        length_steps, SHARED_KV_GROUPS, query_groups, PER_HEAD_DIM
    )
    key_unrotated = jnp.dot(hidden_one, weight_key, preferred_element_type=jnp.float32).reshape(
        length_steps, SHARED_KV_GROUPS, PER_HEAD_DIM
    )
    key_normed, key_inverse = rms_parts(key_unrotated)
    key_half_float = rotate(key_normed * gain_key.astype(jnp.float32), cosine_table, sine_table)
    key_half_float = key_half_float.astype(jnp.bfloat16).reshape(
        length_steps, SHARED_KV_GROUPS * PER_HEAD_DIM
    )
    value_half_float = jnp.dot(hidden_one, weight_value, preferred_element_type=jnp.float32).astype(
        jnp.bfloat16
    )
    question_vectors = lax.axis_index("ctx") * length_steps + jnp.arange(
        length_steps, dtype=jnp.int32
    )
    running_maximum = jnp.full(
        (SHARED_KV_GROUPS, query_groups, length_steps), BLOCKED_SCORE, jnp.float32
    )
    key_portion = lax.all_gather(key_half_float, "ctx", axis=0, tiled=True).reshape(
        -1, SHARED_KV_GROUPS, PER_HEAD_DIM
    )
    value_portion = lax.all_gather(value_half_float, "ctx", axis=0, tiled=True).reshape(
        -1, SHARED_KV_GROUPS, PER_HEAD_DIM
    )
    count_total = key_portion.shape[0]
    scores = (
        jnp.einsum(
            "tkgd,nkd->kgtn", query_half_float, key_portion, preferred_element_type=jnp.float32
        )
        * scale
    )
    key_rows = jnp.arange(count_total, dtype=jnp.int32)
    allowed = key_rows[None, :] <= question_vectors[:, None]
    scores = jnp.where(allowed, scores, BLOCKED_SCORE)
    new_max = jnp.maximum(running_maximum, jnp.max(scores, -1))
    weights = jnp.where(allowed, jnp.exp(scores - new_max[..., None]), 0.0)
    run_sum = jnp.sum(weights, -1)
    run_acc = jnp.einsum(
        "kgtn,nkd->kgtd",
        weights.astype(jnp.bfloat16),
        value_portion,
        preferred_element_type=jnp.float32,
    )
    running_maximum, run_sum, run_acc = (new_max, run_sum, run_acc)
    log_total = running_maximum + jnp.log(run_sum)
    attn_heads = run_acc / run_sum[..., None]
    attn_bf = (
        jnp.transpose(attn_heads, (2, 0, 1, 3))
        .reshape(length_steps, QUERY_HEADS * PER_HEAD_DIM)
        .astype(jnp.bfloat16)
    )
    resid = inputs + jnp.dot(attn_bf, weight_out, preferred_element_type=jnp.float32)
    normed_two, inverse_two = rms_parts(resid)
    hidden_two = (normed_two * gain_mlp.astype(jnp.float32)).astype(jnp.bfloat16)
    gate_value = jnp.dot(hidden_two, weight_gate, preferred_element_type=jnp.float32)
    up_value = jnp.dot(hidden_two, weight_up, preferred_element_type=jnp.float32)
    gate_sig = jax.nn.sigmoid(gate_value)
    gate_act = gate_value * gate_sig
    mixed_bf = (gate_act * up_value).astype(jnp.bfloat16)
    result = resid + jnp.dot(mixed_bf, weight_down, preferred_element_type=jnp.float32)
    back_weights = (
        lax.all_gather(attn_gain, "shard", axis=0, tiled=True),
        lax.all_gather(query_weight, "shard", axis=0, tiled=True),
        lax.all_gather(key_matrix, "shard", axis=0, tiled=True),
        lax.all_gather(value_matrix, "shard", axis=0, tiled=True),
        lax.all_gather(query_gain, "shard", axis=0, tiled=True),
        lax.all_gather(key_gain, "shard", axis=0, tiled=True),
        lax.all_gather(out_weight, "shard", axis=0, tiled=True),
        lax.all_gather(mlp_gain, "shard", axis=0, tiled=True),
        lax.all_gather(gate_weight, "shard", axis=0, tiled=True),
        lax.all_gather(up_weight, "shard", axis=0, tiled=True),
        lax.all_gather(down_weight, "shard", axis=0, tiled=True),
    )
    (
        mixer_norm_scale,
        weight_query,
        weight_key,
        weight_value,
        gain_query,
        gain_key,
        weight_out,
        gain_mlp,
        weight_gate,
        weight_up,
        weight_down,
    ) = back_weights
    grad_result = cotangent[0].astype(jnp.float32)
    grad_result_bf = grad_result.astype(jnp.bfloat16)
    grad_down_w = jnp.einsum(
        "tf,td->fd", mixed_bf, grad_result_bf, preferred_element_type=jnp.float32
    )
    grad_mixed = jnp.einsum(
        "td,fd->tf", grad_result_bf, weight_down, preferred_element_type=jnp.float32
    )
    grad_gate_bf = (
        grad_mixed * up_value * gate_sig * (1.0 + gate_value * (1.0 - gate_sig))
    ).astype(jnp.bfloat16)
    grad_up_bf = (grad_mixed * gate_act).astype(jnp.bfloat16)
    grad_gate_w = jnp.einsum(
        "td,tf->df", hidden_two, grad_gate_bf, preferred_element_type=jnp.float32
    )
    grad_up_w = jnp.einsum("td,tf->df", hidden_two, grad_up_bf, preferred_element_type=jnp.float32)
    grad_hidden_two = jnp.einsum(
        "tf,df->td", grad_gate_bf, weight_gate, preferred_element_type=jnp.float32
    ) + jnp.einsum("tf,df->td", grad_up_bf, weight_up, preferred_element_type=jnp.float32)
    grad_gain_mlp = jnp.sum(grad_hidden_two * normed_two, 0)
    grad_resid = grad_result + rms_back(
        grad_hidden_two * gain_mlp.astype(jnp.float32), normed_two, inverse_two
    )
    grad_resid_bf = grad_resid.astype(jnp.bfloat16)
    grad_out_w = jnp.einsum("tq,td->qd", attn_bf, grad_resid_bf, preferred_element_type=jnp.float32)
    attention_gradient_half = jnp.einsum(
        "td,qd->tq", grad_resid_bf, weight_out, preferred_element_type=jnp.float32
    ).astype(jnp.bfloat16)
    heads_gradient_half = attention_gradient_half.reshape(
        length_steps, SHARED_KV_GROUPS, query_groups, PER_HEAD_DIM
    )
    delta = jnp.einsum("tkgd,kgtd->kgt", heads_gradient_half.astype(jnp.float32), attn_heads)
    every_key_row, every_value_row = (
        lax.all_gather(key_half_float, "ctx", axis=0, tiled=True),
        lax.all_gather(value_half_float, "ctx", axis=0, tiled=True),
    )
    grand_aggregate = every_key_row.shape[0]
    block_step = min(512, grand_aggregate)
    count_total = grand_aggregate // block_step
    key_block_list = every_key_row.reshape(count_total, block_step, SHARED_KV_GROUPS, PER_HEAD_DIM)
    value_block_list = every_value_row.reshape(
        count_total, block_step, SHARED_KV_GROUPS, PER_HEAD_DIM
    )
    starts = jnp.arange(count_total) * block_step

    def back_block(question_cotangent, block_inputs):
        key_block, value_block, start = block_inputs
        scores = (
            jnp.einsum(
                "tkgd,nkd->kgtn", query_half_float, key_block, preferred_element_type=jnp.float32
            )
            * scale
        )
        key_rows = start + jnp.arange(block_step, dtype=jnp.int32)
        allowed = key_rows[None, :] <= question_vectors[:, None]
        probs = jnp.where(allowed, jnp.exp(scores - log_total[..., None]), 0.0)
        probs_bf = probs.astype(jnp.bfloat16)
        value_block_gradient = jnp.einsum(
            "kgtn,tkgd->nkd", probs_bf, heads_gradient_half, preferred_element_type=jnp.float32
        )
        grad_probs = jnp.einsum(
            "tkgd,nkd->kgtn", heads_gradient_half, value_block, preferred_element_type=jnp.float32
        )
        grad_scores_bf = (probs * (grad_probs - delta[..., None])).astype(jnp.bfloat16)
        question_cotangent = (
            question_cotangent
            + jnp.einsum(
                "kgtn,nkd->tkgd", grad_scores_bf, key_block, preferred_element_type=jnp.float32
            )
            * scale
        )
        key_block_gradient = (
            jnp.einsum(
                "kgtn,tkgd->nkd",
                grad_scores_bf,
                query_half_float,
                preferred_element_type=jnp.float32,
            )
            * scale
        )
        return (
            question_cotangent,
            (
                key_block_gradient.reshape(block_step, SHARED_KV_GROUPS * PER_HEAD_DIM),
                value_block_gradient.reshape(block_step, SHARED_KV_GROUPS * PER_HEAD_DIM),
            ),
        )

    question_cotangent, (lookup_partial_terms, payload_partial_terms) = lax.scan(
        back_block,
        jnp.zeros((length_steps, SHARED_KV_GROUPS, query_groups, PER_HEAD_DIM), jnp.float32),
        (key_block_list, value_block_list, starts),
    )
    key_gradient, grad_value = (
        lax.psum_scatter(
            lookup_partial_terms.reshape(grand_aggregate, SHARED_KV_GROUPS * PER_HEAD_DIM).astype(
                jnp.bfloat16
            ),
            "ctx",
            scatter_dimension=0,
            tiled=True,
        ).astype(jnp.float32),
        lax.psum_scatter(
            payload_partial_terms.reshape(grand_aggregate, SHARED_KV_GROUPS * PER_HEAD_DIM).astype(
                jnp.bfloat16
            ),
            "ctx",
            scatter_dimension=0,
            tiled=True,
        ).astype(jnp.float32),
    )
    grad_query_rot = rotate_reverse(
        question_cotangent.reshape(length_steps, QUERY_HEADS, PER_HEAD_DIM),
        cosine_table,
        sine_table,
    )
    grad_gain_query = jnp.sum(grad_query_rot * query_normed, (0, 1))
    grad_query_bf = rms_back(
        grad_query_rot * gain_query.astype(jnp.float32), query_normed, query_inverse
    )
    grad_query_bf = grad_query_bf.reshape(length_steps, QUERY_HEADS * PER_HEAD_DIM).astype(
        jnp.bfloat16
    )
    key_rotated_gradient = rotate_reverse(
        key_gradient.reshape(length_steps, SHARED_KV_GROUPS, PER_HEAD_DIM), cosine_table, sine_table
    )
    grad_gain_key = jnp.sum(key_rotated_gradient * key_normed, (0, 1))
    key_gradient_half = rms_back(
        key_rotated_gradient * gain_key.astype(jnp.float32), key_normed, key_inverse
    )
    key_gradient_half = key_gradient_half.reshape(
        length_steps, SHARED_KV_GROUPS * PER_HEAD_DIM
    ).astype(jnp.bfloat16)
    grad_value_bf = grad_value.astype(jnp.bfloat16)
    grad_query_w = jnp.einsum(
        "td,tq->dq", hidden_one, grad_query_bf, preferred_element_type=jnp.float32
    )
    grad_key_w = jnp.einsum(
        "td,tq->dq", hidden_one, key_gradient_half, preferred_element_type=jnp.float32
    )
    grad_value_w = jnp.einsum(
        "td,tq->dq", hidden_one, grad_value_bf, preferred_element_type=jnp.float32
    )
    grad_hidden_one = (
        jnp.einsum("tq,dq->td", grad_query_bf, weight_query, preferred_element_type=jnp.float32)
        + jnp.einsum("tq,dq->td", key_gradient_half, weight_key, preferred_element_type=jnp.float32)
        + jnp.einsum("tq,dq->td", grad_value_bf, weight_value, preferred_element_type=jnp.float32)
    )
    grad_gain_attn = jnp.sum(grad_hidden_one * normed_one, 0)
    grad_inputs = grad_resid + rms_back(
        grad_hidden_one * mixer_norm_scale.astype(jnp.float32), normed_one, inverse_one
    )
    summed_parts = (
        lax.psum_scatter(
            grad_gain_attn.astype(jnp.bfloat16), "shard", scatter_dimension=0, tiled=True
        ).astype(jnp.float32),
        lax.psum_scatter(
            grad_query_w.astype(jnp.bfloat16), "shard", scatter_dimension=0, tiled=True
        ).astype(jnp.float32),
        lax.psum_scatter(
            grad_key_w.astype(jnp.bfloat16), "shard", scatter_dimension=0, tiled=True
        ).astype(jnp.float32),
        lax.psum_scatter(
            grad_value_w.astype(jnp.bfloat16), "shard", scatter_dimension=0, tiled=True
        ).astype(jnp.float32),
        lax.psum_scatter(
            grad_gain_query.astype(jnp.bfloat16), "shard", scatter_dimension=0, tiled=True
        ).astype(jnp.float32),
        lax.psum_scatter(
            grad_gain_key.astype(jnp.bfloat16), "shard", scatter_dimension=0, tiled=True
        ).astype(jnp.float32),
        lax.psum_scatter(
            grad_out_w.astype(jnp.bfloat16), "shard", scatter_dimension=0, tiled=True
        ).astype(jnp.float32),
        lax.psum_scatter(
            grad_gain_mlp.astype(jnp.bfloat16), "shard", scatter_dimension=0, tiled=True
        ).astype(jnp.float32),
        lax.psum_scatter(
            grad_gate_w.astype(jnp.bfloat16), "shard", scatter_dimension=0, tiled=True
        ).astype(jnp.float32),
        lax.psum_scatter(
            grad_up_w.astype(jnp.bfloat16), "shard", scatter_dimension=0, tiled=True
        ).astype(jnp.float32),
        lax.psum_scatter(
            grad_down_w.astype(jnp.bfloat16), "shard", scatter_dimension=0, tiled=True
        ).astype(jnp.float32),
    )
    owned = (
        lax.psum(summed_parts[0].astype(jnp.bfloat16), "ctx").astype(jnp.float32),
        lax.psum(summed_parts[1].astype(jnp.bfloat16), "ctx").astype(jnp.float32),
        lax.psum(summed_parts[2].astype(jnp.bfloat16), "ctx").astype(jnp.float32),
        lax.psum(summed_parts[3].astype(jnp.bfloat16), "ctx").astype(jnp.float32),
        lax.psum(summed_parts[4].astype(jnp.bfloat16), "ctx").astype(jnp.float32),
        lax.psum(summed_parts[5].astype(jnp.bfloat16), "ctx").astype(jnp.float32),
        lax.psum(summed_parts[6].astype(jnp.bfloat16), "ctx").astype(jnp.float32),
        lax.psum(summed_parts[7].astype(jnp.bfloat16), "ctx").astype(jnp.float32),
        lax.psum(summed_parts[8].astype(jnp.bfloat16), "ctx").astype(jnp.float32),
        lax.psum(summed_parts[9].astype(jnp.bfloat16), "ctx").astype(jnp.float32),
        lax.psum(summed_parts[10].astype(jnp.bfloat16), "ctx").astype(jnp.float32),
    )
    return (
        result.astype(jnp.bfloat16)[None],
        grad_inputs[None],
        owned[0],
        owned[1],
        owned[2],
        owned[3],
        owned[4],
        owned[5],
        owned[6],
        owned[7],
        owned[8],
        owned[9],
        owned[10],
    )


def solution(mesh):
    in_specs = (
        P("shard", "ctx", None),
        P("shard", "ctx"),
        P("shard"),
        P("shard", None),
        P("shard", None),
        P("shard", None),
        P("shard"),
        P("shard"),
        P("shard", None),
        P("shard"),
        P("shard", None),
        P("shard", None),
        P("shard", None),
        P("shard", "ctx", None),
    )
    out_specs = (
        P("shard", "ctx", None),
        P("shard", "ctx", None),
        P("shard"),
        P("shard", None),
        P("shard", None),
        P("shard", None),
        P("shard"),
        P("shard"),
        P("shard", None),
        P("shard"),
        P("shard", None),
        P("shard", None),
        P("shard", None),
    )
    return jax.shard_map(shards, mesh=mesh, in_specs=in_specs, out_specs=out_specs, check_vma=False)
```

profile of v0, /device:TPU:1, one launch (start us, length us, event | category | flops | bytes accessed | tf_op | source)
XLA Modules:
  0.0 1424.3 jit_solution(17745493801193261717)
XLA Ops:
  14.7 35.8 %all-reduce.9 = (bf16[1024]{0:T(1024)(128)(2,1)S(1)}, bf16[128]{0:T(256)(128)(2,1)S(1)}, bf16[128]{0:T(256)(128)(2,1)S(1)}, bf16[1024]{0:T(1024)(128)(2,1)S(1)}) all-reduce(bf16[1024]{0:T(1024)(128)(2,1)S(1)} %dynamic-update-slice, bf16[128]{0:T(256)(128)(2,1)S(1)} %dynamic-update-slice.1, ...), channel_id=1, replica_groups=mesh['shard'=16,'ctx'=8] {'shard'}, use_global_device_ids=true, to_apply=%add | all-reduce | flops 2304 | bytes 9216
  52.6 10.2 all-gather.10.cloned.1.call-done
  62.7 2.9 copy.65
  68.2 44.1 %all-gather.16.cloned.1.call-done = bf16[1024,1024]{1,0:T(8,128)(2,1)} async-done(((bf16[64,1024]{1,0:T(8,128)(2,1)}), bf16[1024,1024]{1,0:T(8,128)(2,1)}) %all-gather.16.cloned.1.call-update) | async-done | bytes 2097168 | tf_op jit(solution)/shard_map/all_gather | solution.py:70
  112.2 2.8 convolution_convert_fusion.8
  120.5 49.2 %all-gather.12.cloned.1.call-done = bf16[1024,1024]{0,1:T(8,128)(2,1)} async-done(((bf16[128,1024]{0,1:T(8,128)(2,1)}), bf16[1024,1024]{0,1:T(8,128)(2,1)}) %all-gather.12.cloned.1.call-update) | async-done | bytes 2097168 | tf_op jit(solution)/shard_map/all_gather | solution.py:126
  169.7 3.3 reshape.256
  173.0 3.8 copy.72
  176.8 47.0 %all-gather.18.cloned.1.call-done = bf16[1024,1024]{1,0:T(8,128)(2,1)} async-done(((bf16[128,1024]{1,0:T(8,128)(2,1)}), bf16[1024,1024]{1,0:T(8,128)(2,1)}) %all-gather.18.cloned.1.call-update) | async-done | bytes 2097168 | tf_op jit(solution)/shard_map/all_gather | solution.py:129
  223.8 3.7 copy.122
  230.1 54.7 %all-gather.14.cloned.1.call-done = bf16[1024,2048]{1,0:T(8,128)(2,1)} async-done(((bf16[64,2048]{1,0:T(8,128)(2,1)}), bf16[1024,2048]{1,0:T(8,128)(2,1)}) %all-gather.14.cloned.1.call-update) | async-done | bytes 4194320 | tf_op jit(solution)/shard_map/all_gather | solution.py:68
  284.8 6.4 copy.66
  291.2 3.5 multiply_reduce_fusion.3
  300.6 3.2 fusion.36
  303.8 38.0 %all-gather.20.cloned.1.call-done = bf16[2048,1024]{1,0:T(8,128)(2,1)} async-done(((bf16[128,1024]{1,0:T(8,128)(2,1)}), bf16[2048,1024]{1,0:T(8,128)(2,1)}) %all-gather.20.cloned.1.call-update) | async-done | bytes 4194320 | tf_op jit(solution)/shard_map/all_gather | solution.py:73
  341.8 3.0 multiply_reduce_fusion.8
  345.6 61.5 %all-gather.22.cloned.1.call-done = bf16[1024,3072]{1,0:T(8,128)(2,1)} async-done(((bf16[64,3072]{1,0:T(8,128)(2,1)}), bf16[1024,3072]{1,0:T(8,128)(2,1)}) %all-gather.22.cloned.1.call-update) | async-done | bytes 6291472 | tf_op jit(solution)/shard_map/all_gather | solution.py:75
  407.1 5.0 fusion.78
  412.1 60.0 %all-gather.24.cloned.1.call-done = bf16[1024,3072]{1,0:T(8,128)(2,1)} async-done(((bf16[64,3072]{1,0:T(8,128)(2,1)}), bf16[1024,3072]{1,0:T(8,128)(2,1)}) %all-gather.24.cloned.1.call-update) | async-done | bytes 6291472 | tf_op jit(solution)/shard_map/all_gather | solution.py:76
  472.1 4.9 fusion.79
  477.0 60.0 %all-gather.26.cloned.1.call-done = bf16[3072,1024]{1,0:T(8,128)(2,1)} async-done(((bf16[192,1024]{1,0:T(8,128)(2,1)}), bf16[3072,1024]{1,0:T(8,128)(2,1)}) %all-gather.26.cloned.1.call-update) | async-done | bytes 6291472 | tf_op jit(solution)/shard_map/all_gather | solution.py:77
  537.1 7.0 multiply_convert_fusion
  544.1 5.6 fusion.80
  549.7 2.9 multiply_reduce_fusion.4
  559.1 43.8 %while.15 = (s32[]{:T(128)}, f32[128,8,2,128]{0,3,2,1:T(8,128)}, bf16[2,512,1024]{2,1,0:T(8,128)(2,1)}, bf16[2,512,1024]{2,1,0:T(8,128)(2,1)}, bf16[2,512,8,128]...) while((s32[]{:T(128)}, f32[128,8,2,128]{0,3,2,1:T(8,128)}, ...), condition=%wide.region_8.9_spmd.clone, body=%wide.region_7.8_spmd.clone.sunk | while | flops 1354564224 | bytes 62159760 | solution.py:282
  568.7 4.3 fusion.149
  578.0 2.8 fusion.148
  590.5 4.3 fusion.149
  599.8 3.1 fusion.148
  606.5 3.3 convolution_convert_fusion.4
  610.0 3.3 convolution_convert_fusion.3
  613.4 37.9 %reduce-scatter.10.cloned.1.call-done = bf16[128,1024]{1,0:T(8,128)(2,1)} async-done(((bf16[1024,1024]{1,0:T(8,128)(2,1)}), bf16[128,1024]{1,0:T(8,128)(2,1)}) %reduce-scatter.10.cloned.1.call-update) | async-done | bytes 262160 | tf_op jit(solution)/shard_map/reduce_scatter | solution.py:288
  656.5 49.7 %reduce-scatter.12.cloned.1.call-done = bf16[128,1024]{1,0:T(8,128)(2,1)} async-done(((bf16[1024,1024]{1,0:T(8,128)(2,1)}), bf16[128,1024]{1,0:T(8,128)(2,1)}) %reduce-scatter.12.cloned.1.call-update) | async-done | bytes 262160 | tf_op jit(solution)/shard_map/reduce_scatter | solution.py:296
  706.2 3.1 convolution_convert_fusion.6
  709.7 4.5 convolution_convert_fusion.2
  715.4 4.4 convolution_convert_fusion.1
  721.0 4.5 convolution_convert_fusion
  726.9 64.0 %reduce-scatter.14.cloned.1.call-done = bf16[64,2048]{1,0:T(8,128)(2,1)} async-done(((bf16[1024,2048]{1,0:T(8,128)(2,1)}), bf16[64,2048]{1,0:T(8,128)(2,1)}) %reduce-scatter.14.cloned.1.call-update) | async-done | bytes 262160 | tf_op jit(solution)/shard_map/reduce_scatter | solution.py:350
  790.9 83.5 %reduce-scatter.20.cloned.1.call-done = bf16[128,1024]{1,0:T(8,128)(2,1)} async-done(((bf16[2048,1024]{1,0:T(8,128)(2,1)}), bf16[128,1024]{1,0:T(8,128)(2,1)}) %reduce-scatter.20.cloned.1.call-update) | async-done | bytes 262160 | tf_op jit(solution)/shard_map/reduce_scatter | solution.py:365
  874.4 72.8 %reduce-scatter.16.cloned.1.call-done = bf16[64,1024]{1,0:T(8,128)(2,1)} async-done(((bf16[1024,1024]{1,0:T(8,128)(2,1)}), bf16[64,1024]{1,0:T(8,128)(2,1)}) %reduce-scatter.16.cloned.1.call-update) | async-done | bytes 131088 | tf_op jit(solution)/shard_map/reduce_scatter | solution.py:353
  947.2 73.7 %reduce-scatter.18.cloned.1.call-done = bf16[64,1024]{1,0:T(8,128)(2,1)} async-done(((bf16[1024,1024]{1,0:T(8,128)(2,1)}), bf16[64,1024]{1,0:T(8,128)(2,1)}) %reduce-scatter.18.cloned.1.call-update) | async-done | bytes 131088 | tf_op jit(solution)/shard_map/reduce_scatter | solution.py:356
  1020.9 93.3 %reduce-scatter.22.cloned.1.call-done = bf16[64,3072]{1,0:T(8,128)(2,1)} async-done(((bf16[1024,3072]{1,0:T(8,128)(2,1)}), bf16[64,3072]{1,0:T(8,128)(2,1)}) %reduce-scatter.22.cloned.1.call-update) | async-done | bytes 393232 | tf_op jit(solution)/shard_map/reduce_scatter | solution.py:371
  1114.2 92.3 %reduce-scatter.24.cloned.1.call-done = bf16[64,3072]{1,0:T(8,128)(2,1)} async-done(((bf16[1024,3072]{1,0:T(8,128)(2,1)}), bf16[64,3072]{1,0:T(8,128)(2,1)}) %reduce-scatter.24.cloned.1.call-update) | async-done | bytes 393232 | tf_op jit(solution)/shard_map/reduce_scatter | solution.py:374
  1206.5 92.3 %reduce-scatter.26.cloned.1.call-done = bf16[192,1024]{1,0:T(8,128)(2,1)} async-done(((bf16[3072,1024]{1,0:T(8,128)(2,1)}), bf16[192,1024]{1,0:T(8,128)(2,1)}) %reduce-scatter.26.cloned.1.call-update) | async-done | bytes 393232 | tf_op jit(solution)/shard_map/reduce_scatter | solution.py:377
  1298.9 4.9 fusion.33
  1307.8 35.7 %all-reduce.8 = (bf16[1024]{0:T(1024)(128)(2,1)S(1)}, bf16[128]{0:T(256)(128)(2,1)S(1)}, bf16[128]{0:T(256)(128)(2,1)S(1)}, bf16[1024]{0:T(1024)(128)(2,1)S(1)}) all-reduce(bf16[1024]{0:T(1024)(128)(2,1)S(1)} %get-tuple-element.164, bf16[128]{0:T(256)(128)(2,1)S(1)} %copy-done.55, ...), channel_id=4, replica_groups=mesh['shard'=16,'ctx'=8] {'shard'}, use_global_device_ids=true, to_apply=%region_15.16.clone | all-reduce | flops 2304 | bytes 9216
  1343.8 15.1 %all-reduce.10 = (bf16[64]{0:T(256)(128)(2,1)S(1)}, bf16[8]{0:T(256)(128)(2,1)S(1)}, bf16[8]{0:T(256)(128)(2,1)S(1)}, bf16[64]{0:T(256)(128)(2,1)S(1)}) all-reduce(bf16[64]{0:T(256)(128)(2,1)S(1)} %dynamic-slice.5, bf16[8]{0:T(256)(128)(2,1)S(1)} %dynamic-slice.7, ...), channel_id=1, replica_groups=mesh['shard'=16,'ctx'=8] {'ctx'}, use_global_device_ids=true, to_apply=%region_16.17 | all-reduce | flops 144 | bytes 576 | tf_op jit(solution)/shard_map/psum | solution.py:382
  1361.9 45.4 %all-reduce.14.cloned.1.call-done = (bf16[64,2048]{1,0:T(8,128)(2,1)}, bf16[64,1024]{1,0:T(8,128)(2,1)}, bf16[64,1024]{1,0:T(8,128)(2,1)}, bf16[128,1024]{1,0:T(...) async-done(((bf16[64,2048]{1,0:T(8,128)(2,1)}, bf16[64,1024]{1,0:T(8,128)(2,1)}, bf16[64,1024]{1,0:T(8,128)(2,1)}, ...) | async-done | bytes 1966096 | tf_op jit(solution)/shard_map/psum | solution.py:383
  (271 shorter events, 89.3 us)
Async XLA Ops:
  7.2 58.4 %copy-start.5 = (bf16[1,128,1024]{2,1,0:T(8,128)(2,1)S(1)}, bf16[1,128,1024]{2,1,0:T(8,128)(2,1)}, u32[]{:S(2)}) copy-start(bf16[1,128,1024]{2,1,0:T(8,128)(2,1)} %param.16) | copy-start | bytes 786436
  7.2 55.5 %all-gather.10.cloned.1.call-start = ((), (), s32[]{:S(2)}) async-start(), calls=%async_computation.9 | async-start | bytes 2228224 | tf_op jit(solution)/shard_map/all_gather | solution.py:69
  7.9 104.3 %all-gather.16.cloned.1.call-start = ((), (), s32[]{:S(2)}) async-start(), calls=%async_computation.12 | async-start | bytes 2228224 | tf_op jit(solution)/shard_map/all_gather | solution.py:70
  8.7 161.0 %all-gather.12.cloned.1.call-start = ((), (), s32[]{:S(2)}) async-start(), calls=%async_computation.10 | async-start | bytes 2359296 | tf_op jit(solution)/shard_map/all_gather | solution.py:126
  50.5 16.1 %copy-start.52 = (f32[128]{0:T(128)}, f32[128]{0:T(128)S(1)}, u32[]{:S(2)}) copy-start(f32[128]{0:T(128)S(1)} %convert_element_type.222) | copy-start | bytes 1540
  51.4 243.7 %copy-start.34 = (f32[128,128]{0,1:T(8,128)}, f32[128,128]{0,1:T(8,128)S(1)}, u32[]{:S(2)}) copy-start(f32[128,128]{0,1:T(8,128)S(1)} %get-tuple-element.241) | copy-start | bytes 196612
  52.6 238.6 %copy-start.46 = (f32[128]{0:T(128)}, f32[128]{0:T(128)S(1)}, u32[]{:S(2)}) copy-start(f32[128]{0:T(128)S(1)} %add_rsqrt_fusion.3) | copy-start | bytes 1540
  68.1 155.7 %all-gather.18.cloned.1.call-start = ((), (), s32[]{:S(2)}) async-start(), calls=%async_computation.13 | async-start | bytes 2359296 | tf_op jit(solution)/shard_map/all_gather | solution.py:129
  115.1 169.7 %all-gather.14.cloned.1.call-start = ((), (), s32[]{:S(2)}) async-start(), calls=%async_computation.11 | async-start | bytes 4456448 | tf_op jit(solution)/shard_map/all_gather | solution.py:68
  115.6 226.1 %all-gather.20.cloned.1.call-start = ((), (), s32[]{:S(2)}) async-start(), calls=%async_computation.14 | async-start | bytes 4456448 | tf_op jit(solution)/shard_map/all_gather | solution.py:73
  116.2 290.9 %all-gather.22.cloned.1.call-start = ((), (), s32[]{:S(2)}) async-start(), calls=%async_computation.15 | async-start | bytes 6684672 | tf_op jit(solution)/shard_map/all_gather | solution.py:75
  117.0 355.1 %all-gather.24.cloned.1.call-start = ((), (), s32[]{:S(2)}) async-start(), calls=%async_computation.16 | async-start | bytes 6684672 | tf_op jit(solution)/shard_map/all_gather | solution.py:76
  117.7 419.3 %all-gather.26.cloned.1.call-start = ((), (), s32[]{:S(2)}) async-start(), calls=%async_computation.17 | async-start | bytes 6684672 | tf_op jit(solution)/shard_map/all_gather | solution.py:77
  118.5 532.8 %reduce-scatter.10.cloned.1.call-start = ((), (), s32[]{:S(2)}) async-start(), calls=%async_computation.18 | async-start | bytes 2359296 | tf_op jit(solution)/shard_map/reduce_scatter | solution.py:288
  118.5 176.2 %copy-start.53 = (f32[128]{0:T(128)}, f32[128]{0:T(128)S(1)}, u32[]{:S(2)}) copy-start(f32[128]{0:T(128)S(1)} %convert_element_type.226) | copy-start | bytes 1540
  303.8 41.7 %copy-start.25 = (bf16[128,8,2,128]{0,3,2,1:T(8,128)(2,1)}, bf16[128,8,2,128]{0,3,2,1:T(8,128)(2,1)S(1)}, u32[]{:S(2)}) copy-start(bf16[128,8,2,128]{0,3,2,1:T(8,128)(2,1)S(1)} %get-tuple-element.234) | copy-start | bytes 1572868
  303.8 41.7 %copy-start.45 = (f32[1024]{0:T(1024)S(1)}, f32[1024]{0:T(1024)}, u32[]{:S(2)}) copy-start(f32[1024]{0:T(1024)} %convert_element_type.233) | copy-start | bytes 12292
  344.8 207.9 %copy-start.14 = (f32[128,1024]{1,0:T(8,128)}, f32[128,1024]{1,0:T(8,128)S(1)}, u32[]{:S(2)}) copy-start(f32[128,1024]{1,0:T(8,128)S(1)} %get-tuple-element.237) | copy-start | bytes 1572868
  345.6 126.5 %copy-start.10 = (bf16[128,1024]{1,0:T(8,128)(2,1)}, bf16[128,1024]{1,0:T(8,128)(2,1)S(1)}, u32[]{:S(2)}) copy-start(bf16[128,1024]{1,0:T(8,128)(2,1)S(1)} %multiply_convert_fusion.5) | copy-start | bytes 786436
  412.1 124.9 %copy-start.37 = (bf16[1,128,1024]{2,1,0:T(8,128)(2,1)S(1)}, bf16[1,128,1024]{2,1,0:T(8,128)(2,1)}, u32[]{:S(2)}) copy-start(bf16[1,128,1024]{2,1,0:T(8,128)(2,1)} %param.29) | copy-start | bytes 786436
  544.1 8.6 copy-start.27
  544.1 8.6 copy-start.29
  544.1 5.6 copy-start.4
  559.1 6.3 copy-start.1
  575.3 5.5 copy-start.57
  580.8 6.4 copy-start.1
  580.9 4.9 copy-start.41
  597.1 5.8 copy-start.57
  603.0 103.2 %reduce-scatter.12.cloned.1.call-start = ((), (), s32[]{:S(2)}) async-start(), calls=%async_computation.19 | async-start | bytes 2359296 | tf_op jit(solution)/shard_map/reduce_scatter | solution.py:296
  603.7 187.2 %reduce-scatter.14.cloned.1.call-start = ((), (), s32[]{:S(2)}) async-start(), calls=%async_computation.20 | async-start | bytes 4456448 | tf_op jit(solution)/shard_map/reduce_scatter | solution.py:350
  609.9 264.5 %reduce-scatter.20.cloned.1.call-start = ((), (), s32[]{:S(2)}) async-start(), calls=%async_computation.23 | async-start | bytes 4456448 | tf_op jit(solution)/shard_map/reduce_scatter | solution.py:365
  613.3 39.2 %copy-start.13 = (f32[128,8,128]{0,2,1:T(8,128)S(1)}, f32[128,8,128]{0,2,1:T(8,128)}, u32[]{:S(2)}) copy-start(f32[128,8,128]{0,2,1:T(8,128)} %copy-done.12) | copy-start | bytes 1572868
  613.3 40.9 %copy-start.48 = (f32[128]{0:T(128)S(1)}, f32[128]{0:T(128)}, u32[]{:S(2)}) copy-start(f32[128]{0:T(128)} %copy-done.46) | copy-start | bytes 1540
  613.4 333.8 %reduce-scatter.16.cloned.1.call-start = ((), (), s32[]{:S(2)}) async-start(), calls=%async_computation.21 | async-start | bytes 2228224 | tf_op jit(solution)/shard_map/reduce_scatter | solution.py:353
  654.2 55.2 %copy-start.31 = (bf16[128,8,128]{0,2,1:T(8,128)(2,1)}, bf16[128,8,128]{0,2,1:T(8,128)(2,1)S(1)}, u32[]{:S(2)}) copy-start(bf16[128,8,128]{0,2,1:T(8,128)(2,1)S(1)} %multiply_convert_fusion.4) | copy-start | bytes 786436
  654.2 55.5 %copy-start.11 = (bf16[128,1024]{1,0:T(8,128)(2,1)S(1)}, bf16[128,1024]{1,0:T(8,128)(2,1)}, u32[]{:S(2)}) copy-start(bf16[128,1024]{1,0:T(8,128)(2,1)} %copy-done.10) | copy-start | bytes 786436
  654.2 55.5 %copy-start.30 = (bf16[128,3072]{1,0:T(8,128)(2,1)S(1)}, bf16[128,3072]{1,0:T(8,128)(2,1)}, u32[]{:S(2)}) copy-start(bf16[128,3072]{1,0:T(8,128)(2,1)} %copy-done.29) | copy-start | bytes 2359300
  656.4 364.5 %reduce-scatter.18.cloned.1.call-start = ((), (), s32[]{:S(2)}) async-start(), calls=%async_computation.22 | async-start | bytes 2228224 | tf_op jit(solution)/shard_map/reduce_scatter | solution.py:356
  709.4 404.8 %reduce-scatter.22.cloned.1.call-start = ((), (), s32[]{:S(2)}) async-start(), calls=%async_computation.24 | async-start | bytes 6684672 | tf_op jit(solution)/shard_map/reduce_scatter | solution.py:371
  714.3 492.3 %reduce-scatter.24.cloned.1.call-start = ((), (), s32[]{:S(2)}) async-start(), calls=%async_computation.25 | async-start | bytes 6684672 | tf_op jit(solution)/shard_map/reduce_scatter | solution.py:374
  719.8 579.0 %reduce-scatter.26.cloned.1.call-start = ((), (), s32[]{:S(2)}) async-start(), calls=%async_computation.26 | async-start | bytes 6684672 | tf_op jit(solution)/shard_map/reduce_scatter | solution.py:377
  725.5 573.3 %copy-start.15 = (f32[128,1024]{1,0:T(8,128)S(1)}, f32[128,1024]{1,0:T(8,128)}, u32[]{:S(2)}) copy-start(f32[128,1024]{1,0:T(8,128)} %copy-done.14) | copy-start | bytes 1572868
  725.5 681.8 %all-reduce.14.cloned.1.call-start = ((), (), s32[]{:S(2)}) async-start(), calls=%async_computation.27 | async-start | bytes 3932160 | tf_op jit(solution)/shard_map/psum | solution.py:383
  1298.9 5.8 copy-start.19
  1298.9 5.8 copy-start.40
  1407.4 7.7 copy-start.42
  1407.4 8.5 copy-start.44
  1407.4 9.2 copy-start.43
  (36 other events, 108.7 us)
Sparse Core Ops, SparseCore 0:
  10.4 52.2 all-gather.9
  65.1 47.0 all-gather.15
  114.4 55.2 all-gather.11
  171.7 52.0 all-gather.17
  226.1 58.6 all-gather.13
  287.1 54.6 all-gather.19
  344.2 62.8 all-gather.21
  409.5 62.5 all-gather.23
  474.5 62.5 all-gather.25
  603.1 48.1 reduce-scatter.9
  653.7 52.4 reduce-scatter.11
  710.1 80.7 reduce-scatter.13
  795.5 78.8 reduce-scatter.19
  878.2 68.9 reduce-scatter.15
  951.0 69.8 reduce-scatter.17
  1024.9 89.2 reduce-scatter.21
  1118.2 88.2 reduce-scatter.23
  1210.5 88.2 reduce-scatter.25
  1301.9 105.3 all-reduce.13
where the time goes:
time: 1430 us; the launch traced here: 1420 us
  waiting for transfers between devices  1130 us (79%)
  matrix products  101 us (7%)
  blocking collectives  86.5 us (6%)
  local copies, waits for them, and re-layouts  52.1 us (4%)
  other arithmetic  30.8 us (2%)
  between operations  17.9 us (1%)
    reduce_scatter x1, waiting for transfers between devices, shards(): lax.psum_scatter(grad_gate_w.astype(jnp.bfloat16), 'shard', scatter_dimen...  93.3 us
    reduce_scatter x1, waiting for transfers between devices, shards(): lax.psum_scatter(grad_up_w.astype(jnp.bfloat16), 'shard', scatter_dimensi...  92.3 us
    reduce_scatter x1, waiting for transfers between devices, shards(): lax.psum_scatter(grad_down_w.astype(jnp.bfloat16), 'shard', scatter_dimen...  92.3 us
    reduce_scatter x1, waiting for transfers between devices, shards(): lax.psum_scatter(grad_out_w.astype(jnp.bfloat16), 'shard', scatter_dimens...  83.5 us
    reduce_scatter x1, waiting for transfers between devices, shards(): lax.psum_scatter(grad_value_w.astype(jnp.bfloat16), 'shard', scatter_dime...  73.7 us
    reduce_scatter x1, waiting for transfers between devices, shards(): lax.psum_scatter(grad_key_w.astype(jnp.bfloat16), 'shard', scatter_dimens...  72.8 us
    unnamed x2, blocking collectives  71.4 us
    reduce_scatter x1, waiting for transfers between devices, shards(): lax.psum_scatter(grad_query_w.astype(jnp.bfloat16), 'shard', scatter_dime...  64 us
  transfers between devices with their start and end apart: 19, of which 19 were waited for; matrix products, arithmetic and copies ran while one was open for 7% of the time, Pallas kernels for 0%

commit v1 on v0

v1 whole, which is shorter than its diff:
```python
import jax
import jax.numpy as jnp
from jax import lax
from jax.experimental import pallas as pl
from jax.experimental.pallas import tpu as pltpu
from jax.sharding import PartitionSpec as P

MESH = pl.DeviceIdType.MESH
BF = jnp.bfloat16
F32 = jnp.float32

NS = 16
NC = 8
T = 128
SEQ = 1024
D = 1024
HD = 128
QW = 256
FW = 384
EPSILON = 1e-06
ROPE_BASE = 1000000.0
BLOCKED_SCORE = -1e30
SMALL = 2304

ALL = slice(None)
ROWS = ((slice(0, 48), ALL), (slice(48, 96), ALL), (slice(96, 128), ALL))


def lanes(width):
    n = width // 128
    a = (n + 2) // 3 * 128
    b = a + (n + 1) // 3 * 128
    return ((ALL, slice(0, a)), (ALL, slice(a, b)), (ALL, slice(b, width)))


def view(ref, part):
    return ref.at[tuple(pl.ds(p.start, p.stop - p.start) if p != ALL else p for p in part)]


class Ring:
    def __init__(self, me, device):
        self.a = me // 2
        self.b = lax.rem(me, 2)
        self.device = device

    def idx(self, da, db):
        return lax.rem(self.a + da + 4, 4) * 2 + lax.rem(self.b + db, 2)

    def dev(self, da, db):
        return self.device(self.idx(da, db))


class Net:
    def __init__(self, send, recv, local):
        self.s, self.r, self.l = send, recv, local
        self.n = 0
        self.m = 0

    def send(self, src, dst, to):
        k = self.n
        self.n += 1
        c = pltpu.make_async_remote_copy(
            src_ref=src, dst_ref=dst, send_sem=self.s.at[k], recv_sem=self.r.at[k],
            device_id=to, device_id_type=MESH,
        )
        c.start()
        return c

    def copy(self, src, dst):
        k = self.m
        self.m += 1
        c = pltpu.make_async_copy(src, dst, self.l.at[k])
        c.start()
        return c


def places():
    s = lax.axis_index("shard")
    c = lax.axis_index("ctx")
    core = lax.rem(s, 2)
    ctx = Ring(c, lambda i: (s, i))
    chips = Ring(s // 2, lambda i: (i * 2 + core, c))
    sibling = (s + 1 - 2 * core, c)
    half, rest = lax.rem(s, 2), s // 2
    goes = (8 * half + c, rest)
    comes = (2 * c + s // 8, lax.rem(s, 8))
    stays = jnp.logical_and(goes[0] == s, goes[1] == c)
    return s, c, core, ctx, chips, sibling, goes, comes, stays


def ring_devices(ring):
    return [ring.dev(-1, 0), ring.dev(1, 0), ring.dev(0, 1)]


def greet(devices, moved=None):
    barrier = pltpu.get_barrier_semaphore()
    for d in devices:
        pl.semaphore_signal(barrier, inc=1, device_id=d, device_id_type=MESH)
    if moved is not None:
        goes, comes, stays = moved

        @pl.when(jnp.logical_not(stays))
        def _():
            for d in (goes, comes):
                pl.semaphore_signal(barrier, inc=1, device_id=d, device_id_type=MESH)
            pl.semaphore_wait(barrier, len(devices) + 2)

        @pl.when(stays)
        def _():
            pl.semaphore_wait(barrier, len(devices))

    else:
        pl.semaphore_wait(barrier, len(devices))


def drive(*threads):
    threads = list(threads)
    while threads:
        for t in list(threads):
            try:
                next(t)
            except StopIteration:
                threads.remove(t)


def move(net, items, to, stays):
    base = net.n
    net.n += len(items)

    def remote(k, src, dst):
        return pltpu.make_async_remote_copy(
            src_ref=src, dst_ref=dst, send_sem=net.s.at[base + k], recv_sem=net.r.at[base + k],
            device_id=to, device_id_type=MESH,
        )

    @pl.when(jnp.logical_not(stays))
    def _():
        for k, (src, dst) in enumerate(items):
            remote(k, src, dst).start()

    @pl.when(stays)
    def _():
        for k, (src, dst) in enumerate(items):
            pltpu.make_async_copy(src, dst, net.r.at[base + k]).start()

    yield

    @pl.when(jnp.logical_not(stays))
    def _():
        for k, (src, dst) in enumerate(items):
            remote(k, src, dst).wait()

    @pl.when(stays)
    def _():
        for k, (src, dst) in enumerate(items):
            pltpu.make_async_copy(src, dst, net.r.at[base + k]).wait()


def gather(net, ring, items, slot=lambda i: i, sibling=None):
    left, right, pair = ring_devices(ring)
    me = ring.idx(0, 0)
    over = []

    def pass_on(places):
        if sibling is not None:
            for _, dst, _ in items:
                for i in places:
                    over.append(net.send(dst.at[slot(i)], dst.at[slot(i)], sibling))

    first, local = [], []
    for own, dst, _ in items:
        here = dst.at[slot(me)]
        src = here if own is None else own
        for n in (left, right, pair):
            first.append(net.send(src, here, n))
        if sibling is not None:
            over.append(net.send(src, here, sibling))
        if own is not None:
            local.append(net.copy(own, here))
    yield
    for c in first:
        c.wait_recv()
    second = []
    a, b, z = ring.idx(-1, 0), ring.idx(1, 0), ring.idx(0, 1)
    for _, dst, _ in items:
        for i, n in ((a, right), (z, left), (a, pair)):
            second.append(net.send(dst.at[slot(i)], dst.at[slot(i)], n))
    pass_on((a, b, z))
    yield
    for c in second:
        c.wait_recv()
    third = []
    az, bz, o, oz = ring.idx(-1, 1), ring.idx(1, 1), ring.idx(2, 0), ring.idx(2, 1)
    for _, dst, parts in items:
        for i, n, part in ((az, right, parts[0]), (bz, left, parts[1]), (o, pair, parts[2])):
            if part is not None:
                r = view(dst.at[slot(i)], part)
                third.append(net.send(r, r, n))
    pass_on((az, bz, o))
    yield
    for c in third:
        c.wait_recv()
    pass_on((oz,))
    for c in local:
        c.wait()
    for c in first + second + third:
        c.wait_send()
    if sibling is not None:
        yield
        for c in over:
            c.wait()


def reduce(net, ring, items, result):
    left, right, pair = ring_devices(ring)
    me, a, b, z = ring.idx(0, 0), ring.idx(-1, 0), ring.idx(1, 0), ring.idx(0, 1)
    az, bz, o, oz = ring.idx(-1, 1), ring.idx(1, 1), ring.idx(2, 0), ring.idx(2, 1)

    def plus(x, y):
        return (x.astype(F32) + y.astype(F32)).astype(BF)

    first, second, third = [], [], []
    for p, parts, land, _ in items:
        for n, part in zip((left, right, pair), parts):
            first.append(net.send(view(p.at[oz], part), view(land.at[0], part), n))
    yield
    for c in first:
        c.wait_recv()
    for p, parts, land, sums in items:
        for k, (i, part) in enumerate(((o, parts[2]), (bz, parts[1]), (az, parts[0]))):
            sums[k] = p[i]
            sums[(k,) + part] = plus(p[(i,) + part], land[(0,) + part])
        for k, n in enumerate((left, right, pair)):
            second.append(net.send(sums.at[k], land.at[1 + k], n))
    yield
    for c in second:
        c.wait_recv()
    for p, parts, land, sums in items:
        third.append(net.send(p.at[b], land.at[5], right))
        sums[3] = (p[a].astype(F32) + land[1].astype(F32) + land[3].astype(F32)).astype(BF)
        third.append(net.send(sums.at[3], land.at[4], left))
        sums[4] = plus(p[z], land[2])
        third.append(net.send(sums.at[4], land.at[6], pair))
    yield
    for c in third:
        c.wait_recv()
    for k, (p, parts, land, sums) in enumerate(items):
        result(
            k,
            (p[me].astype(F32) + land[4].astype(F32))
            + (land[5].astype(F32) + land[6].astype(F32)),
        )
    for c in first + second + third:
        c.wait_send()


def reduce_scratch(shape):
    return [pltpu.VMEM((7,) + shape, BF), pltpu.VMEM((5,) + shape, BF)]


def reduce_shard(net, chips, core, sibling, items, result):
    over = []
    for p, _, half, _, _, _ in items:
        over.append(net.send(p.at[1 - core], half, sibling))
    yield
    for c in over:
        c.wait_recv()
    for p, _, half, both, _, _ in items:

        @pl.loop(0, 8)
        def _(j):
            both[j] = (p[core, j].astype(F32) + half[j].astype(F32)).astype(BF)

    yield from reduce(net, chips, [(i[3], i[1], i[4], i[5]) for i in items], result)
    for c in over:
        c.wait_send()


def shard_scratch(shape):
    return [pltpu.VMEM((8,) + shape, BF), pltpu.VMEM((8,) + shape, BF)] + reduce_scratch(shape)


def rms_parts(v):
    inverse = lax.rsqrt(jnp.mean(v * v, -1, keepdims=True) + EPSILON)
    return v * inverse, inverse


def rms_back(g, n, inverse):
    return inverse * (g - n * jnp.mean(g * n, -1, keepdims=True))


def remote_call(body, outs, ins, args, scratch, copies, locals_, number, vmem=None):
    sems = [
        pltpu.SemaphoreType.DMA((copies,)),
        pltpu.SemaphoreType.DMA((copies,)),
        pltpu.SemaphoreType.DMA((locals_,)),
    ]
    space = {"v": pl.BlockSpec(memory_space=pltpu.VMEM), "h": pl.BlockSpec(memory_space=pl.ANY)}
    return pl.pallas_call(
        body,
        out_shape=[jax.ShapeDtypeStruct(s, d) for s, d, _ in outs],
        in_specs=[space[k] for k in ins],
        out_specs=[space[k] for _, _, k in outs],
        scratch_shapes=list(scratch) + sems,
        compiler_params=pltpu.CompilerParams(
            collective_id=number, has_side_effects=True, vmem_limit_bytes=vmem
        ),
    )(*args)


WCOL1 = 640
WCOL2 = 768


def start_body(tok, cot, pos, w1, wo, x_all, g_all, p_all, w1_all, wo_all, ss, rs, ls):
    s, c, core, ctx, chips, sibling, goes, comes, stays = places()
    net = Net(ss, rs, ls)
    greet(ring_devices(ctx) + ring_devices(chips) + [sibling], (goes, comes, stays))

    def by_shard():
        yield from move(net, [(wo.at[c], wo_all.at[goes[0]])], goes, stays)
        yield from gather(
            net, chips, [(w1, w1_all, lanes(WCOL1)), (None, wo_all, lanes(D))],
            lambda i: i * 2 + core, sibling,
        )

    def by_ctx():
        yield from gather(net, ctx, [(tok, x_all, ROWS), (pos, p_all, ((ALL, ALL), None, None))])
        yield from gather(net, ctx, [(cot, g_all, ROWS)])

    drive(by_ctx(), by_shard())


def attn_join_body(
    part, tok, gain, w2, wd, h_all, resid_ref, w2_all, wd_all,
    hid, land, sums, ss, rs, ls,
):
    s, c, core, ctx, chips, sibling, goes, comes, stays = places()
    net = Net(ss, rs, ls)
    greet(ring_devices(ctx) + ring_devices(chips) + [sibling], (goes, comes, stays))

    def by_shard():
        yield from move(net, [(wd.at[c], wd_all.at[goes[0]])], goes, stays)
        yield from gather(
            net, chips, [(w2, w2_all, lanes(WCOL2)), (None, wd_all, lanes(D))],
            lambda i: i * 2 + core, sibling,
        )

    def got(k, total):
        resid = tok[...].astype(F32) + total
        resid_ref[...] = resid
        normed, _ = rms_parts(resid)
        hid[...] = (normed * gain[...]).astype(BF)

    def by_ctx():
        yield from reduce(net, ctx, [(part, ROWS, land, sums)], got)
        yield from gather(net, ctx, [(hid, h_all, ROWS)])

    drive(by_ctx(), by_shard())


def mlp_join_body(
    down_part, back_part, resid_ref, cot, gain, gw2, gwd,
    out_ref, ga_all, gres_ref, ggain_ref, gw2_sum, gwd_sum,
    ga, land1, sums1, land2, sums2, h1, b1, l1, t1, h2, b2, l2, t2, ss, rs, ls,
):
    s, c, core, ctx, chips, sibling, goes, comes, stays = places()
    net = Net(ss, rs, ls)
    greet(ring_devices(ctx) + ring_devices(chips) + [sibling])

    def got_shard(k, total):
        (gw2_sum, gwd_sum)[k][...] = total.astype(BF)

    def got_down(k, total):
        out_ref[...] = (resid_ref[...] + total).astype(BF)

    def got_back(k, total):
        normed, inverse = rms_parts(resid_ref[...])
        ggain_ref[...] = jnp.sum(total * normed, 0, keepdims=True)
        gres = cot[...].astype(F32) + rms_back(total * gain[...], normed, inverse)
        gres_ref[...] = gres
        ga[...] = gres.astype(BF)

    def by_ctx():
        yield from reduce(net, ctx, [(back_part, ROWS, land1, sums1)], got_back)
        yield from gather(net, ctx, [(ga, ga_all, ROWS)])

    def later():
        yield
        yield
        yield
        yield from reduce(net, ctx, [(down_part, ROWS, land2, sums2)], got_down)

    by_shard = reduce_shard(
        net, chips, core, sibling,
        [(gw2, lanes(WCOL2), h1, b1, l1, t1), (gwd, lanes(D), h2, b2, l2, t2)], got_shard,
    )
    drive(by_ctx(), later(), by_shard)


def end_body(
    part, tok, gres_ref, gain, ggain, gqk, gw1, gwo, gw2_sum, gwd_sum,
    gx_ref, small_ref, q_out, k_out, v_out, o_out, gate_out, up_out, down_out,
    land, sums, h1, b1, l1, t1, h2, b2, l2, t2,
    s1, so, a1, ao, a2, ad, own_d, sm, smc, sm2, sms, ss, rs, ls,
):
    s, c, core, ctx, chips, sibling, goes, comes, stays = places()
    net = Net(ss, rs, ls)
    ctx_peers = [(s, lax.rem(c + d, NC)) for d in range(1, NC)]
    shard_peers = [(lax.rem(s + d, NS), c) for d in range(1, NS)]
    greet(ctx_peers + shard_peers, (goes, comes, stays))

    def got_input(k, total):
        normed, inverse = rms_parts(tok[...].astype(F32))
        sm[:, 0:D] = jnp.sum(total * normed, 0, keepdims=True)
        sm[:, D : 2 * D] = ggain[...]
        sm[:, 2 * D :] = gqk[...]
        gx_ref[...] = gres_ref[...] + rms_back(total * gain[...], normed, inverse)

    def by_ctx():
        yield from reduce(net, ctx, [(part, ROWS, land, sums)], got_input)
        smc[c] = sm[...]
        sent = [net.send(sm, smc.at[c], d) for d in ctx_peers]
        yield
        for x in sent:
            x.wait()
        total = smc[0]
        for i in range(1, NC):
            total = total + smc[i]
        sm2[...] = total
        sms[s] = total
        sent = [net.send(sm2, sms.at[s], d) for d in shard_peers]
        yield
        for x in sent:
            x.wait()
        total = sms[0]
        for i in range(1, NS):
            total = total + sms[i]
        small_ref[...] = total

    def mlp():
        yield
        yield
        yield from move(net, [(gwd_sum, own_d)], comes, stays)
        yield from gather(net, ctx, [(gw2_sum, a2, lanes(WCOL2)), (own_d, ad, lanes(D))])
        for i in range(NC):
            gate_out[:, FW * i : FW * (i + 1)] = a2[i, :, 0:FW].astype(F32)
            up_out[:, FW * i : FW * (i + 1)] = a2[i, :, FW : 2 * FW].astype(F32)
            down_out[24 * i : 24 * (i + 1), :] = ad[i].astype(F32)

    def got_shard(k, total):
        (s1, so)[k][...] = total.astype(BF)

    def attn():
        yield from reduce_shard(
            net, chips, core, sibling,
            [(gw1, lanes(512), h1, b1, l1, t1), (gwo, lanes(D), h2, b2, l2, t2)], got_shard,
        )
        yield from move(net, [(so, ao.at[comes[1]])], comes, stays)
        yield from gather(net, ctx, [(s1, a1, lanes(512)), (None, ao, lanes(D))])
        for i in range(NC):
            q_out[:, QW * i : QW * (i + 1)] = a1[i, :, 0:QW].astype(F32)
            k_out[:, HD * i : HD * (i + 1)] = a1[i, :, QW : QW + HD].astype(F32)
            v_out[:, HD * i : HD * (i + 1)] = a1[i, :, QW + HD :].astype(F32)
            o_out[16 * i : 16 * (i + 1), :] = ao[i].astype(F32)

    drive(by_ctx(), attn(), mlp())


def rotate(values, cosine, sine):
    turned = jnp.concatenate([-values[..., HD // 2 :], values[..., : HD // 2]], -1)
    return values * cosine + turned * sine


def rotate_reverse(grads, cosine, sine):
    t = grads * sine
    return grads * cosine + jnp.concatenate([t[..., HD // 2 :], -t[..., : HD // 2]], -1)


def dot(a, b, dims, out=F32):
    return lax.dot_general(a, b, (dims, ((), ())), preferred_element_type=F32).astype(out)


NN = ((1,), (0,))
NT = ((1,), (1,))
TN = ((0,), (0,))


def by_owner(g, rows):
    return jnp.transpose(g.reshape(8, 2, rows, g.shape[1]), (1, 0, 2, 3))


def shards(
    tokens, positions, attn_gain, query_weight, key_matrix, value_matrix, query_gain, key_gain,
    out_weight, mlp_gain, gate_weight, up_weight, down_weight, cotangent,
):
    c = lax.axis_index("ctx")
    s = lax.axis_index("shard")
    tok, cot = tokens[0], cotangent[0]

    def cut(w, width):
        return lax.dynamic_slice(w, (0, c * width), (w.shape[0], width))

    row0 = jnp.concatenate([attn_gain, mlp_gain])[None]
    row1 = jnp.concatenate([query_gain, key_gain, jnp.zeros((112,), BF)])[None]
    gains = jnp.concatenate([row0, row1, jnp.zeros((62, 128), BF)], 0)
    w1 = jnp.concatenate(
        [cut(query_weight, QW), cut(key_matrix, HD), cut(value_matrix, HD), gains], 1
    )
    w2 = jnp.concatenate([cut(gate_weight, FW), cut(up_weight, FW)], 1)
    wo = out_weight.reshape(8, 16, D)
    wd = down_weight.reshape(8, 24, D)

    x_all, g_all, p_all, w1_all, wo_all = remote_call(
        start_body,
        [
            ((NC, T, D), BF, "h"), ((NC, T, D), BF, "h"), ((NC, 1, T), jnp.int32, "h"),
            ((NS, 64, WCOL1), BF, "h"), ((NS, 16, D), BF, "h"),
        ],
        "hhhhh", (tok, cot, positions, w1, wo), [], 80, 8, 0,
    )
    gain_attn = w1_all[:, 0, 512:576].reshape(1, D).astype(F32)
    gain_mlp = w1_all[:, 0, 576:640].reshape(1, D).astype(F32)
    gain_q = w1_all[:, 1, 512:520].reshape(HD).astype(F32)
    gain_k = w1_all[:, 1, 520:528].reshape(HD).astype(F32)
    wqkv = w1_all[:, :, 0:512].reshape(D, 512)
    wout = wo_all.reshape(QW, D)
    half = HD // 2
    freq = jnp.power(ROPE_BASE, -jnp.arange(half, dtype=F32) * (2.0 / HD))
    angle = p_all.reshape(SEQ).astype(F32)[:, None] * freq[None, :]
    cosine = jnp.concatenate([jnp.cos(angle)] * 2, -1)
    sine = jnp.concatenate([jnp.sin(angle)] * 2, -1)

    x = x_all.reshape(SEQ, D)
    normed_one, _ = rms_parts(x.astype(F32))
    hidden_one = (normed_one * gain_attn).astype(BF)
    raw = dot(hidden_one, wqkv, NN)
    value = raw[:, QW + HD :].astype(BF)
    q_raw = raw[:, :QW].reshape(SEQ, 2, HD)
    k_raw = raw[:, QW : QW + HD]
    q_normed, q_inverse = rms_parts(q_raw)
    k_normed, k_inverse = rms_parts(k_raw)
    cosine_q, sine_q = cosine[:, None, :], sine[:, None, :]
    queries = rotate(q_normed * gain_q, cosine_q, sine_q).astype(BF)
    keys = rotate(k_normed * gain_k, cosine, sine).astype(BF)
    scale = HD**-0.5
    scores = jnp.einsum("thd,nd->htn", queries, keys, preferred_element_type=F32) * scale
    order = jnp.arange(SEQ)
    allowed = order[None, :] <= order[:, None]
    scores = jnp.where(allowed, scores, BLOCKED_SCORE)
    top = jnp.max(scores, -1, keepdims=True)
    weights = jnp.where(allowed, jnp.exp(scores - top), 0.0)
    total = jnp.sum(weights, -1, keepdims=True)
    heads = (
        jnp.einsum("htn,nd->htd", weights.astype(BF), value, preferred_element_type=F32) / total
    )
    log_total = top + jnp.log(total)
    attended = jnp.transpose(heads, (1, 0, 2)).reshape(SEQ, QW).astype(BF)
    out_part = dot(attended, wout, NN, BF).reshape(NC, T, D)

    h_all, resid, w2_all, wd_all = remote_call(
        attn_join_body,
        [
            ((NC, T, D), BF, "h"), ((T, D), F32, "v"),
            ((NS, 64, WCOL2), BF, "h"), ((NS, 24, D), BF, "h"),
        ],
        "vvvhh", (out_part, tok, gain_mlp, w2, wd),
        [pltpu.VMEM((T, D), BF)] + reduce_scratch((T, D)), 80, 8, 1, 40 << 20,
    )
    hidden_two = h_all.reshape(SEQ, D)
    wgu = w2_all.reshape(D, 2 * FW)
    wdown = wd_all.reshape(FW, D)
    g_full = g_all.reshape(SEQ, D)
    both = dot(hidden_two, wgu, NN)
    gate, up = both[:, :FW], both[:, FW:]
    sig = jax.nn.sigmoid(gate)
    act = gate * sig
    mixed = (act * up).astype(BF)
    down_part = dot(mixed, wdown, NN, BF).reshape(NC, T, D)
    grad_mixed = dot(g_full, wdown, NT)
    grad_gate = (grad_mixed * up * sig * (1.0 + gate * (1.0 - sig))).astype(BF)
    grad_up = (grad_mixed * act).astype(BF)
    grad_gu = jnp.concatenate([grad_gate, grad_up], 1)
    back_part = dot(grad_gu, wgu, NT, BF).reshape(NC, T, D)
    gw2 = by_owner(dot(hidden_two, grad_gu, TN, BF), 64)
    gwd = by_owner(dot(mixed, g_full, TN, BF), 24)

    output, ga_all, grad_resid, ggain_mlp, gw2_sum, gwd_sum = remote_call(
        mlp_join_body,
        [
            ((T, D), BF, "v"), ((NC, T, D), BF, "h"), ((T, D), F32, "v"), ((1, D), F32, "v"),
            ((64, WCOL2), BF, "v"), ((24, D), BF, "v"),
        ],
        "v" * 7, (down_part, back_part, resid, cot, gain_mlp, gw2, gwd),
        [pltpu.VMEM((T, D), BF)] + reduce_scratch((T, D)) * 2
        + shard_scratch((64, WCOL2)) + shard_scratch((24, D)),
        80, 8, 2, 56 << 20,
    )
    ga = ga_all.reshape(SEQ, D)
    gwo = by_owner(dot(attended, ga, TN, BF), 16)
    grad_att = dot(ga, wout, NT, BF).reshape(SEQ, 2, HD)
    delta = jnp.einsum("thd,htd->ht", grad_att.astype(F32), heads)
    scores = jnp.einsum("thd,nd->htn", queries, keys, preferred_element_type=F32) * scale
    probs = jnp.where(allowed, jnp.exp(scores - log_total), 0.0)
    probs_bf = probs.astype(BF)
    grad_value = jnp.einsum("htn,thd->nd", probs_bf, grad_att, preferred_element_type=F32)
    grad_probs = jnp.einsum("thd,nd->htn", grad_att, value, preferred_element_type=F32)
    grad_scores = (probs * (grad_probs - delta[..., None])).astype(BF)
    grad_q = jnp.einsum("htn,nd->thd", grad_scores, keys, preferred_element_type=F32) * scale
    grad_k = jnp.einsum("htn,thd->nd", grad_scores, queries, preferred_element_type=F32) * scale
    wq = rotate_reverse(grad_q, cosine_q, sine_q)
    wk = rotate_reverse(grad_k, cosine, sine)
    gq_gain = jnp.sum(wq * q_normed, (0, 1))
    gk_gain = jnp.sum(wk * k_normed, 0)
    gq = rms_back(wq * gain_q, q_normed, q_inverse).reshape(SEQ, QW).astype(BF)
    gk = rms_back(wk * gain_k, k_normed, k_inverse).astype(BF)
    gqkv = jnp.concatenate([gq, gk, grad_value.astype(BF)], 1)
    gw1 = by_owner(dot(hidden_one, gqkv, TN, BF), 64)
    in_part = dot(gqkv, wqkv, NT, BF).reshape(NC, T, D)
    gqk = jnp.concatenate([gq_gain, gk_gain])[None]

    outs = remote_call(
        end_body,
        [
            ((T, D), F32, "v"), ((1, SMALL), F32, "v"),
            ((64, 2048), F32, "v"), ((64, 1024), F32, "v"), ((64, 1024), F32, "v"),
            ((128, D), F32, "v"), ((64, 3072), F32, "v"), ((64, 3072), F32, "v"),
            ((192, D), F32, "v"),
        ],
        "v" * 10,
        (in_part, tok, grad_resid, gain_attn, ggain_mlp, gqk, gw1, gwo, gw2_sum, gwd_sum),
        reduce_scratch((T, D)) + shard_scratch((64, 512)) + shard_scratch((16, D))
        + [
            pltpu.VMEM((64, 512), BF), pltpu.VMEM((16, D), BF),
            pltpu.VMEM((NC, 64, 512), BF), pltpu.VMEM((NC, 16, D), BF),
            pltpu.VMEM((NC, 64, WCOL2), BF), pltpu.VMEM((NC, 24, D), BF),
            pltpu.VMEM((24, D), BF),
            pltpu.VMEM((1, SMALL), F32), pltpu.VMEM((NC, 1, SMALL), F32),
            pltpu.VMEM((1, SMALL), F32), pltpu.VMEM((NS, 1, SMALL), F32),
        ],
        128, 8, 3, 56 << 20,
    )
    gx, small, gwq, gwk, gwv, gwo_out, gwg, gwu, gwd_out = outs
    small = small[0]

    def own(offset, width):
        return lax.dynamic_slice(small, (offset + s * width,), (width,))

    return (
        output[None], gx[None], own(0, 64), gwq, gwk, gwv, own(2 * D, 8), own(2 * D + HD, 8),
        gwo_out, own(D, 64), gwg, gwu, gwd_out,
    )


def solution(mesh):
    split = P("shard", "ctx", None)
    rows, vec = P("shard", None), P("shard")
    in_specs = (
        split, P("shard", "ctx"), vec, rows, rows, rows, vec, vec, rows, vec, rows, rows, rows, split,
    )
    out_specs = (split, split, vec, rows, rows, rows, vec, vec, rows, vec, rows, rows, rows)
    return jax.shard_map(shards, mesh=mesh, in_specs=in_specs, out_specs=out_specs, check_vma=False)
```

time: 1430 us -> 308 us (0.22)
  waiting for transfers between devices: 1130 us -> 0 us
  Pallas kernels: 0 us -> 212 us
  blocking collectives: 86.5 us -> 0 us
  matrix products: 101 us -> 37.8 us
  local copies, waits for them, and re-layouts: 52.1 us -> 23.9 us
  between operations: 17.9 us -> 1.67 us
    reduce_scatter x9 -> x0, waiting for transfers between devices: 660 us -> none  [the longest x1 93.3 us: shards(): lax.psum_scatter(grad_gate_w.astype(jnp.bfloat16), 'shard', scatter_dimen...]
    all_gather x9 -> x0, waiting for transfers between devices: 425 us -> none  [the longest x1 61.5 us: shards(): lax.all_gather(gate_weight, 'shard', axis=0, tiled=True)]
    pallas_call x0 -> x4, Pallas kernels: none -> 212 us  [remote_call(): pl.pallas_call(body, out_shape=[jax.ShapeDtypeStruct(s, d) for s, d, _ in...]
    unnamed x2 -> x0, blocking collectives: 71.4 us -> none
    dot_general x33 -> x18, matrix products: 101 us -> 37.8 us  [the longest x12 21.4 us: dot(): lax.dot_general(a, b, (dims, ((), ())), preferred_element_type=F32)]
    psum x1 -> x0, waiting for transfers between devices: 45.4 us -> none  [shards(): lax.psum(summed_parts[1].astype(jnp.bfloat16), 'ctx').astype(jnp.float32)]
    psum x1 -> x0, blocking collectives: 15.1 us -> none  [shards(): lax.psum(summed_parts[0].astype(jnp.bfloat16), 'ctx').astype(jnp.float32)]
  transfers between devices with their start and end apart: 19 -> 0, of which waited for: 19 -> 0; matrix products, arithmetic and copies ran while one was open for 7% -> 0% of each run, Pallas kernels for 0% -> 0%
where the time goes in v1:
time: 308 us; the launch traced here: 304 us
  Pallas kernels  212 us (69%)
  matrix products  37.8 us (12%)
  other arithmetic  28.6 us (9%)
  local copies, waits for them, and re-layouts  23.9 us (8%)
    pallas_call x4, Pallas kernels, remote_call(): pl.pallas_call(body, out_shape=[jax.ShapeDtypeStruct(s, d) for s, d, _ in...  212 us
    dot_general x12, matrix products, dot(): lax.dot_general(a, b, (dims, ((), ())), preferred_element_type=F32)  21.4 us
    reduce_sum x1, other arithmetic, shards(): total = jnp.sum(weights, -1, keepdims=True)  13.1 us
    unnamed x63, local copies, waits for them, and re-layouts  11.3 us

profile of v1, /device:TPU:1, one launch (start us, length us, event | category | flops | bytes accessed | tf_op | source)
XLA Modules:
  0.0 303.6 jit_solution(14457731550252548866)
XLA Ops:
  0.7 0.8 maximum_bitcast_fusion
  1.6 0.7 constant_dynamic-slice_fusion.6
  3.0 0.8 constant_dynamic-slice_fusion.4
  4.2 50.0 %shard_map.237 = (bf16[8,128,1024]{2,1,0:T(8,128)(2,1)}, bf16[8,128,1024]{2,1,0:T(8,128)(2,1)}, s32[8,1,128]{2,1,0:T(1,128)}, bf16[16,64,640]{2,1,0:T(8,128)(2,1)}, bf16[16,16,1024]{2,1,0:T(8,128)(2,1)}) custom-call(bf16[128,1024]{1,0:T(8,128)(2,1)} %bitcast.157, bf16[128,1024]{1,0:T(8,128)(2,1)} %bitcast.183, s32[1,128]{1,0:T(1,128)} %pos.1, ...), custom_call_target="tpu_custom_call" | custom-call | tf_op jit(solution)/shard_map/pallas_call | solution.py:299
  54.8 2.2 multiply_reduce_fusion
  57.1 0.8 slice_convert_fusion.1
  58.5 0.9 convert_reduce_fusion.1
  59.6 1.0 convert_reduce_fusion
  60.6 2.3 slice.56
  63.0 1.0 multiply_cosine_fusion
  64.0 1.9 fusion.9
  67.2 1.3 fusion.53
  69.9 1.9 fusion.4
  71.9 13.1 %fusion.6 = f32[2,1024]{1,0:T(2,128)S(1)} fusion(f32[1024,1024,2]{1,0,2:T(8,128)S(1)} %get-tuple-element.96, f32[2,1024]{1,0:T(2,128)S(1)} %get-tuple-element.95, pred[1024,1024]{0,1:T(8,128)(4,1)S(1)} %iota_compare_fusion), kind=kLoop, calls=%fused_computation.10 | loop fusion | flops 10483712 | bytes 9453568 | tf_op jit(solution)/shard_map/reduce_sum | solution.py:553
  85.0 2.9 fusion.27
  88.0 0.7 convolution_convert_fusion.2
  89.2 47.3 %shard_map.238 = (bf16[8,128,1024]{2,1,0:T(8,128)(2,1)S(1)}, f32[128,1024]{1,0:T(8,128)S(1)}, bf16[16,64,768]{2,1,0:T(8,128)(2,1)S(1)}, bf16[16,24,1024]{2,1,0:T(8,128)(2,1)S(1)}) custom-call(bf16[8,128,1024]{2,1,0:T(8,128)(2,1)S(1)} %bitcast.156, bf16[128,1024]{1,0:T(8,128)(2,1)S(1)} %bitcast.159, f32[1,1024]{1,0:T(1,128)S(1)} %reshape.240.gain, ...), custom_call_target="tpu_custom_call" | custom-call | tf_op jit(solution)/shard_map/pallas_call | solution.py:299
  136.6 1.9 fusion.54
  138.5 1.6 multiply_convert_fusion.2
  140.1 1.0 convolution_convert_fusion.6
  141.1 1.9 convolution_convert_fusion.4
  143.0 3.1 %convolution_convert_fusion.3 = bf16[1024,1024]{1,0:T(8,128)(2,1)} fusion(bf16[1024,768]{1,0:T(8,128)(2,1)S(1)} %bitcast.164, bf16[1024,384]{0,1:T(8,128)(2,1)S(1)} %get-tuple-element.72, bf16[1024,384]{0,1:T(8,128)(2,1)S(1)} %get-tuple-element.71), kind=kOutput, calls=%fused_computation.25 | convolution fusion | flops 1614807040 | bytes 5242880 | tf_op jit(solution)/shard_map/dot_general | solution.py:481
  146.1 1.3 copy.67
  147.4 0.9 copy.69
  148.3 2.6 convolution_convert_fusion
  151.0 53.9 %shard_map.239 = (bf16[128,1024]{1,0:T(8,128)(2,1)}, bf16[8,128,1024]{2,1,0:T(8,128)(2,1)}, f32[128,1024]{1,0:T(8,128)}, f32[1,1024]{1,0:T(1,128)}, bf16[64,768]{1,0:T(8,128)(2,1)}, /*index=5*/bf16[24,1024]{1,0:T(8,128)(2,1)}) custom-call(bf16[8,128,1024]{2,1,0:T(8,128)(2,1)} %bitcast.174, bf16[8,128,1024]{2,1,0:T(8,128)(2,1)} %bitcast.173, ...), custom_call_target="tpu_custom_call" | custom-call | tf_op jit(solution)/shard_map/pallas_call | solution.py:299
  205.0 2.6 fusion.26
  207.6 0.7 convolution_convert_fusion.7
  208.3 0.8 copy.70
  209.1 5.9 %fusion.21 = bf16[1024,128]{0,1:T(8,128)(2,1)S(1)} fusion(bf16[1024,2,128]{0,2,1:T(8,128)(2,1)S(1)} %bitcast.195, f32[1024,1024,2]{1,0,2:T(8,128)} %copy-done.9, f32[2,1024]{1,0:T(2,128)S(1)} %log_add_fusion, pred[1024,1024]{0,1:T(8,128)(4,1)S(1)} %iota_compare_fusion), kind=kOutput, calls=%fused_computation.42 | convolution fusion | flops 545390592 | bytes 10231808 | tf_op jit(solution)/shard_map/htn,thd->nd/dot_general | solution.py:606
  215.1 3.3 %fusion.1 = bf16[2,1024,1024]{1,2,0:T(8,128)(2,1)S(1)} fusion(f32[1024,1024,2]{1,0,2:T(8,128)S(1)} %bitcast.169, f32[2,1024]{1,0:T(2,128)S(1)} %get-tuple-element.99, f32[2,1024]{1,0:T(2,128)S(1)} %log_add_fusion, pred[1024,1024]{0,1:T(8,128)(4,1)S(1)} %iota_compare_fusion, bf16[1024,2,128]{0,2,1:T(8,128)(2,1)S(1)} %bitcast.196, f32[1024,512]{0,1:T(8,128)S(1)} %fusion.53), kind=kOutput, calls=%fused_computation.2 | convolution fusion | flops 549453824 | bytes 14434304 | tf_op jit(solution)/shard_map/thd,nd->htn/dot_general | solution.py:607
  218.4 1.5 fusion.33
  219.9 0.8 broadcast_multiply_fusion
  221.1 1.1 slice-done
  222.3 1.9 multiply_reduce_fusion.1
  225.8 1.3 convolution_convert_fusion.5
  227.1 2.6 convolution_convert_fusion.1
  229.8 1.0 copy.68
  230.8 60.4 %shard_map.240 = (f32[128,1024]{1,0:T(8,128)}, f32[1,2304]{1,0:T(1,128)}, f32[64,2048]{1,0:T(8,128)}, f32[64,1024]{1,0:T(8,128)}, f32[64,1024]{1,0:T(8,128)}, /*...) custom-call(bf16[8,128,1024]{2,1,0:T(8,128)(2,1)} %bitcast.175, ...), custom_call_target="tpu_custom_call" | custom-call | tf_op jit(solution)/shard_map/pallas_call | solution.py:299
  291.2 1.3 fusion.38
  292.5 1.2 fusion.39
  293.7 0.7 copy.80
  294.5 2.0 copy.81
  296.4 1.9 copy.82
  299.7 0.8 copy.85
  300.5 0.9 copy.86
  301.4 0.9 copy.87
  302.3 0.9 copy.88
  (92 shorter events, 9.2 us)
Async XLA Ops:
  0.6 1.0 copy-start
  54.8 9.2 %copy-start.8 = (bf16[8,128,1024]{2,1,0:T(8,128)(2,1)S(1)}, bf16[8,128,1024]{2,1,0:T(8,128)(2,1)}, u32[]{:S(2)}) copy-start(bf16[8,128,1024]{2,1,0:T(8,128)(2,1)} %get-tuple-element.37) | copy-start | bytes 6291460
  62.9 25.8 %copy-start.5 = (f32[1,1024]{1,0:T(1,128)}, f32[1,1024]{1,0:T(1,128)S(1)}, u32[]{:S(2)}) copy-start(f32[1,1024]{1,0:T(1,128)S(1)} %reshape.240.gain) | copy-start | bytes 12292
  65.9 1.2 copy-start.13
  68.5 152.3 %copy-start.6 = (f32[1024,512]{0,1:T(8,128)}, f32[1024,512]{0,1:T(8,128)S(1)}, u32[]{:S(2)}) copy-start(f32[1024,512]{0,1:T(8,128)S(1)} %fusion.53) | copy-start | bytes 6291460
  71.8 13.2 %copy-start.9 = (f32[1024,1024,2]{1,0,2:T(8,128)}, f32[1024,1024,2]{1,0,2:T(8,128)S(1)}, u32[]{:S(2)}) copy-start(f32[1024,1024,2]{1,0,2:T(8,128)S(1)} %get-tuple-element.96) | copy-start | bytes 25165828
  85.0 3.0 copy-start.12
  88.0 0.8 copy-start.19
  88.0 1.1 copy-start.2
  88.0 1.3 copy-start.4
  136.6 1.9 copy-start.3
  136.6 1.9 copy-start.24
  204.9 2.6 copy-start.11
  204.9 2.6 copy-start.20
  207.6 7.5 %slice-start.1 = ((s8[8388608]{0:T(1024)(128)(4,1)}), s8[4194304]{0:T(1024)(128)(4,1)S(1)}, s32[]{:S(2)}) async-start(s8[8388608]{0:T(1024)(128)(4,1)} %bitcast.168), calls=%async_computation.1 | async-start | bytes 8388608
  209.1 5.9 %slice-start.2 = ((s8[8388608]{0:T(1024)(128)(4,1)}), s8[4194304]{0:T(1024)(128)(4,1)S(1)}, s32[]{:S(2)}) async-start(s8[8388608]{0:T(1024)(128)(4,1)} %bitcast.168), calls=%async_computation.2 | async-start | bytes 8388608
  221.0 1.2 slice-start
  222.3 2.5 copy-start.7
  224.2 1.6 copy-start.10
  225.8 1.3 copy-start.14
  230.8 63.0 %copy-start.21 = (bf16[128,1024]{1,0:T(8,128)(2,1)S(1)}, bf16[128,1024]{1,0:T(8,128)(2,1)}, u32[]{:S(2)}) copy-start(bf16[128,1024]{1,0:T(8,128)(2,1)} %get-tuple-element.46) | copy-start | bytes 786436
  291.2 7.1 %copy-start.23 = (f32[64,1024]{1,0:T(8,128)S(1)}, f32[64,1024]{1,0:T(8,128)}, u32[]{:S(2)}) copy-start(f32[64,1024]{1,0:T(8,128)} %get-tuple-element.128) | copy-start | bytes 786436
  291.2 7.8 %copy-start.22 = (f32[64,1024]{1,0:T(8,128)S(1)}, f32[64,1024]{1,0:T(8,128)}, u32[]{:S(2)}) copy-start(f32[64,1024]{1,0:T(8,128)} %get-tuple-element.129) | copy-start | bytes 786436
  291.2 8.5 %copy-start.18 = (f32[128,1024]{1,0:T(8,128)S(1)}, f32[128,1024]{1,0:T(8,128)}, u32[]{:S(2)}) copy-start(f32[128,1024]{1,0:T(8,128)} %get-tuple-element.132) | copy-start | bytes 1572868
  294.4 6.0 %copy-start.17 = (f32[64,3072]{1,0:T(8,128)S(1)}, f32[64,3072]{1,0:T(8,128)}, u32[]{:S(2)}) copy-start(f32[64,3072]{1,0:T(8,128)} %get-tuple-element.134) | copy-start | bytes 2359300
  298.3 3.1 %copy-start.16 = (f32[64,3072]{1,0:T(8,128)S(1)}, f32[64,3072]{1,0:T(8,128)}, u32[]{:S(2)}) copy-start(f32[64,3072]{1,0:T(8,128)} %get-tuple-element.135) | copy-start | bytes 2359300
  299.7 2.6 copy-start.15
  299.7 3.4 %copy-start.1 = (bf16[64,2048]{1,0:T(8,128)(2,1)S(1)}, bf16[64,2048]{1,0:T(8,128)(2,1)}, u32[]{:S(2)}) copy-start(bf16[64,2048]{1,0:T(8,128)(2,1)} %param.17) | copy-start | bytes 786436

commit v2 on v1

--- a/solution.py
+++ b/solution.py
@@ -23,7 +23,6 @@
 SMALL = 2304
 
 ALL = slice(None)
-ROWS = ((slice(0, 48), ALL), (slice(48, 96), ALL), (slice(96, 128), ALL))
 
 
 def lanes(width):
@@ -163,13 +162,13 @@
 
     def pass_on(places):
         if sibling is not None:
-            for _, dst, _ in items:
+            for _, at, _ in items:
                 for i in places:
-                    over.append(net.send(dst.at[slot(i)], dst.at[slot(i)], sibling))
+                    over.append(net.send(at(slot(i)), at(slot(i)), sibling))
 
     first, local = [], []
-    for own, dst, _ in items:
-        here = dst.at[slot(me)]
+    for own, at, _ in items:
+        here = at(slot(me))
         src = here if own is None else own
         for n in (left, right, pair):
             first.append(net.send(src, here, n))
@@ -182,19 +181,19 @@
         c.wait_recv()
     second = []
     a, b, z = ring.idx(-1, 0), ring.idx(1, 0), ring.idx(0, 1)
-    for _, dst, _ in items:
+    for _, at, _ in items:
         for i, n in ((a, right), (z, left), (a, pair)):
-            second.append(net.send(dst.at[slot(i)], dst.at[slot(i)], n))
+            second.append(net.send(at(slot(i)), at(slot(i)), n))
     pass_on((a, b, z))
     yield
     for c in second:
         c.wait_recv()
     third = []
     az, bz, o, oz = ring.idx(-1, 1), ring.idx(1, 1), ring.idx(2, 0), ring.idx(2, 1)
-    for _, dst, parts in items:
+    for _, at, parts in items:
         for i, n, part in ((az, right, parts[0]), (bz, left, parts[1]), (o, pair, parts[2])):
             if part is not None:
-                r = view(dst.at[slot(i)], part)
+                r = view(at(slot(i)), part)
                 third.append(net.send(r, r, n))
     pass_on((az, bz, o))
     yield
@@ -222,36 +221,58 @@
     first, second, third = [], [], []
     for p, parts, land, _ in items:
         for n, part in zip((left, right, pair), parts):
-            first.append(net.send(view(p.at[oz], part), view(land.at[0], part), n))
+            first.append(net.send(view(p(oz), part), view(land.at[0], part), n))
     yield
     for c in first:
         c.wait_recv()
     for p, parts, land, sums in items:
-        for k, (i, part) in enumerate(((o, parts[2]), (bz, parts[1]), (az, parts[0]))):
-            sums[k] = p[i]
-            sums[(k,) + part] = plus(p[(i,) + part], land[(0,) + part])
-        for k, n in enumerate((left, right, pair)):
+        for k, (i, part, n) in enumerate(
+            ((o, parts[2], left), (bz, parts[1], right), (az, parts[0], pair))
+        ):
+            sums[k] = p(i)[...]
+            sums[(k,) + part] = plus(p(i)[part], land[(0,) + part])
             second.append(net.send(sums.at[k], land.at[1 + k], n))
     yield
     for c in second:
         c.wait_recv()
     for p, parts, land, sums in items:
-        third.append(net.send(p.at[b], land.at[5], right))
-        sums[3] = (p[a].astype(F32) + land[1].astype(F32) + land[3].astype(F32)).astype(BF)
+        third.append(net.send(p(b), land.at[5], right))
+        sums[4] = plus(p(z)[...], land[2])
+        third.append(net.send(sums.at[4], land.at[6], pair))
+        sums[3] = (p(a)[...].astype(F32) + land[1].astype(F32) + land[3].astype(F32)).astype(BF)
         third.append(net.send(sums.at[3], land.at[4], left))
-        sums[4] = plus(p[z], land[2])
-        third.append(net.send(sums.at[4], land.at[6], pair))
     yield
     for c in third:
         c.wait_recv()
     for k, (p, parts, land, sums) in enumerate(items):
         result(
             k,
-            (p[me].astype(F32) + land[4].astype(F32))
+            (p(me)[...].astype(F32) + land[4].astype(F32))
             + (land[5].astype(F32) + land[6].astype(F32)),
         )
     for c in first + second + third:
         c.wait_send()
+
+
+def at(ref):
+    return lambda i: ref.at[i]
+
+
+CHUNKS = 2
+CROWS = T // CHUNKS
+CPARTS = ((slice(0, 32), ALL), (slice(32, 48), ALL), (slice(48, 64), ALL))
+
+
+def rows(h):
+    return pl.ds(CROWS * h, CROWS)
+
+
+def chunk(ref, h):
+    return lambda i: ref.at[i, rows(h)]
+
+
+def chunk_scratch():
+    return [pltpu.VMEM((7, CROWS, D), BF), pltpu.VMEM((5, CROWS, D), BF)] * CHUNKS
 
 
 def reduce_scratch(shape):
@@ -271,7 +292,7 @@
         def _(j):
             both[j] = (p[core, j].astype(F32) + half[j].astype(F32)).astype(BF)
 
-    yield from reduce(net, chips, [(i[3], i[1], i[4], i[5]) for i in items], result)
+    yield from reduce(net, chips, [(at(i[3]), i[1], i[4], i[5]) for i in items], result)
     for c in over:
         c.wait_send()
 
@@ -287,6 +308,15 @@
 
 def rms_back(g, n, inverse):
     return inverse * (g - n * jnp.mean(g * n, -1, keepdims=True))
+
+
+def dot(a, b, dims, out=F32):
+    return lax.dot_general(a, b, (dims, ((), ())), preferred_element_type=F32).astype(out)
+
+
+NN = ((1,), (0,))
+NT = ((1,), (1,))
+TN = ((0,), (0,))
 
 
 def remote_call(body, outs, ins, args, scratch, copies, locals_, number, vmem=None):
@@ -312,96 +342,158 @@
 WCOL2 = 768
 
 
-def start_body(tok, cot, pos, w1, wo, x_all, g_all, p_all, w1_all, wo_all, ss, rs, ls):
-    s, c, core, ctx, chips, sibling, goes, comes, stays = places()
-    net = Net(ss, rs, ls)
-    greet(ring_devices(ctx) + ring_devices(chips) + [sibling], (goes, comes, stays))
-
-    def by_shard():
-        yield from move(net, [(wo.at[c], wo_all.at[goes[0]])], goes, stays)
-        yield from gather(
-            net, chips, [(w1, w1_all, lanes(WCOL1)), (None, wo_all, lanes(D))],
-            lambda i: i * 2 + core, sibling,
-        )
-
-    def by_ctx():
-        yield from gather(net, ctx, [(tok, x_all, ROWS), (pos, p_all, ((ALL, ALL), None, None))])
-        yield from gather(net, ctx, [(cot, g_all, ROWS)])
-
-    drive(by_ctx(), by_shard())
-
-
-def attn_join_body(
-    part, tok, gain, w2, wd, h_all, resid_ref, w2_all, wd_all,
-    hid, land, sums, ss, rs, ls,
+def start_body(
+    tok, cot, pos, w1, wo, w2, wd, x_all, g_all, p_all, w1_all, wo_all, w2_all, wd_all, ss, rs, ls
 ):
     s, c, core, ctx, chips, sibling, goes, comes, stays = places()
     net = Net(ss, rs, ls)
     greet(ring_devices(ctx) + ring_devices(chips) + [sibling], (goes, comes, stays))
 
     def by_shard():
-        yield from move(net, [(wd.at[c], wd_all.at[goes[0]])], goes, stays)
+        moved = [(wo.at[c], wo_all.at[goes[0]]), (wd.at[c], wd_all.at[goes[0]])]
+        yield from move(net, moved, goes, stays)
         yield from gather(
-            net, chips, [(w2, w2_all, lanes(WCOL2)), (None, wd_all, lanes(D))],
+            net, chips,
+            [
+                (w1, at(w1_all), lanes(WCOL1)), (None, at(wo_all), lanes(D)),
+                (w2, at(w2_all), lanes(WCOL2)), (None, at(wd_all), lanes(D)),
+            ],
             lambda i: i * 2 + core, sibling,
         )
 
-    def got(k, total):
-        resid = tok[...].astype(F32) + total
-        resid_ref[...] = resid
-        normed, _ = rms_parts(resid)
-        hid[...] = (normed * gain[...]).astype(BF)
-
-    def by_ctx():
-        yield from reduce(net, ctx, [(part, ROWS, land, sums)], got)
-        yield from gather(net, ctx, [(hid, h_all, ROWS)])
-
-    drive(by_ctx(), by_shard())
-
-
-def mlp_join_body(
-    down_part, back_part, resid_ref, cot, gain, gw2, gwd,
+    def by_ctx(h):
+        items = [(tok.at[rows(h)], chunk(x_all, h), CPARTS)]
+        if h == 0:
+            items.append((pos, at(p_all), ((ALL, ALL), None, None)))
+        yield from gather(net, ctx, items)
+        yield from gather(net, ctx, [(cot.at[rows(h)], chunk(g_all, h), CPARTS)])
+
+    drive(*[by_ctx(h) for h in range(CHUNKS)], by_shard())
+
+
+def mid_body(
+    part, tok, cot, gain, wgu, wd, g_all,
     out_ref, ga_all, gres_ref, ggain_ref, gw2_sum, gwd_sum,
-    ga, land1, sums1, land2, sums2, h1, b1, l1, t1, h2, b2, l2, t2, ss, rs, ls,
+    h_all, mixed, ggu, down_part, back_part, resid, ga, gw2, gwd, gwd_f,
+    la0, sa0, la1, sa1, lb0, sb0, lb1, sb1, lc0, sc0, lc1, sc1,
+    h1, b1, l1, t1, h2, b2, l2, t2, ss, rs, ls,
 ):
     s, c, core, ctx, chips, sibling, goes, comes, stays = places()
     net = Net(ss, rs, ls)
     greet(ring_devices(ctx) + ring_devices(chips) + [sibling])
 
+    def forward(h, land, sums):
+        def got(k, total):
+            r = tok[rows(h)].astype(F32) + total
+            resid[rows(h)] = r
+            normed, _ = rms_parts(r)
+            h_all[c, rows(h)] = (normed * gain[...]).astype(BF)
+
+        yield from reduce(net, ctx, [(chunk(part, h), CPARTS, land, sums)], got)
+        yield from gather(net, ctx, [(None, chunk(h_all, h), CPARTS)])
+
+    def block(i):
+        both = dot(h_all[i], wgu[...], NN)
+        gate, up = both[:, :FW], both[:, FW:]
+        sig = jax.nn.sigmoid(gate)
+        act = gate * sig
+        m = (act * up).astype(BF)
+        mixed[i] = m
+        gm = dot(g_all[i], wd[...], NT)
+        gg = (gm * up * sig * (1.0 + gate * (1.0 - sig))).astype(BF)
+        gu = (gm * act).astype(BF)
+        ggu[i, :, 0:FW] = gg
+        ggu[i, :, FW:] = gu
+        back_part[i] = dot(jnp.concatenate([gg, gu], 1), wgu[...], NT, BF)
+        down_part[i] = dot(m, wd[...], NN, BF)
+
+    def blocks(places):
+        n = len(places)
+
+        @pl.loop(0, n)
+        def _(j):
+            i = places[0]
+            for k in range(1, n):
+                i = jnp.where(j == k, places[k], i)
+            block(i)
+
+    def work():
+        yield
+        yield
+        yield
+        blocks([c])
+        yield
+        blocks([ctx.idx(-1, 0), ctx.idx(1, 0), ctx.idx(0, 1)])
+        yield
+        blocks([ctx.idx(-1, 1), ctx.idx(1, 1), ctx.idx(2, 0)])
+        yield
+        blocks([ctx.idx(2, 1)])
+
+    drive(forward(0, la0, sa0), forward(1, la1, sa1), work())
+
+    def got_back(h):
+        def got(k, total):
+            normed, inverse = rms_parts(resid[rows(h)])
+            g = jnp.sum(total * normed, 0, keepdims=True)
+            if h == 0:
+                ggain_ref[...] = g
+            else:
+                ggain_ref[...] += g
+            gres = cot[rows(h)].astype(F32) + rms_back(total * gain[...], normed, inverse)
+            gres_ref[rows(h)] = gres
+            ga[rows(h)] = gres.astype(BF)
+
+        return got
+
+    def backward(h, land, sums):
+        yield from reduce(net, ctx, [(chunk(back_part, h), CPARTS, land, sums)], got_back(h))
+        yield from gather(net, ctx, [(ga.at[rows(h)], chunk(ga_all, h), CPARTS)])
+
+    def later(h, land, sums):
+        def got(k, total):
+            out_ref[rows(h)] = (resid[rows(h)] + total).astype(BF)
+
+        yield
+        yield
+        yield
+        yield
+        yield from reduce(net, ctx, [(chunk(down_part, h), CPARTS, land, sums)], got)
+
     def got_shard(k, total):
         (gw2_sum, gwd_sum)[k][...] = total.astype(BF)
 
-    def got_down(k, total):
-        out_ref[...] = (resid_ref[...] + total).astype(BF)
-
-    def got_back(k, total):
-        normed, inverse = rms_parts(resid_ref[...])
-        ggain_ref[...] = jnp.sum(total * normed, 0, keepdims=True)
-        gres = cot[...].astype(F32) + rms_back(total * gain[...], normed, inverse)
-        gres_ref[...] = gres
-        ga[...] = gres.astype(BF)
-
-    def by_ctx():
-        yield from reduce(net, ctx, [(back_part, ROWS, land1, sums1)], got_back)
-        yield from gather(net, ctx, [(ga, ga_all, ROWS)])
-
-    def later():
-        yield
-        yield
-        yield
-        yield from reduce(net, ctx, [(down_part, ROWS, land2, sums2)], got_down)
-
-    by_shard = reduce_shard(
-        net, chips, core, sibling,
-        [(gw2, lanes(WCOL2), h1, b1, l1, t1), (gwd, lanes(D), h2, b2, l2, t2)], got_shard,
+    def grads():
+        for q in range(2):
+
+            @pl.loop(4 * q, 4 * q + 4)
+            def _(j):
+                left = h_all[:, :, pl.ds(pl.multiple_of(j * 128, 128), 128)].reshape(SEQ, 128)
+                g = dot(left, ggu[...].reshape(SEQ, 2 * FW), TN, BF)
+                gw2[0, j] = g[0:64]
+                gw2[1, j] = g[64:128]
+
+            yield
+        for j in range(3):
+            left = mixed[:, :, 128 * j : 128 * (j + 1)].reshape(SEQ, 128)
+            gwd_f[128 * j : 128 * (j + 1)] = dot(left, g_all[...].reshape(SEQ, D), TN)
+        for i in range(NS):
+            gwd[i % 2, i // 2] = gwd_f[24 * i : 24 * (i + 1)].astype(BF)
+        yield
+        yield from reduce_shard(
+            net, chips, core, sibling,
+            [(gw2, lanes(WCOL2), h1, b1, l1, t1), (gwd, lanes(D), h2, b2, l2, t2)], got_shard,
+        )
+
+    drive(
+        backward(0, lb0, sb0), backward(1, lb1, sb1),
+        later(0, lc0, sc0), later(1, lc1, sc1), grads(),
     )
-    drive(by_ctx(), later(), by_shard)
 
 
 def end_body(
     part, tok, gres_ref, gain, ggain, gqk, gw1, gwo, gw2_sum, gwd_sum,
     gx_ref, small_ref, q_out, k_out, v_out, o_out, gate_out, up_out, down_out,
-    land, sums, h1, b1, l1, t1, h2, b2, l2, t2,
+    la0, sa0, la1, sa1, h1, b1, l1, t1, h2, b2, l2, t2,
     s1, so, a1, ao, a2, ad, own_d, sm, smc, sm2, sms, ss, rs, ls,
 ):
     s, c, core, ctx, chips, sibling, goes, comes, stays = places()
@@ -410,15 +502,28 @@
     shard_peers = [(lax.rem(s + d, NS), c) for d in range(1, NS)]
     greet(ctx_peers + shard_peers, (goes, comes, stays))
 
-    def got_input(k, total):
-        normed, inverse = rms_parts(tok[...].astype(F32))
-        sm[:, 0:D] = jnp.sum(total * normed, 0, keepdims=True)
+    def got_input(h):
+        def got(k, total):
+            normed, inverse = rms_parts(tok[rows(h)].astype(F32))
+            g = jnp.sum(total * normed, 0, keepdims=True)
+            if h == 0:
+                sm[:, 0:D] = g
+            else:
+                sm[:, 0:D] += g
+            gx_ref[rows(h)] = gres_ref[rows(h)] + rms_back(total * gain[...], normed, inverse)
+
+        return got
+
+    def by_ctx(h, land, sums):
+        yield from reduce(net, ctx, [(chunk(part, h), CPARTS, land, sums)], got_input(h))
+
+    def small():
+        yield
+        yield
+        yield
+        yield
         sm[:, D : 2 * D] = ggain[...]
         sm[:, 2 * D :] = gqk[...]
-        gx_ref[...] = gres_ref[...] + rms_back(total * gain[...], normed, inverse)
-
-    def by_ctx():
-        yield from reduce(net, ctx, [(part, ROWS, land, sums)], got_input)
         smc[c] = sm[...]
         sent = [net.send(sm, smc.at[c], d) for d in ctx_peers]
         yield
@@ -442,7 +547,7 @@
         yield
         yield
         yield from move(net, [(gwd_sum, own_d)], comes, stays)
-        yield from gather(net, ctx, [(gw2_sum, a2, lanes(WCOL2)), (own_d, ad, lanes(D))])
+        yield from gather(net, ctx, [(gw2_sum, at(a2), lanes(WCOL2)), (own_d, at(ad), lanes(D))])
         for i in range(NC):
             gate_out[:, FW * i : FW * (i + 1)] = a2[i, :, 0:FW].astype(F32)
             up_out[:, FW * i : FW * (i + 1)] = a2[i, :, FW : 2 * FW].astype(F32)
@@ -457,14 +562,14 @@
             [(gw1, lanes(512), h1, b1, l1, t1), (gwo, lanes(D), h2, b2, l2, t2)], got_shard,
         )
         yield from move(net, [(so, ao.at[comes[1]])], comes, stays)
-        yield from gather(net, ctx, [(s1, a1, lanes(512)), (None, ao, lanes(D))])
+        yield from gather(net, ctx, [(s1, at(a1), lanes(512)), (None, at(ao), lanes(D))])
         for i in range(NC):
             q_out[:, QW * i : QW * (i + 1)] = a1[i, :, 0:QW].astype(F32)
             k_out[:, HD * i : HD * (i + 1)] = a1[i, :, QW : QW + HD].astype(F32)
             v_out[:, HD * i : HD * (i + 1)] = a1[i, :, QW + HD :].astype(F32)
             o_out[16 * i : 16 * (i + 1), :] = ao[i].astype(F32)
 
-    drive(by_ctx(), attn(), mlp())
+    drive(by_ctx(0, la0, sa0), by_ctx(1, la1, sa1), small(), attn(), mlp())
 
 
 def rotate(values, cosine, sine):
@@ -475,15 +580,6 @@
 def rotate_reverse(grads, cosine, sine):
     t = grads * sine
     return grads * cosine + jnp.concatenate([t[..., HD // 2 :], -t[..., : HD // 2]], -1)
-
-
-def dot(a, b, dims, out=F32):
-    return lax.dot_general(a, b, (dims, ((), ())), preferred_element_type=F32).astype(out)
-
-
-NN = ((1,), (0,))
-NT = ((1,), (1,))
-TN = ((0,), (0,))
 
 
 def by_owner(g, rows):
@@ -511,13 +607,14 @@
     wo = out_weight.reshape(8, 16, D)
     wd = down_weight.reshape(8, 24, D)
 
-    x_all, g_all, p_all, w1_all, wo_all = remote_call(
+    x_all, g_all, p_all, w1_all, wo_all, w2_all, wd_all = remote_call(
         start_body,
         [
             ((NC, T, D), BF, "h"), ((NC, T, D), BF, "h"), ((NC, 1, T), jnp.int32, "h"),
             ((NS, 64, WCOL1), BF, "h"), ((NS, 16, D), BF, "h"),
+            ((NS, 64, WCOL2), BF, "h"), ((NS, 24, D), BF, "h"),
         ],
-        "hhhhh", (tok, cot, positions, w1, wo), [], 80, 8, 0,
+        "hhhhhhh", (tok, cot, positions, w1, wo, w2, wd), [], 128, 8, 0,
     )
     gain_attn = w1_all[:, 0, 512:576].reshape(1, D).astype(F32)
     gain_mlp = w1_all[:, 0, 576:640].reshape(1, D).astype(F32)
@@ -558,43 +655,22 @@
     attended = jnp.transpose(heads, (1, 0, 2)).reshape(SEQ, QW).astype(BF)
     out_part = dot(attended, wout, NN, BF).reshape(NC, T, D)
 
-    h_all, resid, w2_all, wd_all = remote_call(
-        attn_join_body,
-        [
-            ((NC, T, D), BF, "h"), ((T, D), F32, "v"),
-            ((NS, 64, WCOL2), BF, "h"), ((NS, 24, D), BF, "h"),
-        ],
-        "vvvhh", (out_part, tok, gain_mlp, w2, wd),
-        [pltpu.VMEM((T, D), BF)] + reduce_scratch((T, D)), 80, 8, 1, 40 << 20,
-    )
-    hidden_two = h_all.reshape(SEQ, D)
-    wgu = w2_all.reshape(D, 2 * FW)
-    wdown = wd_all.reshape(FW, D)
-    g_full = g_all.reshape(SEQ, D)
-    both = dot(hidden_two, wgu, NN)
-    gate, up = both[:, :FW], both[:, FW:]
-    sig = jax.nn.sigmoid(gate)
-    act = gate * sig
-    mixed = (act * up).astype(BF)
-    down_part = dot(mixed, wdown, NN, BF).reshape(NC, T, D)
-    grad_mixed = dot(g_full, wdown, NT)
-    grad_gate = (grad_mixed * up * sig * (1.0 + gate * (1.0 - sig))).astype(BF)
-    grad_up = (grad_mixed * act).astype(BF)
-    grad_gu = jnp.concatenate([grad_gate, grad_up], 1)
-    back_part = dot(grad_gu, wgu, NT, BF).reshape(NC, T, D)
-    gw2 = by_owner(dot(hidden_two, grad_gu, TN, BF), 64)
-    gwd = by_owner(dot(mixed, g_full, TN, BF), 24)
-
     output, ga_all, grad_resid, ggain_mlp, gw2_sum, gwd_sum = remote_call(
-        mlp_join_body,
+        mid_body,
         [
             ((T, D), BF, "v"), ((NC, T, D), BF, "h"), ((T, D), F32, "v"), ((1, D), F32, "v"),
             ((64, WCOL2), BF, "v"), ((24, D), BF, "v"),
         ],
-        "v" * 7, (down_part, back_part, resid, cot, gain_mlp, gw2, gwd),
-        [pltpu.VMEM((T, D), BF)] + reduce_scratch((T, D)) * 2
-        + shard_scratch((64, WCOL2)) + shard_scratch((24, D)),
-        80, 8, 2, 56 << 20,
+        "v" * 7,
+        (out_part, tok, cot, gain_mlp, w2_all.reshape(D, 2 * FW), wd_all.reshape(FW, D), g_all),
+        [
+            pltpu.VMEM((NC, T, D), BF), pltpu.VMEM((NC, T, FW), BF), pltpu.VMEM((NC, T, 2 * FW), BF),
+            pltpu.VMEM((NC, T, D), BF), pltpu.VMEM((NC, T, D), BF), pltpu.VMEM((T, D), F32),
+            pltpu.VMEM((T, D), BF), pltpu.VMEM((2, 8, 64, WCOL2), BF), pltpu.VMEM((2, 8, 24, D), BF),
+            pltpu.VMEM((FW, D), F32),
+        ]
+        + chunk_scratch() * 3 + shard_scratch((64, WCOL2)) + shard_scratch((24, D)),
+        128, 8, 1, 58 << 20,
     )
     ga = ga_all.reshape(SEQ, D)
     gwo = by_owner(dot(attended, ga, TN, BF), 16)
@@ -629,7 +705,7 @@
         ],
         "v" * 10,
         (in_part, tok, grad_resid, gain_attn, ggain_mlp, gqk, gw1, gwo, gw2_sum, gwd_sum),
-        reduce_scratch((T, D)) + shard_scratch((64, 512)) + shard_scratch((16, D))
+        chunk_scratch() + shard_scratch((64, 512)) + shard_scratch((16, D))
         + [
             pltpu.VMEM((64, 512), BF), pltpu.VMEM((16, D), BF),
             pltpu.VMEM((NC, 64, 512), BF), pltpu.VMEM((NC, 16, D), BF),
@@ -638,7 +714,7 @@
             pltpu.VMEM((1, SMALL), F32), pltpu.VMEM((NC, 1, SMALL), F32),
             pltpu.VMEM((1, SMALL), F32), pltpu.VMEM((NS, 1, SMALL), F32),
         ],
-        128, 8, 3, 56 << 20,
+        128, 8, 2, 56 << 20,
     )
     gx, small, gwq, gwk, gwv, gwo_out, gwg, gwu, gwd_out = outs
     small = small[0]

time: 308 us -> 276 us (0.90); the launches traced: 304 us -> 275 us
  other arithmetic: 28.6 us -> 17.8 us
  matrix products: 37.8 us -> 28.5 us
  Pallas kernels: 212 us -> 203 us
    reduce_sum x1, other arithmetic: 13.1 us -> 2.43 us  [shards(): total = jnp.sum(weights, -1, keepdims=True)]
    dot_general x12 -> x6, matrix products: 21.4 us -> 10.9 us  [dot(): lax.dot_general(a, b, (dims, ((), ())), preferred_element_type=F32)]
    pallas_call x4 -> x3, Pallas kernels: 212 us -> 203 us  [remote_call(): pl.pallas_call(body, out_shape=[jax.ShapeDtypeStruct(s, d) for s, d, _ in...]
    unnamed x63 -> x53, local copies, waits for them, and re-layouts: 11.3 us -> 14.8 us
where the time goes in v2:
time: 276 us; the launch traced here: 275 us
  Pallas kernels  203 us (74%)
  matrix products  28.5 us (10%)
  local copies, waits for them, and re-layouts  24.9 us (9%)
  other arithmetic  17.8 us (6%)
    pallas_call x3, Pallas kernels, remote_call(): pl.pallas_call(body, out_shape=[jax.ShapeDtypeStruct(s, d) for s, d, _ in...  203 us
    unnamed x53, local copies, waits for them, and re-layouts  14.8 us
    dot_general x6, matrix products, dot(): lax.dot_general(a, b, (dims, ((), ())), preferred_element_type=F32)  10.9 us
    dot_general x1, matrix products, shards(): jnp.einsum('htn,thd->nd', probs_bf, grad_att, preferred_element_type=F32)  6.3 us

profile of v2, /device:TPU:1, one launch (start us, length us, event | category | flops | bytes accessed | tf_op | source)
XLA Modules:
  0.0 275.3 jit_solution(5770440077230809072)
XLA Ops:
  0.7 0.8 maximum_bitcast_fusion
  1.6 0.7 constant_dynamic-slice_fusion.6
  2.4 0.6 maximum_maximum_fusion.w1
  3.0 0.8 constant_dynamic-slice_fusion.4
  3.8 0.7 pad_maximum_fusion.5.w2
  4.8 54.9 %shard_map.237 = (bf16[8,128,1024]{2,1,0:T(8,128)(2,1)}, bf16[8,128,1024]{2,1,0:T(8,128)(2,1)}, s32[8,1,128]{2,1,0:T(1,128)}, bf16[16,64,640]{2,1,0:T(8,128)(2,1...) custom-call(bf16[128,1024]{1,0:T(8,128)(2,1)} %bitcast.139, ...), custom_call_target="tpu_custom_call" | custom-call | tf_op jit(solution)/shard_map/pallas_call | solution.py:329
  59.8 0.8 convert_element_type.120
  60.6 2.1 multiply_reduce_fusion
  62.7 0.8 slice_convert_fusion.1
  63.4 0.7 reshape.217.gain
  64.1 0.9 convert_reduce_fusion.1
  65.2 0.9 convert_reduce_fusion
  66.2 2.3 slice.50
  68.5 0.7 reshape.216.gain
  69.2 1.0 multiply_cosine_fusion
  70.2 1.9 fusion.9
  72.7 1.3 fusion.50
  74.7 1.1 broadcast_multiply_fusion.2
  76.2 1.9 fusion.4
  78.2 2.4 fusion.6
  80.7 0.8 copy-done.3
  81.4 3.7 %fusion.26 = (bf16[1024,2,128]{0,2,1:T(8,128)(2,1)S(1)}, f32[2,1024,128]{1,2,0:T(8,128)}) fusion(f32[1024,2]{0,1:T(2,128)S(1)} %bitcast.167, f32[1024,1024,2]{1,0,2:T(8,128)S(1)} %get-tuple-element.89, f32[2,1024]{1,0:T(2,128)S(1)} %get-tuple-element.88, pred[1024,1024]{0,1:T(8,128)(4,1)S(1)} %iota_compare_fusion, f32[1024,512]{0,1:T(8,128)S(1)} %fusion.50), kind=kOutput, calls=%fused_computation.40 | convolution fusion | flops 547880960 | bytes 11288576 | tf_op jit(solution)/shard_map/htn,nd->htd/dot_general | solution.py:652
  85.1 0.8 copy-done.17
  85.9 2.1 convolution_convert_fusion.1
  88.0 89.4 %shard_map.238 = (bf16[128,1024]{1,0:T(8,128)(2,1)}, bf16[8,128,1024]{2,1,0:T(8,128)(2,1)}, f32[128,1024]{1,0:T(8,128)}, f32[1,1024]{1,0:T(1,128)}, bf16[64,768]{1,0:T(8,128)(2,1)}, /*index=5*/bf16[24,1024]{1,0:T(8,128)(2,1)}) custom-call(bf16[8,128,1024]{2,1,0:T(8,128)(2,1)} %bitcast.134, bf16[128,1024]{1,0:T(8,128)(2,1)} %bitcast.140, ...), custom_call_target="tpu_custom_call" | custom-call | tf_op jit(solution)/shard_map/pallas_call | solution.py:329
  177.5 2.8 %fusion.25 = (f32[2,1024]{1,0:T(2,128)S(1)}, bf16[1024,256]{0,1:T(8,128)(2,1)S(1)}) fusion(f32[2,1024,128]{1,2,0:T(8,128)} %get-tuple-element.91, f32[2,1024]{1,0:T(2,128)S(1)} %fusion.6, bf16[1024,1024]{1,0:T(8,128)(2,1)} %bitcast.144, bf16[256,1024]{1,0:T(8,128)(2,1)S(1)} %bitcast.148), kind=kOutput, calls=%fused_computation.38 | convolution fusion | flops 538179584 | bytes 4210688 | tf_op jit(solution)/shard_map/dot_general | solution.py:314
  180.3 0.7 convolution_convert_fusion.3
  181.0 0.8 copy.64
  181.8 6.3 %fusion.20 = bf16[1024,128]{0,1:T(8,128)(2,1)S(1)} fusion(bf16[1024,2,128]{0,2,1:T(8,128)(2,1)S(1)} %bitcast.162, f32[1024,1024,2]{1,0,2:T(8,128)} %copy-done.3, f32[2,1024]{1,0:T(2,128)S(1)} %log_add_fusion, pred[1024,1024]{0,1:T(8,128)(4,1)S(1)} %iota_compare_fusion), kind=kOutput, calls=%fused_computation.31 | convolution fusion | flops 545390592 | bytes 10231808 | tf_op jit(solution)/shard_map/htn,thd->nd/dot_general | solution.py:682
  188.2 3.3 %fusion.1 = bf16[2,1024,1024]{1,2,0:T(8,128)(2,1)S(1)} fusion(f32[1024,1024,2]{1,0,2:T(8,128)S(1)} %bitcast.136, f32[2,1024]{1,0:T(2,128)S(1)} %get-tuple-element.92, f32[2,1024]{1,0:T(2,128)S(1)} %log_add_fusion, pred[1024,1024]{0,1:T(8,128)(4,1)S(1)} %iota_compare_fusion, bf16[1024,2,128]{0,2,1:T(8,128)(2,1)S(1)} %bitcast.163, f32[1024,512]{0,1:T(8,128)S(1)} %fusion.50), kind=kOutput, calls=%fused_computation.2 | convolution fusion | flops 549453824 | bytes 14434304 | tf_op jit(solution)/shard_map/thd,nd->htn/dot_general | solution.py:683
  191.6 1.5 fusion.32
  193.1 0.8 broadcast_multiply_fusion
  194.3 0.6 copy-done.6
  196.6 1.3 convolution_convert_fusion.2
  197.9 2.7 convolution_convert_fusion
  200.6 1.1 copy.63
  201.6 58.5 %shard_map.239 = (f32[128,1024]{1,0:T(8,128)}, f32[1,2304]{1,0:T(1,128)}, f32[64,2048]{1,0:T(8,128)}, f32[64,1024]{1,0:T(8,128)}, f32[64,1024]{1,0:T(8,128)}, /*...) custom-call(bf16[8,128,1024]{2,1,0:T(8,128)(2,1)} %bitcast.142, ...), custom_call_target="tpu_custom_call" | custom-call | tf_op jit(solution)/shard_map/pallas_call | solution.py:329
  260.2 1.4 fusion.37
  261.6 1.3 fusion.38
  262.9 0.7 copy.74
  263.6 1.9 copy.75
  265.5 1.9 copy.76
  267.4 1.7 copy.77
  269.1 1.7 copy.78
  270.7 1.9 copy.79
  272.6 0.9 copy.80
  273.5 0.9 copy.81
  274.4 0.9 copy.82
  (72 shorter events, 4.4 us)
Async XLA Ops:
  0.6 1.0 copy-start
  59.7 10.5 %copy-start.2 = (bf16[8,128,1024]{2,1,0:T(8,128)(2,1)S(1)}, bf16[8,128,1024]{2,1,0:T(8,128)(2,1)}, u32[]{:S(2)}) copy-start(bf16[8,128,1024]{2,1,0:T(8,128)(2,1)} %get-tuple-element.35) | copy-start | bytes 6291460
  70.2 4.5 %copy-start.4 = (f32[1024,64]{0,1:T(8,128)}, f32[1024,64]{0,1:T(8,128)S(1)}, u32[]{:S(2)}) copy-start(f32[1024,64]{0,1:T(8,128)S(1)} %get-tuple-element.85) | copy-start | bytes 786436
  70.2 2.4 copy-start.10
  75.8 2.4 copy-start.12
  78.2 3.2 %copy-start.3 = (f32[1024,1024,2]{1,0,2:T(8,128)}, f32[1024,1024,2]{1,0,2:T(8,128)S(1)}, u32[]{:S(2)}) copy-start(f32[1024,1024,2]{1,0,2:T(8,128)S(1)} %get-tuple-element.89) | copy-start | bytes 25165828
  81.4 4.5 %copy-start.9 = (bf16[16,16,1024]{2,1,0:T(8,128)(2,1)S(1)}, bf16[16,16,1024]{2,1,0:T(8,128)(2,1)}, u32[]{:S(2)}) copy-start(bf16[16,16,1024]{2,1,0:T(8,128)(2,1)} %get-tuple-element.38) | copy-start | bytes 1572868
  85.1 0.8 copy-start.17
  177.4 2.8 %copy-start.8 = (bf16[8,128,1024]{2,1,0:T(8,128)(2,1)S(1)}, bf16[8,128,1024]{2,1,0:T(8,128)(2,1)}, u32[]{:S(2)}) copy-start(bf16[8,128,1024]{2,1,0:T(8,128)(2,1)} %get-tuple-element.43) | copy-start | bytes 6291460
  177.4 2.8 %copy-start.18 = (bf16[1024,2,128]{0,2,1:T(8,128)(2,1)S(1)}, bf16[1024,2,128]{0,2,1:T(8,128)(2,1)}, u32[]{:S(2)}) copy-start(bf16[1024,2,128]{0,2,1:T(8,128)(2,1)} %copy-done.17) | copy-start | bytes 1572868
  181.0 7.2 %slice-start = ((s8[8388608]{0:T(1024)(128)(4,1)}), s8[4194304]{0:T(1024)(128)(4,1)S(1)}, s32[]{:S(2)}) async-start(s8[8388608]{0:T(1024)(128)(4,1)} %bitcast.135), calls=%async_computation | async-start | bytes 8388608
  181.8 6.3 %slice-start.1 = ((s8[8388608]{0:T(1024)(128)(4,1)}), s8[4194304]{0:T(1024)(128)(4,1)S(1)}, s32[]{:S(2)}) async-start(s8[8388608]{0:T(1024)(128)(4,1)} %bitcast.135), calls=%async_computation.1 | async-start | bytes 8388608
  188.2 3.4 %copy-start.5 = (f32[1024,64]{0,1:T(8,128)S(1)}, f32[1024,64]{0,1:T(8,128)}, u32[]{:S(2)}) copy-start(f32[1024,64]{0,1:T(8,128)} %copy-done.4) | copy-start | bytes 786436
  191.6 1.6 copy-start.13
  193.9 1.0 copy-start.6
  195.0 1.6 copy-start.7
  196.5 1.4 copy-start.11
  200.6 62.3 %copy-start.19 = (bf16[128,1024]{1,0:T(8,128)(2,1)S(1)}, bf16[128,1024]{1,0:T(8,128)(2,1)}, u32[]{:S(2)}) copy-start(bf16[128,1024]{1,0:T(8,128)(2,1)} %get-tuple-element.42) | copy-start | bytes 786436
  260.2 12.4 %copy-start.16 = (f32[64,3072]{1,0:T(8,128)S(1)}, f32[64,3072]{1,0:T(8,128)}, u32[]{:S(2)}) copy-start(f32[64,3072]{1,0:T(8,128)} %get-tuple-element.127) | copy-start | bytes 2359300
  260.2 13.3 %copy-start.15 = (f32[64,3072]{1,0:T(8,128)S(1)}, f32[64,3072]{1,0:T(8,128)}, u32[]{:S(2)}) copy-start(f32[64,3072]{1,0:T(8,128)} %get-tuple-element.128) | copy-start | bytes 2359300
  260.2 14.2 %copy-start.14 = (f32[192,1024]{1,0:T(8,128)S(1)}, f32[192,1024]{1,0:T(8,128)}, u32[]{:S(2)}) copy-start(f32[192,1024]{1,0:T(8,128)} %get-tuple-element.129) | copy-start | bytes 2359300
  263.6 11.7 %copy-start.1 = (bf16[64,2048]{1,0:T(8,128)(2,1)S(1)}, bf16[64,2048]{1,0:T(8,128)(2,1)}, u32[]{:S(2)}) copy-start(bf16[64,2048]{1,0:T(8,128)(2,1)} %param.17) | copy-start | bytes 786436

commit v3 on v2

--- a/solution.py
+++ b/solution.py
@@ -343,7 +343,9 @@
 
 
 def start_body(
-    tok, cot, pos, w1, wo, w2, wd, x_all, g_all, p_all, w1_all, wo_all, w2_all, wd_all, ss, rs, ls
+    tok, cot, pos, w1, wo, w2, wd, freq,
+    g_all, w1_all, wo_all, w2_all, wd_all, hid, raw, qkv, tab, lse, heads, part, gvec, ghead,
+    x_all, p_all, ss, rs, ls,
 ):
     s, c, core, ctx, chips, sibling, goes, comes, stays = places()
     net = Net(ss, rs, ls)
@@ -353,22 +355,97 @@
         moved = [(wo.at[c], wo_all.at[goes[0]]), (wd.at[c], wd_all.at[goes[0]])]
         yield from move(net, moved, goes, stays)
         yield from gather(
-            net, chips,
-            [
-                (w1, at(w1_all), lanes(WCOL1)), (None, at(wo_all), lanes(D)),
-                (w2, at(w2_all), lanes(WCOL2)), (None, at(wd_all), lanes(D)),
-            ],
+            net, chips, [(w1, at(w1_all), lanes(WCOL1)), (None, at(wo_all), lanes(D))],
             lambda i: i * 2 + core, sibling,
         )
 
-    def by_ctx(h):
+    def first(h):
         items = [(tok.at[rows(h)], chunk(x_all, h), CPARTS)]
         if h == 0:
             items.append((pos, at(p_all), ((ALL, ALL), None, None)))
         yield from gather(net, ctx, items)
+
+    drive(first(0), first(1), by_shard())
+
+    def second(h):
         yield from gather(net, ctx, [(cot.at[rows(h)], chunk(g_all, h), CPARTS)])
 
-    drive(*[by_ctx(h) for h in range(CHUNKS)], by_shard())
+    def by_shard_second():
+        yield from gather(
+            net, chips, [(w2, at(w2_all), lanes(WCOL2)), (None, at(wd_all), lanes(D))],
+            lambda i: i * 2 + core, sibling,
+        )
+
+    def gains():
+        lane = lax.broadcasted_iota(jnp.int32, (8, 128), 1)
+        t = [w1_all[i, 0:16, 512:640].astype(F32)[0:8] for i in range(NS)]
+        for j in range(8):
+            x, y = t[2 * j], t[2 * j + 1]
+            low = lane < 64
+            gvec[0:1, 128 * j : 128 * (j + 1)] = jnp.where(low, x, pltpu.roll(y, 64, 1))[0:1]
+            gvec[1:2, 128 * j : 128 * (j + 1)] = jnp.where(low, pltpu.roll(x, 64, 1), y)[0:1]
+        q = jnp.zeros((8, 128), F32)
+        k = jnp.zeros((8, 128), F32)
+        for i in range(NS):
+            here = lane // 8 == i
+            q = jnp.where(here, pltpu.roll(t[i], 8 * i, 1), q)
+            k = jnp.where(here, pltpu.roll(t[i], (8 * i + 120) % 128, 1), k)
+        ghead[0:1] = q[1:2]
+        ghead[1:2] = k[1:2]
+
+    def project(i):
+        normed, _ = rms_parts(x_all[i].astype(F32))
+        h = (normed * gvec[0:1]).astype(BF)
+        hid[i] = h
+        r = dot(h, w1_all[:, :, 0:512].reshape(D, 512), NN)
+        raw[i] = r
+        angle = freq[...] * p_all[i].astype(F32)
+        cosine = jnp.cos(angle).T
+        sine = jnp.sin(angle).T
+        sine = jnp.where(lax.broadcasted_iota(jnp.int32, (T, HD), 1) < HD // 2, -sine, sine)
+        tab[i, :, 0:HD] = cosine
+        tab[i, :, HD:] = sine
+        for k in range(3):
+            n, _ = rms_parts(r[:, HD * k : HD * (k + 1)])
+            u = n * ghead[k // 2 : k // 2 + 1]
+            qkv[i, :, HD * k : HD * (k + 1)] = (u * cosine + pltpu.roll(u, 64, 1) * sine).astype(BF)
+        qkv[i, :, 3 * HD :] = r[:, 3 * HD :].astype(BF)
+
+    def attend(h, n):
+        width = 256 * (n + 1)
+        q = qkv[2 * n : 2 * n + 2, :, HD * h : HD * (h + 1)].reshape(256, HD)
+        k = qkv[0 : 2 * n + 2, :, 2 * HD : 3 * HD].reshape(width, HD)
+        v = qkv[0 : 2 * n + 2, :, 3 * HD :].reshape(width, HD)
+        score = dot(q, k, NT) * HD**-0.5
+        row = lax.broadcasted_iota(jnp.int32, (256, width), 0) + 256 * n
+        col = lax.broadcasted_iota(jnp.int32, (256, width), 1)
+        score = jnp.where(col <= row, score, BLOCKED_SCORE)
+        top = jnp.max(score, -1, keepdims=True)
+        e = jnp.exp(score - top)
+        total = jnp.sum(e, -1, keepdims=True)
+        o = dot(e.astype(BF), v, NN) / total
+        heads[2 * n : 2 * n + 2, :, HD * h : HD * (h + 1)] = o.reshape(2, T, HD)
+        lse[h, 256 * n : 256 * (n + 1)] = top + jnp.log(total)
+
+    def work():
+        gains()
+        pl.loop(0, 4)(project)
+        yield
+        pl.loop(4, 8)(project)
+        for h in range(2):
+            attend(h, 0)
+        yield
+        for n in range(1, 4):
+            for h in range(2):
+                attend(h, n)
+            if n < 3:
+                yield
+
+        @pl.loop(0, NC)
+        def _(i):
+            part[i] = dot(heads[i].astype(BF), wo_all[...].reshape(QW, D), NN, BF)
+
+    drive(second(0), second(1), by_shard_second(), work())
 
 
 def mid_body(
@@ -607,53 +684,43 @@
     wo = out_weight.reshape(8, 16, D)
     wd = down_weight.reshape(8, 24, D)
 
-    x_all, g_all, p_all, w1_all, wo_all, w2_all, wd_all = remote_call(
+    half = HD // 2
+    freq = jnp.power(ROPE_BASE, -jnp.arange(half, dtype=F32) * (2.0 / HD))
+    freq = jnp.broadcast_to(jnp.concatenate([freq, freq])[:, None], (HD, T))
+
+    (
+        g_all, w1_all, wo_all, w2_all, wd_all, hid, raw, qkv, tab, lse, heads, out_part, gvec, ghead,
+    ) = remote_call(
         start_body,
         [
-            ((NC, T, D), BF, "h"), ((NC, T, D), BF, "h"), ((NC, 1, T), jnp.int32, "h"),
-            ((NS, 64, WCOL1), BF, "h"), ((NS, 16, D), BF, "h"),
+            ((NC, T, D), BF, "h"), ((NS, 64, WCOL1), BF, "v"), ((NS, 16, D), BF, "v"),
             ((NS, 64, WCOL2), BF, "h"), ((NS, 24, D), BF, "h"),
+            ((NC, T, D), BF, "v"), ((NC, T, 512), F32, "v"), ((NC, T, 512), BF, "v"),
+            ((NC, T, 2 * HD), F32, "v"), ((2, SEQ, 1), F32, "v"), ((NC, T, QW), F32, "v"),
+            ((NC, T, D), BF, "v"), ((2, D), F32, "v"), ((2, HD), F32, "v"),
         ],
-        "hhhhhhh", (tok, cot, positions, w1, wo, w2, wd), [], 128, 8, 0,
+        "hhhhhhhv", (tok, cot, positions, w1, wo, w2, wd, freq),
+        [pltpu.VMEM((NC, T, D), BF), pltpu.VMEM((NC, 1, T), jnp.int32)], 128, 8, 0, 56 << 20,
     )
-    gain_attn = w1_all[:, 0, 512:576].reshape(1, D).astype(F32)
-    gain_mlp = w1_all[:, 0, 576:640].reshape(1, D).astype(F32)
-    gain_q = w1_all[:, 1, 512:520].reshape(HD).astype(F32)
-    gain_k = w1_all[:, 1, 520:528].reshape(HD).astype(F32)
+    gain_attn, gain_mlp = gvec[0:1], gvec[1:2]
     wqkv = w1_all[:, :, 0:512].reshape(D, 512)
     wout = wo_all.reshape(QW, D)
-    half = HD // 2
-    freq = jnp.power(ROPE_BASE, -jnp.arange(half, dtype=F32) * (2.0 / HD))
-    angle = p_all.reshape(SEQ).astype(F32)[:, None] * freq[None, :]
-    cosine = jnp.concatenate([jnp.cos(angle)] * 2, -1)
-    sine = jnp.concatenate([jnp.sin(angle)] * 2, -1)
-
-    x = x_all.reshape(SEQ, D)
-    normed_one, _ = rms_parts(x.astype(F32))
-    hidden_one = (normed_one * gain_attn).astype(BF)
-    raw = dot(hidden_one, wqkv, NN)
-    value = raw[:, QW + HD :].astype(BF)
-    q_raw = raw[:, :QW].reshape(SEQ, 2, HD)
-    k_raw = raw[:, QW : QW + HD]
-    q_normed, q_inverse = rms_parts(q_raw)
-    k_normed, k_inverse = rms_parts(k_raw)
+    cosine, sine = tab.reshape(SEQ, 2 * HD)[:, :HD], tab.reshape(SEQ, 2 * HD)[:, HD:]
+    sine = jnp.concatenate([-sine[:, :half], sine[:, half:]], 1)
     cosine_q, sine_q = cosine[:, None, :], sine[:, None, :]
-    queries = rotate(q_normed * gain_q, cosine_q, sine_q).astype(BF)
-    keys = rotate(k_normed * gain_k, cosine, sine).astype(BF)
+    gain_q, gain_k = ghead[0], ghead[1]
+    hidden_one = hid.reshape(SEQ, D)
+    raw = raw.reshape(SEQ, 512)
+    q_normed, q_inverse = rms_parts(raw[:, :QW].reshape(SEQ, 2, HD))
+    k_normed, k_inverse = rms_parts(raw[:, QW : QW + HD])
+    qkv = qkv.reshape(SEQ, 512)
+    queries, keys, value = qkv[:, :QW].reshape(SEQ, 2, HD), qkv[:, QW : QW + HD], qkv[:, QW + HD :]
     scale = HD**-0.5
-    scores = jnp.einsum("thd,nd->htn", queries, keys, preferred_element_type=F32) * scale
     order = jnp.arange(SEQ)
     allowed = order[None, :] <= order[:, None]
-    scores = jnp.where(allowed, scores, BLOCKED_SCORE)
-    top = jnp.max(scores, -1, keepdims=True)
-    weights = jnp.where(allowed, jnp.exp(scores - top), 0.0)
-    total = jnp.sum(weights, -1, keepdims=True)
-    heads = (
-        jnp.einsum("htn,nd->htd", weights.astype(BF), value, preferred_element_type=F32) / total
-    )
-    log_total = top + jnp.log(total)
-    attended = jnp.transpose(heads, (1, 0, 2)).reshape(SEQ, QW).astype(BF)
-    out_part = dot(attended, wout, NN, BF).reshape(NC, T, D)
+    log_total = lse
+    attended = heads.reshape(SEQ, QW).astype(BF)
+    heads = jnp.transpose(heads.reshape(SEQ, 2, HD), (1, 0, 2))
 
     output, ga_all, grad_resid, ggain_mlp, gw2_sum, gwd_sum = remote_call(
         mid_body,

time: 276 us -> 296 us (1.072)
  local copies, waits for them, and re-layouts: 24.9 us -> 43.3 us
  Pallas kernels: 203 us -> 220 us
  matrix products: 28.5 us -> 18.2 us
  other arithmetic: 17.8 us -> 11 us
    pallas_call x3, Pallas kernels: 203 us -> 220 us  [remote_call(): pl.pallas_call(body, out_shape=[jax.ShapeDtypeStruct(s, d) for s, d, _ in...]
    slice x1 -> x8, local copies, waits for them, and re-layouts: 0.07 us -> 12.2 us  [the longest x2 3.11 us: shards(): qkv[:, :QW].reshape(SEQ, 2, HD)]
    convert_element_type x7 -> x0, other arithmetic: 6.33 us -> none  [the longest x2 2.42 us: shards(): hidden_one = (normed_one * gain_attn).astype(BF)]
    unnamed x53 -> x44, local copies, waits for them, and re-layouts: 14.8 us -> 20.5 us
    dot_general x1, matrix products: 6.3 us -> 2.39 us  [shards(): jnp.einsum('htn,thd->nd', probs_bf, grad_att, preferred_element_type=F32)]
    dot_general x1 -> x0, matrix products: 3.71 us -> none  [shards(): jnp.einsum('htn,nd->htd', weights.astype(BF), value, preferred_element_ty...]
    unnamed x1, other arithmetic: 0.01 us -> 3.2 us
    dot_general x6 -> x4, matrix products: 10.9 us -> 7.97 us  [dot(): lax.dot_general(a, b, (dims, ((), ())), preferred_element_type=F32)]
where the time goes in v3:
time: 296 us; the launch traced here: 294 us
  Pallas kernels  220 us (74%)
  local copies, waits for them, and re-layouts  43.3 us (15%)
  matrix products  18.2 us (6%)
  other arithmetic  11 us (4%)
    pallas_call x3, Pallas kernels, remote_call(): pl.pallas_call(body, out_shape=[jax.ShapeDtypeStruct(s, d) for s, d, _ in...  220 us
    unnamed x44, local copies, waits for them, and re-layouts  20.5 us
    dot_general x4, matrix products, dot(): lax.dot_general(a, b, (dims, ((), ())), preferred_element_type=F32)  7.97 us

profile of v3, /device:TPU:1, one launch (start us, length us, event | category | flops | bytes accessed | tf_op | source)
XLA Modules:
  0.0 294.0 jit_solution(18055560078648571188)
XLA Ops:
  0.8 0.8 maximum_bitcast_fusion
  1.6 0.7 constant_dynamic-slice_fusion.6
  3.0 0.7 broadcast_in_dim.48.freq
  3.7 0.8 constant_dynamic-slice_fusion.4
  5.2 1.3 iota_compare_fusion
  6.5 73.7 %shard_map.237 = (bf16[8,128,1024]{2,1,0:T(8,128)(2,1)}, bf16[16,64,640]{2,1,0:T(8,128)(2,1)}, bf16[16,16,1024]{2,1,0:T(8,128)(2,1)}, bf16[16,64,768]{2,1,0:T(8,...) custom-call(bf16[128,1024]{1,0:T(8,128)(2,1)} %bitcast.114, ...), custom_call_target="tpu_custom_call" | custom-call | tf_op jit(solution)/shard_map/pallas_call | solution.py:329
  80.2 0.8 slice_bitcast_fusion.6
  81.0 1.6 reduce.1
  82.6 1.4 fusion.32
  83.9 87.1 %shard_map.238 = (bf16[128,1024]{1,0:T(8,128)(2,1)}, bf16[8,128,1024]{2,1,0:T(8,128)(2,1)}, f32[128,1024]{1,0:T(8,128)}, f32[1,1024]{1,0:T(1,128)}, bf16[64,768]{1,0:T(8,128)(2,1)}, /*index=5*/bf16[24,1024]{1,0:T(8,128)(2,1)}) custom-call(bf16[8,128,1024]{2,1,0:T(8,128)(2,1)} %get-tuple-element.42.part, bf16[128,1024]{1,0:T(8,128)(2,1)} %bitcast.115, ...), custom_call_target="tpu_custom_call" | custom-call | tf_op jit(solution)/shard_map/pallas_call | solution.py:329
  171.1 3.3 %convolution_convert_fusion.2 = bf16[1024,256]{0,1:T(8,128)(2,1)} fusion(bf16[1024,1024]{1,0:T(8,128)(2,1)} %bitcast.120, bf16[256,1024]{1,0:T(8,128)(2,1)S(1)} %bitcast.146), kind=kOutput, calls=%fused_computation.15 | convolution fusion | flops 537133056 | bytes 3145728 | tf_op jit(solution)/shard_map/dot_general | solution.py:314
  174.4 0.7 fusion.8
  175.7 0.8 copy.75
  176.5 1.9 slice.80
  178.4 1.3 slice.71
  180.0 1.2 copy.71
  181.5 1.9 slice.73
  183.3 1.2 copy.40
  184.6 1.9 slice.75
  186.5 2.0 copy.68
  188.5 2.3 fusion.30
  190.8 1.2 copy.69
  192.0 0.7 neg.15
  192.8 1.2 copy.70
  194.0 2.1 copy.60
  196.1 3.2 %fusion.16 = f32[2,1024]{0,1:T(8,128)} fusion(f32[2,1024,128]{2,0,1:T(2,128)} %copy.60, f32[1024,2,128]{2,1,0:T(2,128)S(1)} %reshape.129), kind=kLoop, calls=%fused_computation.23 | loop fusion | flops 522240 | bytes 2105344
  199.3 1.2 copy.61
  200.5 1.3 slice.69
  201.8 2.3 fusion.20
  204.2 2.4 fusion.13
  206.6 3.3 %fusion.1 = bf16[2,1024,1024]{1,2,0:T(8,128)(2,1)S(1)} fusion(f32[1024,1024,2]{1,0,2:T(8,128)S(1)} %fusion.20, f32[2,1024]{1,0:T(2,128)S(1)} %copy.61, f32[2,1024]{1,0:T(2,128)S(1)} %reduce.1, pred[1024,1024]{0,1:T(8,128)(4,1)S(1)} %copy-done.7, bf16[1024,2,128]{0,2,1:T(8,128)(2,1)S(1)} %bitcast.137, bf16[1024,512]{1,0:T(8,128)(2,1)S(1)} %bitcast.128), kind=kOutput, calls=%fused_computation.2 | convolution fusion | flops 549453824 | bytes 14434304 | tf_op jit(solution)/shard_map/thd,nd->htn/dot_general | solution.py:750
  209.9 1.5 fusion.19
  211.4 0.8 broadcast_multiply_fusion
  214.3 1.3 convolution_convert_fusion.1
  215.6 2.7 convolution_convert_fusion
  218.3 1.1 copy.74
  219.3 59.6 %shard_map.239 = (f32[128,1024]{1,0:T(8,128)}, f32[1,2304]{1,0:T(1,128)}, f32[64,2048]{1,0:T(8,128)}, f32[64,1024]{1,0:T(8,128)}, f32[64,1024]{1,0:T(8,128)}, /*...) custom-call(bf16[8,128,1024]{2,1,0:T(8,128)(2,1)} %bitcast.119, ...), custom_call_target="tpu_custom_call" | custom-call | tf_op jit(solution)/shard_map/pallas_call | solution.py:329
  279.0 1.4 fusion.23
  280.4 1.3 fusion.24
  281.6 0.7 copy.85
  282.3 1.9 copy.86
  284.3 1.9 copy.87
  286.1 1.7 copy.88
  287.8 1.7 copy.89
  289.5 1.9 copy.90
  291.4 0.9 copy.91
  292.2 0.9 copy.92
  293.1 0.9 copy.93
  (52 shorter events, 4.7 us)
Async XLA Ops:
  0.6 1.0 copy-start
  80.2 90.9 %copy-start.14 = (bf16[16,16,1024]{2,1,0:T(8,128)(2,1)S(1)}, bf16[16,16,1024]{2,1,0:T(8,128)(2,1)}, u32[]{:S(2)}) copy-start(bf16[16,16,1024]{2,1,0:T(8,128)(2,1)} %get-tuple-element.52) | copy-start | bytes 1572868
  171.1 3.3 %copy-start.2 = (f32[8,128,256]{2,1,0:T(8,128)S(1)}, f32[8,128,256]{2,1,0:T(8,128)}, u32[]{:S(2)}) copy-start(f32[8,128,256]{2,1,0:T(8,128)} %get-tuple-element.53) | copy-start | bytes 3145732
  171.1 3.3 %copy-start.3 = (bf16[8,128,1024]{2,1,0:T(8,128)(2,1)S(1)}, bf16[8,128,1024]{2,1,0:T(8,128)(2,1)}, u32[]{:S(2)}) copy-start(bf16[8,128,1024]{2,1,0:T(8,128)(2,1)} %get-tuple-element.51) | copy-start | bytes 6291460
  201.8 2.3 copy-start.7
  201.8 2.3 copy-start.11
  204.2 2.4 copy-start.5
  206.6 3.3 %copy-start.6 = (f32[1024,64]{0,1:T(8,128)S(1)}, f32[1024,64]{0,1:T(8,128)}, u32[]{:S(2)}) copy-start(f32[1024,64]{0,1:T(8,128)} %neg.15) | copy-start | bytes 786436
  211.4 1.0 copy-start.4
  212.7 1.6 copy-start.13
  218.3 63.4 %copy-start.12 = (bf16[128,1024]{1,0:T(8,128)(2,1)S(1)}, bf16[128,1024]{1,0:T(8,128)(2,1)}, u32[]{:S(2)}) copy-start(bf16[128,1024]{1,0:T(8,128)(2,1)} %get-tuple-element.47) | copy-start | bytes 786436
  279.0 12.4 %copy-start.10 = (f32[64,3072]{1,0:T(8,128)S(1)}, f32[64,3072]{1,0:T(8,128)}, u32[]{:S(2)}) copy-start(f32[64,3072]{1,0:T(8,128)} %get-tuple-element.126) | copy-start | bytes 2359300
  279.0 13.3 %copy-start.9 = (f32[64,3072]{1,0:T(8,128)S(1)}, f32[64,3072]{1,0:T(8,128)}, u32[]{:S(2)}) copy-start(f32[64,3072]{1,0:T(8,128)} %get-tuple-element.127) | copy-start | bytes 2359300
  279.0 14.2 %copy-start.8 = (f32[192,1024]{1,0:T(8,128)S(1)}, f32[192,1024]{1,0:T(8,128)}, u32[]{:S(2)}) copy-start(f32[192,1024]{1,0:T(8,128)} %get-tuple-element.128) | copy-start | bytes 2359300
  282.3 11.7 %copy-start.1 = (bf16[64,2048]{1,0:T(8,128)(2,1)S(1)}, bf16[64,2048]{1,0:T(8,128)(2,1)}, u32[]{:S(2)}) copy-start(bf16[64,2048]{1,0:T(8,128)(2,1)} %param.17) | copy-start | bytes 786436

commit v4 on v3

--- a/solution.py
+++ b/solution.py
@@ -450,9 +450,9 @@
 
 def mid_body(
     part, tok, cot, gain, wgu, wd, g_all,
-    out_ref, ga_all, gres_ref, ggain_ref, gw2_sum, gwd_sum,
-    h_all, mixed, ggu, down_part, back_part, resid, ga, gw2, gwd, gwd_f,
-    la0, sa0, la1, sa1, lb0, sb0, lb1, sb1, lc0, sc0, lc1, sc1,
+    ga_all, gres_ref, ggain_ref, gw2_sum, gwd_sum, down_part, resid,
+    h_all, mixed, ggu, back_part, ga, gw2, gwd, gwd_f,
+    la0, sa0, la1, sa1, lb0, sb0, lb1, sb1,
     h1, b1, l1, t1, h2, b2, l2, t2, ss, rs, ls,
 ):
     s, c, core, ctx, chips, sibling, goes, comes, stays = places()
@@ -526,16 +526,6 @@
         yield from reduce(net, ctx, [(chunk(back_part, h), CPARTS, land, sums)], got_back(h))
         yield from gather(net, ctx, [(ga.at[rows(h)], chunk(ga_all, h), CPARTS)])
 
-    def later(h, land, sums):
-        def got(k, total):
-            out_ref[rows(h)] = (resid[rows(h)] + total).astype(BF)
-
-        yield
-        yield
-        yield
-        yield
-        yield from reduce(net, ctx, [(chunk(down_part, h), CPARTS, land, sums)], got)
-
     def got_shard(k, total):
         (gw2_sum, gwd_sum)[k][...] = total.astype(BF)
 
@@ -562,22 +552,136 @@
         )
 
     drive(
-        backward(0, lb0, sb0), backward(1, lb1, sb1),
-        later(0, lc0, sc0), later(1, lc1, sc1), grads(),
+        backward(0, lb0, sb0), backward(1, lb1, sb1), grads(),
     )
 
 
 def end_body(
-    part, tok, gres_ref, gain, ggain, gqk, gw1, gwo, gw2_sum, gwd_sum,
-    gx_ref, small_ref, q_out, k_out, v_out, o_out, gate_out, up_out, down_out,
-    la0, sa0, la1, sa1, h1, b1, l1, t1, h2, b2, l2, t2,
-    s1, so, a1, ao, a2, ad, own_d, sm, smc, sm2, sms, ss, rs, ls,
+    ga_all, tok, gres_ref, resid, gvec, ghead, ggain, wo_all, gw2_sum, gwd_sum,
+    down_h, qkv_h, lse_h, heads_h, raw_h, tab_h, hid_h, w1_h,
+    out_ref, gx_ref, small_ref, a1, ao, a2, ad,
+    down_part, qkv, lse, heads, raw, tab, hid, w1_all,
+    gatt, delta, gwo_f, gk_f, gv_f, gqkv, part, gw1, gwo,
+    la0, sa0, la1, sa1, lb0, sb0, lb1, sb1, h1, b1, l1, t1, h2, b2, l2, t2,
+    s1, so, own_d, sm, smc, sm2, sms, ss, rs, ls,
 ):
     s, c, core, ctx, chips, sibling, goes, comes, stays = places()
     net = Net(ss, rs, ls)
+    loads = [
+        net.copy(x, y)
+        for x, y in (
+            (heads_h, heads), (qkv_h, qkv), (lse_h, lse), (down_h, down_part),
+            (raw_h, raw), (tab_h, tab), (hid_h, hid), (w1_h, w1_all),
+        )
+    ]
     ctx_peers = [(s, lax.rem(c + d, NC)) for d in range(1, NC)]
     shard_peers = [(lax.rem(s + d, NS), c) for d in range(1, NS)]
     greet(ctx_peers + shard_peers, (goes, comes, stays))
+
+    def feed_forward(h, land, sums):
+        def got(k, total):
+            out_ref[rows(h)] = (resid[rows(h)] + total).astype(BF)
+
+        if h == 0:
+            loads[3].wait()
+        yield from reduce(net, ctx, [(chunk(down_part, h), CPARTS, land, sums)], got)
+
+    def feed_forward_grads():
+        yield from move(net, [(gwd_sum, own_d)], comes, stays)
+        yield from gather(net, ctx, [(gw2_sum, at(a2), lanes(WCOL2)), (own_d, at(ad), lanes(D))])
+
+    def got_out(k, total):
+        so[...] = total.astype(BF)
+
+    def out_grad():
+        for j in range(2):
+            left = heads[:, :, HD * j : HD * (j + 1)].reshape(SEQ, HD).astype(BF)
+            gwo_f[HD * j : HD * (j + 1)] = dot(left, ga_all[...].reshape(SEQ, D), TN)
+        for i in range(NS):
+            gwo[i % 2, i // 2] = gwo_f[16 * i : 16 * (i + 1)].astype(BF)
+        yield from reduce_shard(
+            net, chips, core, sibling, [(gwo, lanes(D), h2, b2, l2, t2)], got_out
+        )
+        yield from move(net, [(so, ao.at[comes[1]])], comes, stays)
+        yield from gather(net, ctx, [(None, at(ao), lanes(D))])
+
+    def head_grads(i):
+        g = dot(ga_all[i], wo_all[...].reshape(QW, D), NT, BF)
+        gatt[i] = g
+        both = g.astype(F32) * heads[i]
+        for h in range(2):
+            delta[h, pl.ds(pl.multiple_of(i * T, T), T)] = jnp.sum(
+                both[:, HD * h : HD * (h + 1)], -1, keepdims=True
+            )
+
+    def attend_back(h, n, fresh):
+        width = 256 * (n + 1)
+        here = slice(2 * n, 2 * n + 2)
+        mine = slice(HD * h, HD * (h + 1))
+        q = qkv[here, :, mine].reshape(256, HD)
+        k = qkv[0 : 2 * n + 2, :, 2 * HD : 3 * HD].reshape(width, HD)
+        v = qkv[0 : 2 * n + 2, :, 3 * HD :].reshape(width, HD)
+        g = gatt[here, :, mine].reshape(256, HD)
+        span = slice(256 * n, 256 * (n + 1))
+        score = dot(q, k, NT) * HD**-0.5
+        row = lax.broadcasted_iota(jnp.int32, (256, width), 0) + 256 * n
+        col = lax.broadcasted_iota(jnp.int32, (256, width), 1)
+        p = jnp.where(col <= row, jnp.exp(score - lse[h, span]), 0.0)
+        gv = dot(p.astype(BF), g, TN)
+        gs = (p * (dot(g, v, NT) - delta[h, span])).astype(BF)
+        gk = dot(gs, q, TN)
+        if fresh:
+            gv_f[0:width] = gv
+            gk_f[0:width] = gk
+        else:
+            gv_f[0:width] += gv
+            gk_f[0:width] += gk
+        gq = dot(gs, k, NN) * HD**-0.5
+        turn_back(gq, here, mine, 0, fresh)
+
+    def turn_back(g, here, mine, kind, fresh):
+        n = g.shape[0]
+        cosine = tab[here, :, 0:HD].reshape(n, HD)
+        sine = tab[here, :, HD:].reshape(n, HD)
+        w = g * cosine - pltpu.roll(g, 64, 1) * sine
+        u, inverse = rms_parts(raw[here, :, mine].reshape(n, HD))
+        gain = jnp.sum(w * u, 0, keepdims=True)
+        place = slice(2 * D + HD * kind, 2 * D + HD * (kind + 1))
+        if fresh:
+            sm[:, place] = gain
+        else:
+            sm[:, place] += gain
+        r = rms_back(w * ghead[kind : kind + 1], u, inverse).astype(BF)
+        gqkv[here, :, mine] = r.reshape(n // T, T, HD)
+
+    def work():
+        yield
+        pl.loop(0, NC)(head_grads)
+        loads[1].wait()
+        loads[2].wait()
+        loads[4].wait()
+        loads[5].wait()
+        yield
+        for n in (3, 2, 1, 0):
+            for h in range(2):
+                attend_back(h, n, n == 3 and h == 0)
+            if n:
+                yield
+        for m in range(2):
+            here = slice(4 * m, 4 * m + 4)
+            span = slice(512 * m, 512 * (m + 1))
+            turn_back(gk_f[span] * HD**-0.5, here, slice(2 * HD, 3 * HD), 1, m == 0)
+            gqkv[here, :, 3 * HD :] = gv_f[span].astype(BF).reshape(4, T, HD)
+        loads[6].wait()
+        loads[7].wait()
+
+        @pl.loop(0, NC)
+        def _(i):
+            part[i] = dot(gqkv[i], w1_all[:, :, 0:512].reshape(D, 512), NT, BF)
+
+    loads[0].wait()
+    background = out_grad()
+    drive(feed_forward(0, lb0, sb0), feed_forward(1, lb1, sb1), background, feed_forward_grads(), work())
 
     def got_input(h):
         def got(k, total):
@@ -587,7 +691,7 @@
                 sm[:, 0:D] = g
             else:
                 sm[:, 0:D] += g
-            gx_ref[rows(h)] = gres_ref[rows(h)] + rms_back(total * gain[...], normed, inverse)
+            gx_ref[rows(h)] = gres_ref[rows(h)] + rms_back(total * gvec[0:1], normed, inverse)
 
         return got
 
@@ -600,7 +704,6 @@
         yield
         yield
         sm[:, D : 2 * D] = ggain[...]
-        sm[:, 2 * D :] = gqk[...]
         smc[c] = sm[...]
         sent = [net.send(sm, smc.at[c], d) for d in ctx_peers]
         yield
@@ -620,47 +723,38 @@
             total = total + sms[i]
         small_ref[...] = total
 
-    def mlp():
-        yield
-        yield
-        yield from move(net, [(gwd_sum, own_d)], comes, stays)
-        yield from gather(net, ctx, [(gw2_sum, at(a2), lanes(WCOL2)), (own_d, at(ad), lanes(D))])
-        for i in range(NC):
-            gate_out[:, FW * i : FW * (i + 1)] = a2[i, :, 0:FW].astype(F32)
-            up_out[:, FW * i : FW * (i + 1)] = a2[i, :, FW : 2 * FW].astype(F32)
-            down_out[24 * i : 24 * (i + 1), :] = ad[i].astype(F32)
-
     def got_shard(k, total):
-        (s1, so)[k][...] = total.astype(BF)
-
-    def attn():
+        s1[...] = total.astype(BF)
+
+    def grads():
+        @pl.loop(0, 8)
+        def _(j):
+            left = hid[:, :, pl.ds(pl.multiple_of(j * 128, 128), 128)].reshape(SEQ, 128)
+            g = dot(left, gqkv[...].reshape(SEQ, 512), TN, BF)
+            gw1[0, j] = g[0:64]
+            gw1[1, j] = g[64:128]
+
         yield from reduce_shard(
-            net, chips, core, sibling,
-            [(gw1, lanes(512), h1, b1, l1, t1), (gwo, lanes(D), h2, b2, l2, t2)], got_shard,
+            net, chips, core, sibling, [(gw1, lanes(512), h1, b1, l1, t1)], got_shard
         )
-        yield from move(net, [(so, ao.at[comes[1]])], comes, stays)
-        yield from gather(net, ctx, [(s1, at(a1), lanes(512)), (None, at(ao), lanes(D))])
-        for i in range(NC):
-            q_out[:, QW * i : QW * (i + 1)] = a1[i, :, 0:QW].astype(F32)
-            k_out[:, HD * i : HD * (i + 1)] = a1[i, :, QW : QW + HD].astype(F32)
-            v_out[:, HD * i : HD * (i + 1)] = a1[i, :, QW + HD :].astype(F32)
-            o_out[16 * i : 16 * (i + 1), :] = ao[i].astype(F32)
-
-    drive(by_ctx(0, la0, sa0), by_ctx(1, la1, sa1), small(), attn(), mlp())
-
-
-def rotate(values, cosine, sine):
-    turned = jnp.concatenate([-values[..., HD // 2 :], values[..., : HD // 2]], -1)
-    return values * cosine + turned * sine
-
-
-def rotate_reverse(grads, cosine, sine):
-    t = grads * sine
-    return grads * cosine + jnp.concatenate([t[..., HD // 2 :], -t[..., : HD // 2]], -1)
-
-
-def by_owner(g, rows):
-    return jnp.transpose(g.reshape(8, 2, rows, g.shape[1]), (1, 0, 2, 3))
+        yield from gather(net, ctx, [(s1, at(a1), lanes(512))])
+
+    drive(by_ctx(0, la0, sa0), by_ctx(1, la1, sa1), grads(), small())
+
+
+def assemble_body(
+    out, gx, a1, ao, a2, ad, out_ref, gx_ref, q_out, k_out, v_out, o_out, gate_out, up_out, down_out
+):
+    out_ref[...] = out[...]
+    gx_ref[...] = gx[...]
+    for i in range(NC):
+        q_out[:, QW * i : QW * (i + 1)] = a1[i, :, 0:QW].astype(F32)
+        k_out[:, HD * i : HD * (i + 1)] = a1[i, :, QW : QW + HD].astype(F32)
+        v_out[:, HD * i : HD * (i + 1)] = a1[i, :, QW + HD :].astype(F32)
+        o_out[16 * i : 16 * (i + 1), :] = ao[i].astype(F32)
+        gate_out[:, FW * i : FW * (i + 1)] = a2[i, :, 0:FW].astype(F32)
+        up_out[:, FW * i : FW * (i + 1)] = a2[i, :, FW : 2 * FW].astype(F32)
+        down_out[24 * i : 24 * (i + 1), :] = ad[i].astype(F32)
 
 
 def shards(
@@ -702,88 +796,64 @@
         "hhhhhhhv", (tok, cot, positions, w1, wo, w2, wd, freq),
         [pltpu.VMEM((NC, T, D), BF), pltpu.VMEM((NC, 1, T), jnp.int32)], 128, 8, 0, 56 << 20,
     )
-    gain_attn, gain_mlp = gvec[0:1], gvec[1:2]
-    wqkv = w1_all[:, :, 0:512].reshape(D, 512)
-    wout = wo_all.reshape(QW, D)
-    cosine, sine = tab.reshape(SEQ, 2 * HD)[:, :HD], tab.reshape(SEQ, 2 * HD)[:, HD:]
-    sine = jnp.concatenate([-sine[:, :half], sine[:, half:]], 1)
-    cosine_q, sine_q = cosine[:, None, :], sine[:, None, :]
-    gain_q, gain_k = ghead[0], ghead[1]
-    hidden_one = hid.reshape(SEQ, D)
-    raw = raw.reshape(SEQ, 512)
-    q_normed, q_inverse = rms_parts(raw[:, :QW].reshape(SEQ, 2, HD))
-    k_normed, k_inverse = rms_parts(raw[:, QW : QW + HD])
-    qkv = qkv.reshape(SEQ, 512)
-    queries, keys, value = qkv[:, :QW].reshape(SEQ, 2, HD), qkv[:, QW : QW + HD], qkv[:, QW + HD :]
-    scale = HD**-0.5
-    order = jnp.arange(SEQ)
-    allowed = order[None, :] <= order[:, None]
-    log_total = lse
-    attended = heads.reshape(SEQ, QW).astype(BF)
-    heads = jnp.transpose(heads.reshape(SEQ, 2, HD), (1, 0, 2))
-
-    output, ga_all, grad_resid, ggain_mlp, gw2_sum, gwd_sum = remote_call(
+    ga_all, grad_resid, ggain_mlp, gw2_sum, gwd_sum, down_part, resid = remote_call(
         mid_body,
         [
-            ((T, D), BF, "v"), ((NC, T, D), BF, "h"), ((T, D), F32, "v"), ((1, D), F32, "v"),
-            ((64, WCOL2), BF, "v"), ((24, D), BF, "v"),
+            ((NC, T, D), BF, "h"), ((T, D), F32, "v"), ((1, D), F32, "v"),
+            ((64, WCOL2), BF, "v"), ((24, D), BF, "v"), ((NC, T, D), BF, "v"), ((T, D), F32, "v"),
         ],
         "v" * 7,
-        (out_part, tok, cot, gain_mlp, w2_all.reshape(D, 2 * FW), wd_all.reshape(FW, D), g_all),
+        (out_part, tok, cot, gvec[1:2], w2_all.reshape(D, 2 * FW), wd_all.reshape(FW, D), g_all),
         [
             pltpu.VMEM((NC, T, D), BF), pltpu.VMEM((NC, T, FW), BF), pltpu.VMEM((NC, T, 2 * FW), BF),
-            pltpu.VMEM((NC, T, D), BF), pltpu.VMEM((NC, T, D), BF), pltpu.VMEM((T, D), F32),
+            pltpu.VMEM((NC, T, D), BF),
             pltpu.VMEM((T, D), BF), pltpu.VMEM((2, 8, 64, WCOL2), BF), pltpu.VMEM((2, 8, 24, D), BF),
             pltpu.VMEM((FW, D), F32),
         ]
-        + chunk_scratch() * 3 + shard_scratch((64, WCOL2)) + shard_scratch((24, D)),
+        + chunk_scratch() * 2 + shard_scratch((64, WCOL2)) + shard_scratch((24, D)),
         128, 8, 1, 58 << 20,
     )
-    ga = ga_all.reshape(SEQ, D)
-    gwo = by_owner(dot(attended, ga, TN, BF), 16)
-    grad_att = dot(ga, wout, NT, BF).reshape(SEQ, 2, HD)
-    delta = jnp.einsum("thd,htd->ht", grad_att.astype(F32), heads)
-    scores = jnp.einsum("thd,nd->htn", queries, keys, preferred_element_type=F32) * scale
-    probs = jnp.where(allowed, jnp.exp(scores - log_total), 0.0)
-    probs_bf = probs.astype(BF)
-    grad_value = jnp.einsum("htn,thd->nd", probs_bf, grad_att, preferred_element_type=F32)
-    grad_probs = jnp.einsum("thd,nd->htn", grad_att, value, preferred_element_type=F32)
-    grad_scores = (probs * (grad_probs - delta[..., None])).astype(BF)
-    grad_q = jnp.einsum("htn,nd->thd", grad_scores, keys, preferred_element_type=F32) * scale
-    grad_k = jnp.einsum("htn,thd->nd", grad_scores, queries, preferred_element_type=F32) * scale
-    wq = rotate_reverse(grad_q, cosine_q, sine_q)
-    wk = rotate_reverse(grad_k, cosine, sine)
-    gq_gain = jnp.sum(wq * q_normed, (0, 1))
-    gk_gain = jnp.sum(wk * k_normed, 0)
-    gq = rms_back(wq * gain_q, q_normed, q_inverse).reshape(SEQ, QW).astype(BF)
-    gk = rms_back(wk * gain_k, k_normed, k_inverse).astype(BF)
-    gqkv = jnp.concatenate([gq, gk, grad_value.astype(BF)], 1)
-    gw1 = by_owner(dot(hidden_one, gqkv, TN, BF), 64)
-    in_part = dot(gqkv, wqkv, NT, BF).reshape(NC, T, D)
-    gqk = jnp.concatenate([gq_gain, gk_gain])[None]
-
-    outs = remote_call(
+    output, gx, small, a1, ao, a2, ad = remote_call(
         end_body,
         [
-            ((T, D), F32, "v"), ((1, SMALL), F32, "v"),
-            ((64, 2048), F32, "v"), ((64, 1024), F32, "v"), ((64, 1024), F32, "v"),
-            ((128, D), F32, "v"), ((64, 3072), F32, "v"), ((64, 3072), F32, "v"),
-            ((192, D), F32, "v"),
+            ((T, D), BF, "v"), ((T, D), F32, "v"), ((1, SMALL), F32, "v"),
+            ((NC, 64, 512), BF, "v"), ((NC, 16, D), BF, "v"),
+            ((NC, 64, WCOL2), BF, "v"), ((NC, 24, D), BF, "v"),
         ],
-        "v" * 10,
-        (in_part, tok, grad_resid, gain_attn, ggain_mlp, gqk, gw1, gwo, gw2_sum, gwd_sum),
-        chunk_scratch() + shard_scratch((64, 512)) + shard_scratch((16, D))
+        "v" * 10 + "h" * 8,
+        (
+            ga_all, tok, grad_resid, resid, gvec, ghead, ggain_mlp, wo_all, gw2_sum, gwd_sum,
+            down_part, qkv, lse, heads, raw, tab, hid, w1_all,
+        ),
+        [
+            pltpu.VMEM((NC, T, D), BF), pltpu.VMEM((NC, T, 512), BF), pltpu.VMEM((2, SEQ, 1), F32),
+            pltpu.VMEM((NC, T, QW), F32), pltpu.VMEM((NC, T, 512), F32),
+            pltpu.VMEM((NC, T, 2 * HD), F32), pltpu.VMEM((NC, T, D), BF),
+            pltpu.VMEM((NS, 64, WCOL1), BF),
+            pltpu.VMEM((NC, T, QW), BF), pltpu.VMEM((2, SEQ, 1), F32), pltpu.VMEM((QW, D), F32),
+            pltpu.VMEM((SEQ, HD), F32), pltpu.VMEM((SEQ, HD), F32), pltpu.VMEM((NC, T, 512), BF),
+            pltpu.VMEM((NC, T, D), BF), pltpu.VMEM((2, 8, 64, 512), BF),
+            pltpu.VMEM((2, 8, 16, D), BF),
+        ]
+        + chunk_scratch() * 2 + shard_scratch((64, 512)) + shard_scratch((16, D))
         + [
-            pltpu.VMEM((64, 512), BF), pltpu.VMEM((16, D), BF),
-            pltpu.VMEM((NC, 64, 512), BF), pltpu.VMEM((NC, 16, D), BF),
-            pltpu.VMEM((NC, 64, WCOL2), BF), pltpu.VMEM((NC, 24, D), BF),
-            pltpu.VMEM((24, D), BF),
+            pltpu.VMEM((64, 512), BF), pltpu.VMEM((16, D), BF), pltpu.VMEM((24, D), BF),
             pltpu.VMEM((1, SMALL), F32), pltpu.VMEM((NC, 1, SMALL), F32),
             pltpu.VMEM((1, SMALL), F32), pltpu.VMEM((NS, 1, SMALL), F32),
         ],
-        128, 8, 2, 56 << 20,
+        160, 16, 2, 58 << 20,
     )
-    gx, small, gwq, gwk, gwv, gwo_out, gwg, gwu, gwd_out = outs
+    output, gx, gwq, gwk, gwv, gwo_out, gwg, gwu, gwd_out = pl.pallas_call(
+        assemble_body,
+        out_shape=[
+            jax.ShapeDtypeStruct((T, D), BF), jax.ShapeDtypeStruct((T, D), F32),
+            jax.ShapeDtypeStruct((64, 2048), F32), jax.ShapeDtypeStruct((64, 1024), F32),
+            jax.ShapeDtypeStruct((64, 1024), F32), jax.ShapeDtypeStruct((128, D), F32),
+            jax.ShapeDtypeStruct((64, 3072), F32), jax.ShapeDtypeStruct((64, 3072), F32),
+            jax.ShapeDtypeStruct((192, D), F32),
+        ],
+        compiler_params=pltpu.CompilerParams(vmem_limit_bytes=40 << 20),
+    )(output, gx, a1, ao, a2, ad)
     small = small[0]
 
     def own(offset, width):

time: 296 us -> 267 us (0.902)
  Pallas kernels: 220 us -> 251 us
  local copies, waits for them, and re-layouts: 43.3 us -> 12.5 us
  matrix products: 18.2 us -> 0 us
  other arithmetic: 11 us -> 2.17 us
    pallas_call x3, Pallas kernels: 220 us -> 249 us  [remote_call(): pl.pallas_call(body, out_shape=[jax.ShapeDtypeStruct(s, d) for s, d, _ in...]
    dot_general x9 -> x0, matrix products: 18.2 us -> none  [the longest x4 7.97 us: dot(): lax.dot_general(a, b, (dims, ((), ())), preferred_element_type=F32)]
    unnamed x44 -> x14, local copies, waits for them, and re-layouts: 20.5 us -> 6.29 us
    slice x9 -> x1, local copies, waits for them, and re-layouts: 13.5 us -> 1.3 us  [shards(): gvec[1:2]]
    unnamed x1 -> x0, other arithmetic: 3.2 us -> none
where the time goes in v4:
time: 267 us
  Pallas kernels  251 us (94%)
  local copies, waits for them, and re-layouts  12.5 us (5%)
    pallas_call x3, Pallas kernels, remote_call(): pl.pallas_call(body, out_shape=[jax.ShapeDtypeStruct(s, d) for s, d, _ in...  249 us
    unnamed x14, local copies, waits for them, and re-layouts  6.29 us

profile of v4, /device:TPU:1, one launch (start us, length us, event | category | flops | bytes accessed | tf_op | source)
XLA Modules:
  0.0 266.6 jit_solution(14155172261051821763)
XLA Ops:
  0.6 0.0 copy-start
  0.7 0.8 constant_dynamic-slice_fusion.6
  1.4 0.2 copy-done
  1.6 0.8 maximum_bitcast_fusion
  2.4 0.7 maximum_maximum_fusion.w1
  3.1 0.8 constant_dynamic-slice_fusion.4
  3.9 0.7 pad_maximum_fusion.w2
  4.6 0.1 pad_maximum_fusion.1
  4.7 0.7 broadcast_in_dim.28.freq
  5.4 73.7 %shard_map.237 = (bf16[8,128,1024]{2,1,0:T(8,128)(2,1)}, bf16[16,64,640]{2,1,0:T(8,128)(2,1)}, bf16[16,16,1024]{2,1,0:T(8,128)(2,1)}, bf16[16,64,768]{2,1,0:T(8,...) custom-call(bf16[128,1024]{1,0:T(8,128)(2,1)} %bitcast.20, ...), custom_call_target="tpu_custom_call" | custom-call | tf_op jit(solution)/shard_map/pallas_call | solution.py:329
  79.1 1.3 slice.3.gain
  80.4 80.5 %shard_map.238 = (bf16[8,128,1024]{2,1,0:T(8,128)(2,1)}, f32[128,1024]{1,0:T(8,128)}, f32[1,1024]{1,0:T(1,128)}, bf16[64,768]{1,0:T(8,128)(2,1)}, bf16[24,1024]{...) custom-call(bf16[8,128,1024]{2,1,0:T(8,128)(2,1)} %get-tuple-element.50.part, ...), custom_call_target="tpu_custom_call" | custom-call | tf_op jit(solution)/shard_map/pallas_call | solution.py:329
  160.9 94.8 %shard_map.239 = (bf16[128,1024]{1,0:T(8,128)(2,1)}, f32[128,1024]{1,0:T(8,128)}, f32[1,2304]{1,0:T(1,128)}, bf16[8,64,512]{2,1,0:T(8,128)(2,1)}, bf16[8,16,1024...) custom-call(bf16[8,128,1024]{2,1,0:T(8,128)(2,1)} %get-tuple-element.55.ga_all, ...), custom_call_target="tpu_custom_call" | custom-call | tf_op jit(solution)/shard_map/pallas_call | solution.py:329
  255.7 0.0 copy-start.1
  255.7 1.1 copy-done.1
  256.8 0.0 copy-start.2
  256.8 1.0 copy-done.2
  257.9 0.0 copy-start.3
  257.9 1.0 copy-done.3
  258.9 0.0 copy-start.4
  258.9 1.0 copy-done.4
  259.9 0.0 copy-start.5
  259.9 0.9 copy-done.5
  260.8 0.0 copy-start.6
  260.8 0.9 copy-done.6
  261.8 2.3 shard_map.240
  264.1 1.3 fusion.2
  265.4 1.3 fusion.3
  (4 shorter events, 0.0 us)
Async XLA Ops:
  0.6 1.0 copy-start
  255.7 1.1 copy-start.1
  256.8 1.0 copy-start.2
  257.9 1.0 copy-start.3
  258.9 1.0 copy-start.4
  259.9 0.9 copy-start.5
  260.8 0.9 copy-start.6

commit v5 on v4

--- a/solution.py
+++ b/solution.py
@@ -1,5 +1,6 @@
 import jax
 import jax.numpy as jnp
+import numpy as np
 from jax import lax
 from jax.experimental import pallas as pl
 from jax.experimental.pallas import tpu as pltpu
@@ -26,10 +27,8 @@
 
 
 def lanes(width):
-    n = width // 128
-    a = (n + 2) // 3 * 128
-    b = a + (n + 1) // 3 * 128
-    return ((ALL, slice(0, a)), (ALL, slice(a, b)), (ALL, slice(b, width)))
+    a = (width // 128 + 1) // 2 * 128
+    return ((ALL, slice(0, a)), (ALL, slice(a, width)), None)
 
 
 def view(ref, part):
@@ -112,14 +111,21 @@
         pl.semaphore_wait(barrier, len(devices))
 
 
-def drive(*threads):
+def drive(*threads, until=None):
     threads = list(threads)
+    ended = set()
     while threads:
-        for t in list(threads):
+        for x in list(threads):
+            if id(x) in ended:
+                continue
             try:
-                next(t)
+                next(x)
             except StopIteration:
-                threads.remove(t)
+                ended.add(id(x))
+        threads = [x for x in threads if id(x) not in ended]
+        if until is not None and id(until) in ended:
+            break
+    return threads
 
 
 def move(net, items, to, stays):
@@ -221,6 +227,8 @@
     first, second, third = [], [], []
     for p, parts, land, _ in items:
         for n, part in zip((left, right, pair), parts):
+            if part is None:
+                continue
             first.append(net.send(view(p(oz), part), view(land.at[0], part), n))
     yield
     for c in first:
@@ -229,6 +237,9 @@
         for k, (i, part, n) in enumerate(
             ((o, parts[2], left), (bz, parts[1], right), (az, parts[0], pair))
         ):
+            if part is None:
+                second.append(net.send(p(i), land.at[1 + k], n))
+                continue
             sums[k] = p(i)[...]
             sums[(k,) + part] = plus(p(i)[part], land[(0,) + part])
             second.append(net.send(sums.at[k], land.at[1 + k], n))
@@ -260,7 +271,7 @@
 
 CHUNKS = 2
 CROWS = T // CHUNKS
-CPARTS = ((slice(0, 32), ALL), (slice(32, 48), ALL), (slice(48, 64), ALL))
+CPARTS = ((slice(0, 32), ALL), (slice(32, 64), ALL), None)
 
 
 def rows(h):
@@ -343,21 +354,36 @@
 
 
 def start_body(
-    tok, cot, pos, w1, wo, w2, wd, freq,
-    g_all, w1_all, wo_all, w2_all, wd_all, hid, raw, qkv, tab, lse, heads, part, gvec, ghead,
-    x_all, p_all, ss, rs, ls,
+    tok, cot, pos, wq, wk, wv, wg, wu, gblock, wo, wd, freq,
+    g_all, w1_all, wo_all, w2_all, wd_all, hid_h, raw_h, qkv_h, tab_h, lse, heads_h, part, gvec, ghead,
+    x_all, p_all, w1, w2, hid, raw, qkv, tab, heads, ss, rs, ls,
 ):
     s, c, core, ctx, chips, sibling, goes, comes, stays = places()
     net = Net(ss, rs, ls)
+
+    def cut(w, width):
+        return w.at[:, pl.ds(pl.multiple_of(c * width, 128), width)]
+
+    loads = [
+        net.copy(x, y)
+        for x, y in (
+            (cut(wq, QW), w1.at[:, 0:QW]), (cut(wk, HD), w1.at[:, QW : QW + HD]),
+            (cut(wv, HD), w1.at[:, QW + HD : 512]), (gblock, w1.at[:, 512:WCOL1]),
+            (cut(wg, FW), w2.at[:, 0:FW]), (cut(wu, FW), w2.at[:, FW : 2 * FW]),
+        )
+    ]
     greet(ring_devices(ctx) + ring_devices(chips) + [sibling], (goes, comes, stays))
+    for x in loads:
+        x.wait()
 
     def by_shard():
+        yield from gather(
+            net, chips, [(w1, at(w1_all), lanes(WCOL1))], lambda i: i * 2 + core, sibling
+        )
+
+    def moved():
         moved = [(wo.at[c], wo_all.at[goes[0]]), (wd.at[c], wd_all.at[goes[0]])]
         yield from move(net, moved, goes, stays)
-        yield from gather(
-            net, chips, [(w1, at(w1_all), lanes(WCOL1)), (None, at(wo_all), lanes(D))],
-            lambda i: i * 2 + core, sibling,
-        )
 
     def first(h):
         items = [(tok.at[rows(h)], chunk(x_all, h), CPARTS)]
@@ -365,14 +391,19 @@
             items.append((pos, at(p_all), ((ALL, ALL), None, None)))
         yield from gather(net, ctx, items)
 
-    drive(first(0), first(1), by_shard())
+    weights = by_shard()
+    drive(first(0), weights, first(1), weights, moved())
 
     def second(h):
         yield from gather(net, ctx, [(cot.at[rows(h)], chunk(g_all, h), CPARTS)])
 
     def by_shard_second():
         yield from gather(
-            net, chips, [(w2, at(w2_all), lanes(WCOL2)), (None, at(wd_all), lanes(D))],
+            net, chips,
+            [
+                (w2, at(w2_all), lanes(WCOL2)), (None, at(wd_all), lanes(D)),
+                (None, at(wo_all), lanes(D)),
+            ],
             lambda i: i * 2 + core, sibling,
         )
 
@@ -432,6 +463,8 @@
         pl.loop(0, 4)(project)
         yield
         pl.loop(4, 8)(project)
+        for x, y in ((hid, hid_h), (raw, raw_h), (qkv, qkv_h), (tab, tab_h)):
+            stores.append(net.copy(x, y))
         for h in range(2):
             attend(h, 0)
         yield
@@ -440,24 +473,29 @@
                 attend(h, n)
             if n < 3:
                 yield
+        stores.append(net.copy(heads, heads_h))
 
         @pl.loop(0, NC)
         def _(i):
             part[i] = dot(heads[i].astype(BF), wo_all[...].reshape(QW, D), NN, BF)
 
+    stores = []
     drive(second(0), second(1), by_shard_second(), work())
+    for x in stores:
+        x.wait()
 
 
 def mid_body(
-    part, tok, cot, gain, wgu, wd, g_all,
-    ga_all, gres_ref, ggain_ref, gw2_sum, gwd_sum, down_part, resid,
-    h_all, mixed, ggu, back_part, ga, gw2, gwd, gwd_f,
-    la0, sa0, la1, sa1, lb0, sb0, lb1, sb1,
-    h1, b1, l1, t1, h2, b2, l2, t2, ss, rs, ls,
+    part, tok, cot, gain, wgu_h, wd_h, g_h,
+    ga_all, gres_ref, ggain_ref, gw2_h, gwd_h, down_h, resid,
+    wgu, wd, g_all, down_part, gw2, gwd, h_all, mixed, ggu, back_part, ga, gwd_f,
+    la0, sa0, la1, sa1, lb0, sb0, lb1, sb1, ss, rs, ls,
 ):
     s, c, core, ctx, chips, sibling, goes, comes, stays = places()
     net = Net(ss, rs, ls)
-    greet(ring_devices(ctx) + ring_devices(chips) + [sibling])
+    loads = [net.copy(x, y) for x, y in ((wgu_h, wgu), (wd_h, wd), (g_h, g_all))]
+    stores = []
+    greet(ring_devices(ctx))
 
     def forward(h, land, sums):
         def got(k, total):
@@ -498,6 +536,8 @@
         yield
         yield
         yield
+        for x in loads:
+            x.wait()
         blocks([c])
         yield
         blocks([ctx.idx(-1, 0), ctx.idx(1, 0), ctx.idx(0, 1)])
@@ -507,6 +547,7 @@
         blocks([ctx.idx(2, 1)])
 
     drive(forward(0, la0, sa0), forward(1, la1, sa1), work())
+    stores.append(net.copy(down_part, down_h))
 
     def got_back(h):
         def got(k, total):
@@ -526,9 +567,6 @@
         yield from reduce(net, ctx, [(chunk(back_part, h), CPARTS, land, sums)], got_back(h))
         yield from gather(net, ctx, [(ga.at[rows(h)], chunk(ga_all, h), CPARTS)])
 
-    def got_shard(k, total):
-        (gw2_sum, gwd_sum)[k][...] = total.astype(BF)
-
     def grads():
         for q in range(2):
 
@@ -545,25 +583,23 @@
             gwd_f[128 * j : 128 * (j + 1)] = dot(left, g_all[...].reshape(SEQ, D), TN)
         for i in range(NS):
             gwd[i % 2, i // 2] = gwd_f[24 * i : 24 * (i + 1)].astype(BF)
-        yield
-        yield from reduce_shard(
-            net, chips, core, sibling,
-            [(gw2, lanes(WCOL2), h1, b1, l1, t1), (gwd, lanes(D), h2, b2, l2, t2)], got_shard,
-        )
-
-    drive(
-        backward(0, lb0, sb0), backward(1, lb1, sb1), grads(),
-    )
+        stores.append(net.copy(gw2, gw2_h))
+        stores.append(net.copy(gwd, gwd_h))
+
+    drive(backward(0, lb0, sb0), backward(1, lb1, sb1), grads())
+    for x in stores:
+        x.wait()
 
 
 def end_body(
-    ga_all, tok, gres_ref, resid, gvec, ghead, ggain, wo_all, gw2_sum, gwd_sum,
-    down_h, qkv_h, lse_h, heads_h, raw_h, tab_h, hid_h, w1_h,
+    ga_all, tok, gres_ref, resid, gvec, ghead, ggain, wo_all,
+    gw2_h, gwd_h, down_h, qkv_h, lse_h, heads_h, raw_h, tab_h, hid_h, w1_h,
     out_ref, gx_ref, small_ref, a1, ao, a2, ad,
-    down_part, qkv, lse, heads, raw, tab, hid, w1_all,
+    down_part, qkv, lse, heads, raw, tab, hid, w1_all, gw2, gwd,
     gatt, delta, gwo_f, gk_f, gv_f, gqkv, part, gw1, gwo,
     la0, sa0, la1, sa1, lb0, sb0, lb1, sb1, h1, b1, l1, t1, h2, b2, l2, t2,
-    s1, so, own_d, sm, smc, sm2, sms, ss, rs, ls,
+    h3, b3, l3, t3, h4, b4, l4, t4,
+    s1, so, gw2_sum, gwd_sum, own_d, sm, smc, sm2, sms, ss, rs, ls,
 ):
     s, c, core, ctx, chips, sibling, goes, comes, stays = places()
     net = Net(ss, rs, ls)
@@ -571,7 +607,7 @@
         net.copy(x, y)
         for x, y in (
             (heads_h, heads), (qkv_h, qkv), (lse_h, lse), (down_h, down_part),
-            (raw_h, raw), (tab_h, tab), (hid_h, hid), (w1_h, w1_all),
+            (raw_h, raw), (tab_h, tab), (hid_h, hid), (w1_h, w1_all), (gw2_h, gw2), (gwd_h, gwd),
         )
     ]
     ctx_peers = [(s, lax.rem(c + d, NC)) for d in range(1, NC)]
@@ -586,7 +622,16 @@
             loads[3].wait()
         yield from reduce(net, ctx, [(chunk(down_part, h), CPARTS, land, sums)], got)
 
+    def got_ff(k, total):
+        (gw2_sum, gwd_sum)[k][...] = total.astype(BF)
+
     def feed_forward_grads():
+        loads[8].wait()
+        loads[9].wait()
+        yield from reduce_shard(
+            net, chips, core, sibling,
+            [(gw2, lanes(WCOL2), h3, b3, l3, t3), (gwd, lanes(D), h4, b4, l4, t4)], got_ff,
+        )
         yield from move(net, [(gwd_sum, own_d)], comes, stays)
         yield from gather(net, ctx, [(gw2_sum, at(a2), lanes(WCOL2)), (own_d, at(ad), lanes(D))])
 
@@ -655,7 +700,6 @@
         gqkv[here, :, mine] = r.reshape(n // T, T, HD)
 
     def work():
-        yield
         pl.loop(0, NC)(head_grads)
         loads[1].wait()
         loads[2].wait()
@@ -680,8 +724,11 @@
             part[i] = dot(gqkv[i], w1_all[:, :, 0:512].reshape(D, 512), NT, BF)
 
     loads[0].wait()
-    background = out_grad()
-    drive(feed_forward(0, lb0, sb0), feed_forward(1, lb1, sb1), background, feed_forward_grads(), work())
+    main = work()
+    rest = drive(
+        feed_forward(0, lb0, sb0), feed_forward(1, lb1, sb1), out_grad(), feed_forward_grads(), main,
+        until=main,
+    )
 
     def got_input(h):
         def got(k, total):
@@ -739,21 +786,30 @@
         )
         yield from gather(net, ctx, [(s1, at(a1), lanes(512))])
 
-    drive(by_ctx(0, la0, sa0), by_ctx(1, la1, sa1), grads(), small())
+    last = grads()
+    drive(by_ctx(0, la0, sa0), last, by_ctx(1, la1, sa1), last, *rest, small())
 
 
 def assemble_body(
-    out, gx, a1, ao, a2, ad, out_ref, gx_ref, q_out, k_out, v_out, o_out, gate_out, up_out, down_out
+    out_h, gx_h, a1_h, ao_h, a2_h, ad_h,
+    out_ref, gx_ref, q_out, k_out, v_out, o_out, gate_out, up_out, down_out,
+    a1, ao, a2, ad, sem,
 ):
-    out_ref[...] = out[...]
-    gx_ref[...] = gx[...]
+    pairs = ((a2_h, a2), (a1_h, a1), (ao_h, ao), (ad_h, ad), (out_h, out_ref), (gx_h, gx_ref))
+    loads = [pltpu.make_async_copy(x, y, sem.at[k]) for k, (x, y) in enumerate(pairs)]
+    for x in loads:
+        x.start()
+    loads[0].wait()
+    for i in range(NC):
+        gate_out[:, FW * i : FW * (i + 1)] = a2[i, :, 0:FW].astype(F32)
+        up_out[:, FW * i : FW * (i + 1)] = a2[i, :, FW : 2 * FW].astype(F32)
+    for x in loads[1:]:
+        x.wait()
     for i in range(NC):
         q_out[:, QW * i : QW * (i + 1)] = a1[i, :, 0:QW].astype(F32)
         k_out[:, HD * i : HD * (i + 1)] = a1[i, :, QW : QW + HD].astype(F32)
         v_out[:, HD * i : HD * (i + 1)] = a1[i, :, QW + HD :].astype(F32)
         o_out[16 * i : 16 * (i + 1), :] = ao[i].astype(F32)
-        gate_out[:, FW * i : FW * (i + 1)] = a2[i, :, 0:FW].astype(F32)
-        up_out[:, FW * i : FW * (i + 1)] = a2[i, :, FW : 2 * FW].astype(F32)
         down_out[24 * i : 24 * (i + 1), :] = ad[i].astype(F32)
 
 
@@ -765,22 +821,14 @@
     s = lax.axis_index("shard")
     tok, cot = tokens[0], cotangent[0]
 
-    def cut(w, width):
-        return lax.dynamic_slice(w, (0, c * width), (w.shape[0], width))
-
     row0 = jnp.concatenate([attn_gain, mlp_gain])[None]
     row1 = jnp.concatenate([query_gain, key_gain, jnp.zeros((112,), BF)])[None]
     gains = jnp.concatenate([row0, row1, jnp.zeros((62, 128), BF)], 0)
-    w1 = jnp.concatenate(
-        [cut(query_weight, QW), cut(key_matrix, HD), cut(value_matrix, HD), gains], 1
-    )
-    w2 = jnp.concatenate([cut(gate_weight, FW), cut(up_weight, FW)], 1)
     wo = out_weight.reshape(8, 16, D)
     wd = down_weight.reshape(8, 24, D)
 
-    half = HD // 2
-    freq = jnp.power(ROPE_BASE, -jnp.arange(half, dtype=F32) * (2.0 / HD))
-    freq = jnp.broadcast_to(jnp.concatenate([freq, freq])[:, None], (HD, T))
+    freq = np.power(ROPE_BASE, -np.arange(HD // 2) * (2.0 / HD)).astype(np.float32)
+    freq = np.concatenate([freq, freq])[:, None]
 
     (
         g_all, w1_all, wo_all, w2_all, wd_all, hid, raw, qkv, tab, lse, heads, out_part, gvec, ghead,
@@ -789,29 +837,42 @@
         [
             ((NC, T, D), BF, "h"), ((NS, 64, WCOL1), BF, "v"), ((NS, 16, D), BF, "v"),
             ((NS, 64, WCOL2), BF, "h"), ((NS, 24, D), BF, "h"),
-            ((NC, T, D), BF, "v"), ((NC, T, 512), F32, "v"), ((NC, T, 512), BF, "v"),
-            ((NC, T, 2 * HD), F32, "v"), ((2, SEQ, 1), F32, "v"), ((NC, T, QW), F32, "v"),
+            ((NC, T, D), BF, "h"), ((NC, T, 512), F32, "h"), ((NC, T, 512), BF, "h"),
+            ((NC, T, 2 * HD), F32, "h"), ((2, SEQ, 1), F32, "v"), ((NC, T, QW), F32, "h"),
             ((NC, T, D), BF, "v"), ((2, D), F32, "v"), ((2, HD), F32, "v"),
         ],
-        "hhhhhhhv", (tok, cot, positions, w1, wo, w2, wd, freq),
-        [pltpu.VMEM((NC, T, D), BF), pltpu.VMEM((NC, 1, T), jnp.int32)], 128, 8, 0, 56 << 20,
+        "h" * 11 + "v",
+        (
+            tok, cot, positions, query_weight, key_matrix, value_matrix, gate_weight, up_weight,
+            gains, wo, wd, freq,
+        ),
+        [
+            pltpu.VMEM((NC, T, D), BF), pltpu.VMEM((NC, 1, T), jnp.int32),
+            pltpu.VMEM((64, WCOL1), BF), pltpu.VMEM((64, WCOL2), BF),
+            pltpu.VMEM((NC, T, D), BF), pltpu.VMEM((NC, T, 512), F32),
+            pltpu.VMEM((NC, T, 512), BF), pltpu.VMEM((NC, T, 2 * HD), F32),
+            pltpu.VMEM((NC, T, QW), F32),
+        ],
+        144, 24, 0, 58 << 20,
     )
-    ga_all, grad_resid, ggain_mlp, gw2_sum, gwd_sum, down_part, resid = remote_call(
+    ga_all, grad_resid, ggain_mlp, gw2, gwd, down_part, resid = remote_call(
         mid_body,
         [
             ((NC, T, D), BF, "h"), ((T, D), F32, "v"), ((1, D), F32, "v"),
-            ((64, WCOL2), BF, "v"), ((24, D), BF, "v"), ((NC, T, D), BF, "v"), ((T, D), F32, "v"),
+            ((2, 8, 64, WCOL2), BF, "h"), ((2, 8, 24, D), BF, "h"),
+            ((NC, T, D), BF, "h"), ((T, D), F32, "v"),
         ],
-        "v" * 7,
+        "vvvvhhh",
         (out_part, tok, cot, gvec[1:2], w2_all.reshape(D, 2 * FW), wd_all.reshape(FW, D), g_all),
         [
+            pltpu.VMEM((D, 2 * FW), BF), pltpu.VMEM((FW, D), BF), pltpu.VMEM((NC, T, D), BF),
+            pltpu.VMEM((NC, T, D), BF), pltpu.VMEM((2, 8, 64, WCOL2), BF),
+            pltpu.VMEM((2, 8, 24, D), BF),
             pltpu.VMEM((NC, T, D), BF), pltpu.VMEM((NC, T, FW), BF), pltpu.VMEM((NC, T, 2 * FW), BF),
-            pltpu.VMEM((NC, T, D), BF),
-            pltpu.VMEM((T, D), BF), pltpu.VMEM((2, 8, 64, WCOL2), BF), pltpu.VMEM((2, 8, 24, D), BF),
-            pltpu.VMEM((FW, D), F32),
+            pltpu.VMEM((NC, T, D), BF), pltpu.VMEM((T, D), BF), pltpu.VMEM((FW, D), F32),
         ]
-        + chunk_scratch() * 2 + shard_scratch((64, WCOL2)) + shard_scratch((24, D)),
-        128, 8, 1, 58 << 20,
+        + chunk_scratch() * 2,
+        96, 16, 1, 58 << 20,
     )
     output, gx, small, a1, ao, a2, ad = remote_call(
         end_body,
@@ -820,9 +881,9 @@
             ((NC, 64, 512), BF, "v"), ((NC, 16, D), BF, "v"),
             ((NC, 64, WCOL2), BF, "v"), ((NC, 24, D), BF, "v"),
         ],
-        "v" * 10 + "h" * 8,
+        "v" * 8 + "h" * 10,
         (
-            ga_all, tok, grad_resid, resid, gvec, ghead, ggain_mlp, wo_all, gw2_sum, gwd_sum,
+            ga_all, tok, grad_resid, resid, gvec, ghead, ggain_mlp, wo_all, gw2, gwd,
             down_part, qkv, lse, heads, raw, tab, hid, w1_all,
         ),
         [
@@ -830,19 +891,23 @@
             pltpu.VMEM((NC, T, QW), F32), pltpu.VMEM((NC, T, 512), F32),
             pltpu.VMEM((NC, T, 2 * HD), F32), pltpu.VMEM((NC, T, D), BF),
             pltpu.VMEM((NS, 64, WCOL1), BF),
+            pltpu.VMEM((2, 8, 64, WCOL2), BF), pltpu.VMEM((2, 8, 24, D), BF),
             pltpu.VMEM((NC, T, QW), BF), pltpu.VMEM((2, SEQ, 1), F32), pltpu.VMEM((QW, D), F32),
             pltpu.VMEM((SEQ, HD), F32), pltpu.VMEM((SEQ, HD), F32), pltpu.VMEM((NC, T, 512), BF),
             pltpu.VMEM((NC, T, D), BF), pltpu.VMEM((2, 8, 64, 512), BF),
             pltpu.VMEM((2, 8, 16, D), BF),
         ]
         + chunk_scratch() * 2 + shard_scratch((64, 512)) + shard_scratch((16, D))
+        + shard_scratch((64, WCOL2)) + shard_scratch((24, D))
         + [
-            pltpu.VMEM((64, 512), BF), pltpu.VMEM((16, D), BF), pltpu.VMEM((24, D), BF),
+            pltpu.VMEM((64, 512), BF), pltpu.VMEM((16, D), BF),
+            pltpu.VMEM((64, WCOL2), BF), pltpu.VMEM((24, D), BF), pltpu.VMEM((24, D), BF),
             pltpu.VMEM((1, SMALL), F32), pltpu.VMEM((NC, 1, SMALL), F32),
             pltpu.VMEM((1, SMALL), F32), pltpu.VMEM((NS, 1, SMALL), F32),
         ],
-        160, 16, 2, 58 << 20,
+        176, 24, 2, 58 << 20,
     )
+    any_, whole = pl.BlockSpec(memory_space=pl.ANY), pl.BlockSpec(memory_space=pltpu.VMEM)
     output, gx, gwq, gwk, gwv, gwo_out, gwg, gwu, gwd_out = pl.pallas_call(
         assemble_body,
         out_shape=[
@@ -852,7 +917,14 @@
             jax.ShapeDtypeStruct((64, 3072), F32), jax.ShapeDtypeStruct((64, 3072), F32),
             jax.ShapeDtypeStruct((192, D), F32),
         ],
-        compiler_params=pltpu.CompilerParams(vmem_limit_bytes=40 << 20),
+        in_specs=[any_] * 6,
+        out_specs=[whole] * 9,
+        scratch_shapes=[
+            pltpu.VMEM((NC, 64, 512), BF), pltpu.VMEM((NC, 16, D), BF),
+            pltpu.VMEM((NC, 64, WCOL2), BF), pltpu.VMEM((NC, 24, D), BF),
+            pltpu.SemaphoreType.DMA((6,)),
+        ],
+        compiler_params=pltpu.CompilerParams(vmem_limit_bytes=58 << 20),
     )(output, gx, a1, ao, a2, ad)
     small = small[0]
 

time: 267 us -> 240 us (0.90)
  Pallas kernels: 251 us -> 234 us
  local copies, waits for them, and re-layouts: 12.5 us -> 3.85 us
    pallas_call x3, Pallas kernels: 249 us -> 230 us  [remote_call(): pl.pallas_call(body, out_shape=[jax.ShapeDtypeStruct(s, d) for s, d, _ in...]
    unnamed x14 -> x0, local copies, waits for them, and re-layouts: 6.29 us -> none
where the time goes in v5:
time: 240 us
  Pallas kernels  234 us (98%)
  local copies, waits for them, and re-layouts  3.85 us (2%)
    pallas_call x3, Pallas kernels, remote_call(): pl.pallas_call(body, out_shape=[jax.ShapeDtypeStruct(s, d) for s, d, _ in...  230 us

profile of v5, /device:TPU:1, one launch (start us, length us, event | category | flops | bytes accessed | tf_op | source)
XLA Modules:
  0.0 239.8 jit_solution(2006803720569001028)
XLA Ops:
  0.7 0.8 maximum_bitcast_fusion
  1.4 0.1 pad.2.clone
  1.5 0.7 maximum_maximum_fusion.gblock
  2.2 66.4 %shard_map.246 = (bf16[8,128,1024]{2,1,0:T(8,128)(2,1)}, bf16[16,64,640]{2,1,0:T(8,128)(2,1)}, bf16[16,16,1024]{2,1,0:T(8,128)(2,1)}, bf16[16,64,768]{2,1,0:T(8,...) custom-call(bf16[128,1024]{1,0:T(8,128)(2,1)} %bitcast.20, ...), custom_call_target="tpu_custom_call" | custom-call | tf_op jit(solution)/shard_map/pallas_call | solution.py:340
  68.6 1.3 slice.3.gain
  69.9 67.2 %shard_map.247 = (bf16[8,128,1024]{2,1,0:T(8,128)(2,1)}, f32[128,1024]{1,0:T(8,128)}, f32[1,1024]{1,0:T(1,128)}, bf16[2,8,64,768]{3,2,1,0:T(8,128)(2,1)}, bf16[2...) custom-call(bf16[8,128,1024]{2,1,0:T(8,128)(2,1)} %get-tuple-element.50.part, ...), custom_call_target="tpu_custom_call" | custom-call | tf_op jit(solution)/shard_map/pallas_call | solution.py:340
  137.1 96.2 %shard_map.248 = (bf16[128,1024]{1,0:T(8,128)(2,1)}, f32[128,1024]{1,0:T(8,128)}, f32[1,2304]{1,0:T(1,128)}, bf16[8,64,512]{2,1,0:T(8,128)(2,1)}, bf16[8,16,1024...) custom-call(bf16[8,128,1024]{2,1,0:T(8,128)(2,1)} %get-tuple-element.55.ga_all, ...), custom_call_target="tpu_custom_call" | custom-call | tf_op jit(solution)/shard_map/pallas_call | solution.py:340
  233.4 3.9 %shard_map.249 = (bf16[128,1024]{1,0:T(8,128)(2,1)}, f32[128,1024]{1,0:T(8,128)}, f32[64,2048]{1,0:T(8,128)}, f32[64,1024]{1,0:T(8,128)}, f32[64,1024]{1,0:T(8,1...) custom-call(bf16[128,1024]{1,0:T(8,128)(2,1)} %get-tuple-element.71.out_h, ...), custom_call_target="tpu_custom_call" | custom-call | tf_op jit(solution)/shard_map/pallas_call | solution.py:911
  237.3 1.2 fusion.2
  238.5 1.3 fusion.3
  (2 shorter events, 0.0 us)

commit v6 on v5

--- a/solution.py
+++ b/solution.py
@@ -355,8 +355,8 @@
 
 def start_body(
     tok, cot, pos, wq, wk, wv, wg, wu, gblock, wo, wd, freq,
-    g_all, w1_all, wo_all, w2_all, wd_all, hid_h, raw_h, qkv_h, tab_h, lse, heads_h, part, gvec, ghead,
-    x_all, p_all, w1, w2, hid, raw, qkv, tab, heads, ss, rs, ls,
+    g_all, w1_all, wo_all, w2_all, wd_all, hid_h, raw_h, qkv_h, tab_h, probs_h, heads_h, part, gvec, ghead,
+    x_all, p_all, w1, w2, hid, raw, qkv, tab, probs, heads, ss, rs, ls,
 ):
     s, c, core, ctx, chips, sibling, goes, comes, stays = places()
     net = Net(ss, rs, ls)
@@ -376,28 +376,10 @@
     for x in loads:
         x.wait()
 
-    def by_shard():
+    def weights():
         yield from gather(
             net, chips, [(w1, at(w1_all), lanes(WCOL1))], lambda i: i * 2 + core, sibling
         )
-
-    def moved():
-        moved = [(wo.at[c], wo_all.at[goes[0]]), (wd.at[c], wd_all.at[goes[0]])]
-        yield from move(net, moved, goes, stays)
-
-    def first(h):
-        items = [(tok.at[rows(h)], chunk(x_all, h), CPARTS)]
-        if h == 0:
-            items.append((pos, at(p_all), ((ALL, ALL), None, None)))
-        yield from gather(net, ctx, items)
-
-    weights = by_shard()
-    drive(first(0), weights, first(1), weights, moved())
-
-    def second(h):
-        yield from gather(net, ctx, [(cot.at[rows(h)], chunk(g_all, h), CPARTS)])
-
-    def by_shard_second():
         yield from gather(
             net, chips,
             [
@@ -406,6 +388,17 @@
             ],
             lambda i: i * 2 + core, sibling,
         )
+
+    def moved():
+        moved = [(wo.at[c], wo_all.at[goes[0]]), (wd.at[c], wd_all.at[goes[0]])]
+        yield from move(net, moved, goes, stays)
+
+    def by_ctx(h):
+        items = [(tok.at[rows(h)], chunk(x_all, h), CPARTS)]
+        if h == 0:
+            items.append((pos, at(p_all), ((ALL, ALL), None, None)))
+        yield from gather(net, ctx, items)
+        yield from gather(net, ctx, [(cot.at[rows(h)], chunk(g_all, h), CPARTS)])
 
     def gains():
         lane = lax.broadcasted_iota(jnp.int32, (8, 128), 1)
@@ -454,11 +447,17 @@
         top = jnp.max(score, -1, keepdims=True)
         e = jnp.exp(score - top)
         total = jnp.sum(e, -1, keepdims=True)
-        o = dot(e.astype(BF), v, NN) / total
+        share = 1.0 / total
+        o = dot(e.astype(BF), v, NN) * share
+        e = e * share
+        for m in range(n + 1):
+            probs[h, n * (n + 1) // 2 + m] = e[:, 256 * m : 256 * (m + 1)].astype(BF)
         heads[2 * n : 2 * n + 2, :, HD * h : HD * (h + 1)] = o.reshape(2, T, HD)
-        lse[h, 256 * n : 256 * (n + 1)] = top + jnp.log(total)
 
     def work():
+        yield
+        yield
+        yield
         gains()
         pl.loop(0, 4)(project)
         yield
@@ -474,19 +473,21 @@
             if n < 3:
                 yield
         stores.append(net.copy(heads, heads_h))
+        stores.append(net.copy(probs, probs_h))
 
         @pl.loop(0, NC)
         def _(i):
             part[i] = dot(heads[i].astype(BF), wo_all[...].reshape(QW, D), NN, BF)
 
     stores = []
-    drive(second(0), second(1), by_shard_second(), work())
+    side = weights()
+    drive(by_ctx(0), side, by_ctx(1), side, moved(), work())
     for x in stores:
         x.wait()
 
 
 def mid_body(
-    part, tok, cot, gain, wgu_h, wd_h, g_h,
+    part, tok, cot, gvec, wgu_h, wd_h, g_h,
     ga_all, gres_ref, ggain_ref, gw2_h, gwd_h, down_h, resid,
     wgu, wd, g_all, down_part, gw2, gwd, h_all, mixed, ggu, back_part, ga, gwd_f,
     la0, sa0, la1, sa1, lb0, sb0, lb1, sb1, ss, rs, ls,
@@ -502,7 +503,7 @@
             r = tok[rows(h)].astype(F32) + total
             resid[rows(h)] = r
             normed, _ = rms_parts(r)
-            h_all[c, rows(h)] = (normed * gain[...]).astype(BF)
+            h_all[c, rows(h)] = (normed * gvec[1:2]).astype(BF)
 
         yield from reduce(net, ctx, [(chunk(part, h), CPARTS, land, sums)], got)
         yield from gather(net, ctx, [(None, chunk(h_all, h), CPARTS)])
@@ -557,7 +558,7 @@
                 ggain_ref[...] = g
             else:
                 ggain_ref[...] += g
-            gres = cot[rows(h)].astype(F32) + rms_back(total * gain[...], normed, inverse)
+            gres = cot[rows(h)].astype(F32) + rms_back(total * gvec[1:2], normed, inverse)
             gres_ref[rows(h)] = gres
             ga[rows(h)] = gres.astype(BF)
 
@@ -593,9 +594,9 @@
 
 def end_body(
     ga_all, tok, gres_ref, resid, gvec, ghead, ggain, wo_all,
-    gw2_h, gwd_h, down_h, qkv_h, lse_h, heads_h, raw_h, tab_h, hid_h, w1_h,
+    gw2_h, gwd_h, down_h, qkv_h, probs_h, heads_h, raw_h, tab_h, hid_h, w1_h,
     out_ref, gx_ref, small_ref, a1, ao, a2, ad,
-    down_part, qkv, lse, heads, raw, tab, hid, w1_all, gw2, gwd,
+    down_part, qkv, probs, heads, raw, tab, hid, w1_all, gw2, gwd,
     gatt, delta, gwo_f, gk_f, gv_f, gqkv, part, gw1, gwo,
     la0, sa0, la1, sa1, lb0, sb0, lb1, sb1, h1, b1, l1, t1, h2, b2, l2, t2,
     h3, b3, l3, t3, h4, b4, l4, t4,
@@ -606,7 +607,7 @@
     loads = [
         net.copy(x, y)
         for x, y in (
-            (heads_h, heads), (qkv_h, qkv), (lse_h, lse), (down_h, down_part),
+            (heads_h, heads), (qkv_h, qkv), (probs_h, probs), (down_h, down_part),
             (raw_h, raw), (tab_h, tab), (hid_h, hid), (w1_h, w1_all), (gw2_h, gw2), (gwd_h, gwd),
         )
     ]
@@ -660,29 +661,29 @@
             )
 
     def attend_back(h, n, fresh):
-        width = 256 * (n + 1)
         here = slice(2 * n, 2 * n + 2)
         mine = slice(HD * h, HD * (h + 1))
         q = qkv[here, :, mine].reshape(256, HD)
-        k = qkv[0 : 2 * n + 2, :, 2 * HD : 3 * HD].reshape(width, HD)
-        v = qkv[0 : 2 * n + 2, :, 3 * HD :].reshape(width, HD)
         g = gatt[here, :, mine].reshape(256, HD)
-        span = slice(256 * n, 256 * (n + 1))
-        score = dot(q, k, NT) * HD**-0.5
-        row = lax.broadcasted_iota(jnp.int32, (256, width), 0) + 256 * n
-        col = lax.broadcasted_iota(jnp.int32, (256, width), 1)
-        p = jnp.where(col <= row, jnp.exp(score - lse[h, span]), 0.0)
-        gv = dot(p.astype(BF), g, TN)
-        gs = (p * (dot(g, v, NT) - delta[h, span])).astype(BF)
-        gk = dot(gs, q, TN)
-        if fresh:
-            gv_f[0:width] = gv
-            gk_f[0:width] = gk
-        else:
-            gv_f[0:width] += gv
-            gk_f[0:width] += gk
-        gq = dot(gs, k, NN) * HD**-0.5
-        turn_back(gq, here, mine, 0, fresh)
+        d = delta[h, 256 * n : 256 * (n + 1)]
+        gq = None
+        for m in range(n + 1):
+            k = qkv[2 * m : 2 * m + 2, :, 2 * HD : 3 * HD].reshape(256, HD)
+            v = qkv[2 * m : 2 * m + 2, :, 3 * HD :].reshape(256, HD)
+            p = probs[h, n * (n + 1) // 2 + m]
+            gv = dot(p, g, TN)
+            gs = (p.astype(F32) * (dot(g, v, NT) - d)).astype(BF)
+            gk = dot(gs, q, TN)
+            span = slice(256 * m, 256 * (m + 1))
+            if fresh:
+                gv_f[span] = gv
+                gk_f[span] = gk
+            else:
+                gv_f[span] += gv
+                gk_f[span] += gk
+            x = dot(gs, k, NN)
+            gq = x if gq is None else gq + x
+        turn_back(gq * HD**-0.5, here, mine, 0, fresh)
 
     def turn_back(g, here, mine, kind, fresh):
         n = g.shape[0]
@@ -831,14 +832,14 @@
     freq = np.concatenate([freq, freq])[:, None]
 
     (
-        g_all, w1_all, wo_all, w2_all, wd_all, hid, raw, qkv, tab, lse, heads, out_part, gvec, ghead,
+        g_all, w1_all, wo_all, w2_all, wd_all, hid, raw, qkv, tab, probs, heads, out_part, gvec, ghead,
     ) = remote_call(
         start_body,
         [
             ((NC, T, D), BF, "h"), ((NS, 64, WCOL1), BF, "v"), ((NS, 16, D), BF, "v"),
             ((NS, 64, WCOL2), BF, "h"), ((NS, 24, D), BF, "h"),
             ((NC, T, D), BF, "h"), ((NC, T, 512), F32, "h"), ((NC, T, 512), BF, "h"),
-            ((NC, T, 2 * HD), F32, "h"), ((2, SEQ, 1), F32, "v"), ((NC, T, QW), F32, "h"),
+            ((NC, T, 2 * HD), F32, "h"), ((2, 10, 256, 256), BF, "h"), ((NC, T, QW), F32, "h"),
             ((NC, T, D), BF, "v"), ((2, D), F32, "v"), ((2, HD), F32, "v"),
         ],
         "h" * 11 + "v",
@@ -851,7 +852,7 @@
             pltpu.VMEM((64, WCOL1), BF), pltpu.VMEM((64, WCOL2), BF),
             pltpu.VMEM((NC, T, D), BF), pltpu.VMEM((NC, T, 512), F32),
             pltpu.VMEM((NC, T, 512), BF), pltpu.VMEM((NC, T, 2 * HD), F32),
-            pltpu.VMEM((NC, T, QW), F32),
+            pltpu.VMEM((2, 10, 256, 256), BF), pltpu.VMEM((NC, T, QW), F32),
         ],
         144, 24, 0, 58 << 20,
     )
@@ -863,7 +864,7 @@
             ((NC, T, D), BF, "h"), ((T, D), F32, "v"),
         ],
         "vvvvhhh",
-        (out_part, tok, cot, gvec[1:2], w2_all.reshape(D, 2 * FW), wd_all.reshape(FW, D), g_all),
+        (out_part, tok, cot, gvec, w2_all.reshape(D, 2 * FW), wd_all.reshape(FW, D), g_all),
         [
             pltpu.VMEM((D, 2 * FW), BF), pltpu.VMEM((FW, D), BF), pltpu.VMEM((NC, T, D), BF),
             pltpu.VMEM((NC, T, D), BF), pltpu.VMEM((2, 8, 64, WCOL2), BF),
@@ -884,10 +885,11 @@
         "v" * 8 + "h" * 10,
         (
             ga_all, tok, grad_resid, resid, gvec, ghead, ggain_mlp, wo_all, gw2, gwd,
-            down_part, qkv, lse, heads, raw, tab, hid, w1_all,
+            down_part, qkv, probs, heads, raw, tab, hid, w1_all,
         ),
         [
-            pltpu.VMEM((NC, T, D), BF), pltpu.VMEM((NC, T, 512), BF), pltpu.VMEM((2, SEQ, 1), F32),
+            pltpu.VMEM((NC, T, D), BF), pltpu.VMEM((NC, T, 512), BF),
+            pltpu.VMEM((2, 10, 256, 256), BF),
             pltpu.VMEM((NC, T, QW), F32), pltpu.VMEM((NC, T, 512), F32),
             pltpu.VMEM((NC, T, 2 * HD), F32), pltpu.VMEM((NC, T, D), BF),
             pltpu.VMEM((NS, 64, WCOL1), BF),

time: 240 us -> 238 us (level)
  no operation moved by 1% of the time
where the time goes in v6:
time: 238 us
  Pallas kernels  233 us (98%)
  local copies, waits for them, and re-layouts  2.57 us (1%)
    pallas_call x3, Pallas kernels, remote_call(): pl.pallas_call(body, out_shape=[jax.ShapeDtypeStruct(s, d) for s, d, _ in...  229 us

profile of v6, /device:TPU:1, one launch (start us, length us, event | category | flops | bytes accessed | tf_op | source)
XLA Modules:
  0.0 238.0 jit_solution(17522489191192468671)
XLA Ops:
  0.7 0.8 maximum_bitcast_fusion
  1.4 0.1 pad.2.clone
  1.5 0.7 maximum_maximum_fusion.gblock
  2.2 64.6 %shard_map.246 = (bf16[8,128,1024]{2,1,0:T(8,128)(2,1)}, bf16[16,64,640]{2,1,0:T(8,128)(2,1)}, bf16[16,16,1024]{2,1,0:T(8,128)(2,1)}, bf16[16,64,768]{2,1,0:T(8,...) custom-call(bf16[128,1024]{1,0:T(8,128)(2,1)} %bitcast.20, ...), custom_call_target="tpu_custom_call" | custom-call | tf_op jit(solution)/shard_map/pallas_call | solution.py:340
  66.8 66.2 %shard_map.247 = (bf16[8,128,1024]{2,1,0:T(8,128)(2,1)}, f32[128,1024]{1,0:T(8,128)}, f32[1,1024]{1,0:T(1,128)}, bf16[2,8,64,768]{3,2,1,0:T(8,128)(2,1)}, bf16[2...) custom-call(bf16[8,128,1024]{2,1,0:T(8,128)(2,1)} %get-tuple-element.50.part, ...), custom_call_target="tpu_custom_call" | custom-call | tf_op jit(solution)/shard_map/pallas_call | solution.py:340
  133.0 98.6 %shard_map.248 = (bf16[128,1024]{1,0:T(8,128)(2,1)}, f32[128,1024]{1,0:T(8,128)}, f32[1,2304]{1,0:T(1,128)}, bf16[8,64,512]{2,1,0:T(8,128)(2,1)}, bf16[8,16,1024...) custom-call(bf16[8,128,1024]{2,1,0:T(8,128)(2,1)} %get-tuple-element.55.ga_all, ...), custom_call_target="tpu_custom_call" | custom-call | tf_op jit(solution)/shard_map/pallas_call | solution.py:340
  231.6 3.9 %shard_map.249 = (bf16[128,1024]{1,0:T(8,128)(2,1)}, f32[128,1024]{1,0:T(8,128)}, f32[64,2048]{1,0:T(8,128)}, f32[64,1024]{1,0:T(8,128)}, f32[64,1024]{1,0:T(8,1...) custom-call(bf16[128,1024]{1,0:T(8,128)(2,1)} %get-tuple-element.71.out_h, ...), custom_call_target="tpu_custom_call" | custom-call | tf_op jit(solution)/shard_map/pallas_call | solution.py:913
  235.6 1.3 fusion.2
  236.8 1.2 fusion.3
  (2 shorter events, 0.0 us)

commit v7 on v6

--- a/solution.py
+++ b/solution.py
@@ -24,11 +24,6 @@
 SMALL = 2304
 
 ALL = slice(None)
-
-
-def lanes(width):
-    a = (width // 128 + 1) // 2 * 128
-    return ((ALL, slice(0, a)), (ALL, slice(a, width)), None)
 
 
 def view(ref, part):
@@ -216,6 +211,57 @@
             c.wait()
 
 
+def gather_shard(net, ring, slot, across, sibling, items):
+    me, z = ring.idx(0, 0), ring.idx(0, 1)
+    over, local, first = [], [], []
+
+    def pass_on(at, *places):
+        for i in places:
+            over.append(net.send(at(slot(i)), at(slot(i)), sibling))
+
+    for own, other, at in items:
+        for i in (me, z) if own is None else (me,):
+            here = at(slot(i))
+            src = here if own is None else own
+            for d in (1, 3, 2):
+                first.append(net.send(src, here, ring.dev(d, 0)))
+            over.append(net.send(src, here, sibling))
+        if own is not None:
+            for d in across:
+                first.append(net.send(other, here, d))
+            local.append(net.copy(own, here))
+    yield
+    yield
+    for c in first:
+        c.wait_recv()
+    for own, _, at in items:
+        for d in (1, 3, 2):
+            pass_on(at, ring.idx(d, 0), ring.idx(d, 1))
+        if own is not None:
+            pass_on(at, z)
+    for c in local:
+        c.wait()
+    yield
+    for c in first:
+        c.wait_send()
+    for c in over:
+        c.wait()
+
+
+def gather_peers(net, ring, items):
+    me = ring.idx(0, 0)
+    sent, local = [], []
+    for own, at in items:
+        here = at(me)
+        for d in range(1, 8):
+            sent.append(net.send(here if own is None else own, here, ring.device(lax.rem(me + d, 8))))
+        if own is not None:
+            local.append(net.copy(own, here))
+    yield
+    for c in sent + local:
+        c.wait()
+
+
 def reduce(net, ring, items, result):
     left, right, pair = ring_devices(ring)
     me, a, b, z = ring.idx(0, 0), ring.idx(-1, 0), ring.idx(1, 0), ring.idx(0, 1)
@@ -269,9 +315,9 @@
     return lambda i: ref.at[i]
 
 
-CHUNKS = 2
+CHUNKS = 4
 CROWS = T // CHUNKS
-CPARTS = ((slice(0, 32), ALL), (slice(32, 64), ALL), None)
+CPARTS = ((slice(0, CROWS // 2), ALL), (slice(CROWS // 2, CROWS), ALL), None)
 
 
 def rows(h):
@@ -282,34 +328,45 @@
     return lambda i: ref.at[i, rows(h)]
 
 
+def each(thread, land, sums):
+    return [thread(h, land.at[:, rows(h)], sums.at[:, rows(h)]) for h in range(CHUNKS)]
+
+
 def chunk_scratch():
-    return [pltpu.VMEM((7, CROWS, D), BF), pltpu.VMEM((5, CROWS, D), BF)] * CHUNKS
-
-
-def reduce_scratch(shape):
-    return [pltpu.VMEM((7,) + shape, BF), pltpu.VMEM((5,) + shape, BF)]
+    return [pltpu.VMEM((7, T, D), BF), pltpu.VMEM((5, T, D), BF)]
 
 
 def reduce_shard(net, chips, core, sibling, items, result):
-    over = []
-    for p, _, half, _, _, _ in items:
+    over, sent = [], []
+    for p, half, _, _ in items:
         over.append(net.send(p.at[1 - core], half, sibling))
     yield
+    me = chips.idx(0, 0)
     for c in over:
         c.wait_recv()
-    for p, _, half, both, _, _ in items:
+    for p, half, both, land in items:
 
         @pl.loop(0, 8)
         def _(j):
             both[j] = (p[core, j].astype(F32) + half[j].astype(F32)).astype(BF)
 
-    yield from reduce(net, chips, [(at(i[3]), i[1], i[4], i[5]) for i in items], result)
-    for c in over:
+        for d in range(1, 8):
+            j = lax.rem(me + d, 8)
+            sent.append(net.send(both.at[j], land.at[me], chips.device(j)))
+    yield
+    for c in sent:
+        c.wait_recv()
+    for k, (_, _, both, land) in enumerate(items):
+        total = both[me].astype(F32)
+        for d in range(1, 8):
+            total = total + land[lax.rem(me + d, 8)].astype(F32)
+        result(k, total)
+    for c in over + sent:
         c.wait_send()
 
 
 def shard_scratch(shape):
-    return [pltpu.VMEM((8,) + shape, BF), pltpu.VMEM((8,) + shape, BF)] + reduce_scratch(shape)
+    return [pltpu.VMEM((8,) + shape, BF)] * 3
 
 
 def rms_parts(v):
@@ -356,42 +413,56 @@
 def start_body(
     tok, cot, pos, wq, wk, wv, wg, wu, gblock, wo, wd, freq,
     g_all, w1_all, wo_all, w2_all, wd_all, hid_h, raw_h, qkv_h, tab_h, probs_h, heads_h, part, gvec, ghead,
-    x_all, p_all, w1, w2, hid, raw, qkv, tab, probs, heads, ss, rs, ls,
+    x_all, p_all, w1, w2, v1, v2, hid, raw, qkv, tab, probs, heads, ss, rs, ls,
 ):
     s, c, core, ctx, chips, sibling, goes, comes, stays = places()
     net = Net(ss, rs, ls)
 
-    def cut(w, width):
-        return w.at[:, pl.ds(pl.multiple_of(c * width, 128), width)]
+    other = c + 1 - 2 * lax.rem(c, 2)
+    flip = s + 2 - 4 * lax.rem(s // 2, 2)
+    across = [((lax.rem(s // 4 + d, 4)) * 4 + lax.rem(flip, 4), other) for d in (0, 1, 3, 2)]
+    goes_z = (goes[0] + 2 - 4 * lax.rem(goes[0] // 2, 2), goes[1])
+    comes_z = (2 * c + flip // 8, lax.rem(flip, 8))
+
+    def cut(w, width, i):
+        return w.at[:, pl.ds(pl.multiple_of(i * width, 128), width)]
 
     loads = [
         net.copy(x, y)
+        for i, one, two in ((c, w1, w2), (other, v1, v2))
         for x, y in (
-            (cut(wq, QW), w1.at[:, 0:QW]), (cut(wk, HD), w1.at[:, QW : QW + HD]),
-            (cut(wv, HD), w1.at[:, QW + HD : 512]), (gblock, w1.at[:, 512:WCOL1]),
-            (cut(wg, FW), w2.at[:, 0:FW]), (cut(wu, FW), w2.at[:, FW : 2 * FW]),
+            (cut(wq, QW, i), one.at[:, 0:QW]), (cut(wk, HD, i), one.at[:, QW : QW + HD]),
+            (cut(wv, HD, i), one.at[:, QW + HD : 512]), (gblock, one.at[:, 512:WCOL1]),
+            (cut(wg, FW, i), two.at[:, 0:FW]), (cut(wu, FW, i), two.at[:, FW : 2 * FW]),
         )
     ]
-    greet(ring_devices(ctx) + ring_devices(chips) + [sibling], (goes, comes, stays))
+    greet(
+        ring_devices(ctx) + [chips.dev(d, 0) for d in (1, 2, 3)] + across + [sibling, goes_z, comes_z],
+        (goes, comes, stays),
+    )
     for x in loads:
         x.wait()
 
+    def place(i):
+        return i * 2 + core
+
     def weights():
-        yield from gather(
-            net, chips, [(w1, at(w1_all), lanes(WCOL1))], lambda i: i * 2 + core, sibling
+        yield from gather_shard(
+            net, chips, place, across, sibling, [(w1, v1, at(w1_all))]
         )
-        yield from gather(
-            net, chips,
+        yield from gather_shard(
+            net, chips, place, across, sibling,
             [
-                (w2, at(w2_all), lanes(WCOL2)), (None, at(wd_all), lanes(D)),
-                (None, at(wo_all), lanes(D)),
+                (w2, v2, at(w2_all)), (None, None, at(wd_all)), (None, None, at(wo_all)),
             ],
-            lambda i: i * 2 + core, sibling,
         )
 
     def moved():
         moved = [(wo.at[c], wo_all.at[goes[0]]), (wd.at[c], wd_all.at[goes[0]])]
+        second = [net.send(x, y, goes_z) for x, y in moved]
         yield from move(net, moved, goes, stays)
+        for x in second:
+            x.wait()
 
     def by_ctx(h):
         items = [(tok.at[rows(h)], chunk(x_all, h), CPARTS)]
@@ -481,7 +552,7 @@
 
     stores = []
     side = weights()
-    drive(by_ctx(0), side, by_ctx(1), side, moved(), work())
+    drive(side, *[by_ctx(h) for h in range(CHUNKS)], moved(), work())
     for x in stores:
         x.wait()
 
@@ -490,7 +561,7 @@
     part, tok, cot, gvec, wgu_h, wd_h, g_h,
     ga_all, gres_ref, ggain_ref, gw2_h, gwd_h, down_h, resid,
     wgu, wd, g_all, down_part, gw2, gwd, h_all, mixed, ggu, back_part, ga, gwd_f,
-    la0, sa0, la1, sa1, lb0, sb0, lb1, sb1, ss, rs, ls,
+    la, sa, lb, sb, ss, rs, ls,
 ):
     s, c, core, ctx, chips, sibling, goes, comes, stays = places()
     net = Net(ss, rs, ls)
@@ -547,7 +618,7 @@
         yield
         blocks([ctx.idx(2, 1)])
 
-    drive(forward(0, la0, sa0), forward(1, la1, sa1), work())
+    drive(*each(forward, la, sa), work())
     stores.append(net.copy(down_part, down_h))
 
     def got_back(h):
@@ -587,7 +658,7 @@
         stores.append(net.copy(gw2, gw2_h))
         stores.append(net.copy(gwd, gwd_h))
 
-    drive(backward(0, lb0, sb0), backward(1, lb1, sb1), grads())
+    drive(*each(backward, lb, sb), grads())
     for x in stores:
         x.wait()
 
@@ -598,8 +669,8 @@
     out_ref, gx_ref, small_ref, a1, ao, a2, ad,
     down_part, qkv, probs, heads, raw, tab, hid, w1_all, gw2, gwd,
     gatt, delta, gwo_f, gk_f, gv_f, gqkv, part, gw1, gwo,
-    la0, sa0, la1, sa1, lb0, sb0, lb1, sb1, h1, b1, l1, t1, h2, b2, l2, t2,
-    h3, b3, l3, t3, h4, b4, l4, t4,
+    la, sa, lb, sb, h1, b1, l1, h2, b2, l2,
+    h3, b3, l3, h4, b4, l4,
     s1, so, gw2_sum, gwd_sum, own_d, sm, smc, sm2, sms, ss, rs, ls,
 ):
     s, c, core, ctx, chips, sibling, goes, comes, stays = places()
@@ -631,10 +702,10 @@
         loads[9].wait()
         yield from reduce_shard(
             net, chips, core, sibling,
-            [(gw2, lanes(WCOL2), h3, b3, l3, t3), (gwd, lanes(D), h4, b4, l4, t4)], got_ff,
+            [(gw2, h3, b3, l3), (gwd, h4, b4, l4)], got_ff,
         )
         yield from move(net, [(gwd_sum, own_d)], comes, stays)
-        yield from gather(net, ctx, [(gw2_sum, at(a2), lanes(WCOL2)), (own_d, at(ad), lanes(D))])
+        yield from gather_peers(net, ctx, [(gw2_sum, at(a2)), (own_d, at(ad))])
 
     def got_out(k, total):
         so[...] = total.astype(BF)
@@ -646,10 +717,10 @@
         for i in range(NS):
             gwo[i % 2, i // 2] = gwo_f[16 * i : 16 * (i + 1)].astype(BF)
         yield from reduce_shard(
-            net, chips, core, sibling, [(gwo, lanes(D), h2, b2, l2, t2)], got_out
+            net, chips, core, sibling, [(gwo, h2, b2, l2)], got_out
         )
         yield from move(net, [(so, ao.at[comes[1]])], comes, stays)
-        yield from gather(net, ctx, [(None, at(ao), lanes(D))])
+        yield from gather_peers(net, ctx, [(None, at(ao))])
 
     def head_grads(i):
         g = dot(ga_all[i], wo_all[...].reshape(QW, D), NT, BF)
@@ -727,7 +798,7 @@
     loads[0].wait()
     main = work()
     rest = drive(
-        feed_forward(0, lb0, sb0), feed_forward(1, lb1, sb1), out_grad(), feed_forward_grads(), main,
+        *each(feed_forward, lb, sb), out_grad(), feed_forward_grads(), main,
         until=main,
     )
 
@@ -783,12 +854,13 @@
             gw1[1, j] = g[64:128]
 
         yield from reduce_shard(
-            net, chips, core, sibling, [(gw1, lanes(512), h1, b1, l1, t1)], got_shard
+            net, chips, core, sibling, [(gw1, h1, b1, l1)], got_shard
         )
-        yield from gather(net, ctx, [(s1, at(a1), lanes(512))])
+        yield from gather_peers(net, ctx, [(s1, at(a1))])
 
     last = grads()
-    drive(by_ctx(0, la0, sa0), last, by_ctx(1, la1, sa1), last, *rest, small())
+    tokens = each(by_ctx, la, sa)
+    drive(*tokens, last, *rest, small())
 
 
 def assemble_body(
@@ -850,11 +922,12 @@
         [
             pltpu.VMEM((NC, T, D), BF), pltpu.VMEM((NC, 1, T), jnp.int32),
             pltpu.VMEM((64, WCOL1), BF), pltpu.VMEM((64, WCOL2), BF),
+            pltpu.VMEM((64, WCOL1), BF), pltpu.VMEM((64, WCOL2), BF),
             pltpu.VMEM((NC, T, D), BF), pltpu.VMEM((NC, T, 512), F32),
             pltpu.VMEM((NC, T, 512), BF), pltpu.VMEM((NC, T, 2 * HD), F32),
             pltpu.VMEM((2, 10, 256, 256), BF), pltpu.VMEM((NC, T, QW), F32),
         ],
-        144, 24, 0, 58 << 20,
+        224, 32, 0, 58 << 20,
     )
     ga_all, grad_resid, ggain_mlp, gw2, gwd, down_part, resid = remote_call(
         mid_body,
@@ -873,7 +946,7 @@
             pltpu.VMEM((NC, T, D), BF), pltpu.VMEM((T, D), BF), pltpu.VMEM((FW, D), F32),
         ]
         + chunk_scratch() * 2,
-        96, 16, 1, 58 << 20,
+        192, 16, 1, 58 << 20,
     )
     output, gx, small, a1, ao, a2, ad = remote_call(
         end_body,
@@ -907,7 +980,7 @@
             pltpu.VMEM((1, SMALL), F32), pltpu.VMEM((NC, 1, SMALL), F32),
             pltpu.VMEM((1, SMALL), F32), pltpu.VMEM((NS, 1, SMALL), F32),
         ],
-        176, 24, 2, 58 << 20,
+        224, 32, 2, 58 << 20,
     )
     any_, whole = pl.BlockSpec(memory_space=pl.ANY), pl.BlockSpec(memory_space=pltpu.VMEM)
     output, gx, gwq, gwk, gwv, gwo_out, gwg, gwu, gwd_out = pl.pallas_call(

time: 238 us -> 259 us (1.088)
  Pallas kernels: 233 us -> 254 us
    pallas_call x3, Pallas kernels: 229 us -> 250 us  [remote_call(): pl.pallas_call(body, out_shape=[jax.ShapeDtypeStruct(s, d) for s, d, _ in...]
where the time goes in v7:
time: 259 us; the launch traced here: 258 us
  Pallas kernels  254 us (98%)
    pallas_call x3, Pallas kernels, remote_call(): pl.pallas_call(body, out_shape=[jax.ShapeDtypeStruct(s, d) for s, d, _ in...  250 us

profile of v7, /device:TPU:1, one launch (start us, length us, event | category | flops | bytes accessed | tf_op | source)
XLA Modules:
  0.0 258.4 jit_solution(13526617717078057474)
XLA Ops:
  0.7 0.8 maximum_bitcast_fusion
  1.4 0.1 pad.2.clone
  1.5 0.7 maximum_maximum_fusion.gblock
  2.2 63.7 %shard_map.246 = (bf16[8,128,1024]{2,1,0:T(8,128)(2,1)}, bf16[16,64,640]{2,1,0:T(8,128)(2,1)}, bf16[16,16,1024]{2,1,0:T(8,128)(2,1)}, bf16[16,64,768]{2,1,0:T(8,...) custom-call(bf16[128,1024]{1,0:T(8,128)(2,1)} %bitcast.20, ...), custom_call_target="tpu_custom_call" | custom-call | tf_op jit(solution)/shard_map/pallas_call | solution.py:397
  66.0 69.5 %shard_map.247 = (bf16[8,128,1024]{2,1,0:T(8,128)(2,1)}, f32[128,1024]{1,0:T(8,128)}, f32[1,1024]{1,0:T(1,128)}, bf16[2,8,64,768]{3,2,1,0:T(8,128)(2,1)}, bf16[2...) custom-call(bf16[8,128,1024]{2,1,0:T(8,128)(2,1)} %get-tuple-element.50.part, ...), custom_call_target="tpu_custom_call" | custom-call | tf_op jit(solution)/shard_map/pallas_call | solution.py:397
  135.5 116.5 %shard_map.248 = (bf16[128,1024]{1,0:T(8,128)(2,1)}, f32[128,1024]{1,0:T(8,128)}, f32[1,2304]{1,0:T(1,128)}, bf16[8,64,512]{2,1,0:T(8,128)(2,1)}, bf16[8,16,1024...) custom-call(bf16[8,128,1024]{2,1,0:T(8,128)(2,1)} %get-tuple-element.55.ga_all, ...), custom_call_target="tpu_custom_call" | custom-call | tf_op jit(solution)/shard_map/pallas_call | solution.py:397
  252.0 3.9 %shard_map.249 = (bf16[128,1024]{1,0:T(8,128)(2,1)}, f32[128,1024]{1,0:T(8,128)}, f32[64,2048]{1,0:T(8,128)}, f32[64,1024]{1,0:T(8,128)}, f32[64,1024]{1,0:T(8,1...) custom-call(bf16[128,1024]{1,0:T(8,128)(2,1)} %get-tuple-element.71.out_h, ...), custom_call_target="tpu_custom_call" | custom-call | tf_op jit(solution)/shard_map/pallas_call | solution.py:986
  256.0 1.3 fusion.2
  257.2 1.2 fusion.3
  (2 shorter events, 0.0 us)

commit v8 on v7

--- a/solution.py
+++ b/solution.py
@@ -24,6 +24,11 @@
 SMALL = 2304
 
 ALL = slice(None)
+
+
+def lanes(width):
+    a = (width // 128 + 1) // 2 * 128
+    return ((ALL, slice(0, a)), (ALL, slice(a, width)), None)
 
 
 def view(ref, part):
@@ -248,20 +253,6 @@
         c.wait()
 
 
-def gather_peers(net, ring, items):
-    me = ring.idx(0, 0)
-    sent, local = [], []
-    for own, at in items:
-        here = at(me)
-        for d in range(1, 8):
-            sent.append(net.send(here if own is None else own, here, ring.device(lax.rem(me + d, 8))))
-        if own is not None:
-            local.append(net.copy(own, here))
-    yield
-    for c in sent + local:
-        c.wait()
-
-
 def reduce(net, ring, items, result):
     left, right, pair = ring_devices(ring)
     me, a, b, z = ring.idx(0, 0), ring.idx(-1, 0), ring.idx(1, 0), ring.idx(0, 1)
@@ -336,37 +327,30 @@
     return [pltpu.VMEM((7, T, D), BF), pltpu.VMEM((5, T, D), BF)]
 
 
+def reduce_scratch(shape):
+    return [pltpu.VMEM((7,) + shape, BF), pltpu.VMEM((5,) + shape, BF)]
+
+
 def reduce_shard(net, chips, core, sibling, items, result):
-    over, sent = [], []
-    for p, half, _, _ in items:
+    over = []
+    for p, _, half, _, _, _ in items:
         over.append(net.send(p.at[1 - core], half, sibling))
     yield
-    me = chips.idx(0, 0)
     for c in over:
         c.wait_recv()
-    for p, half, both, land in items:
+    for p, _, half, both, _, _ in items:
 
         @pl.loop(0, 8)
         def _(j):
             both[j] = (p[core, j].astype(F32) + half[j].astype(F32)).astype(BF)
 
-        for d in range(1, 8):
-            j = lax.rem(me + d, 8)
-            sent.append(net.send(both.at[j], land.at[me], chips.device(j)))
-    yield
-    for c in sent:
-        c.wait_recv()
-    for k, (_, _, both, land) in enumerate(items):
-        total = both[me].astype(F32)
-        for d in range(1, 8):
-            total = total + land[lax.rem(me + d, 8)].astype(F32)
-        result(k, total)
-    for c in over + sent:
+    yield from reduce(net, chips, [(at(i[3]), i[1], i[4], i[5]) for i in items], result)
+    for c in over:
         c.wait_send()
 
 
 def shard_scratch(shape):
-    return [pltpu.VMEM((8,) + shape, BF)] * 3
+    return [pltpu.VMEM((8,) + shape, BF), pltpu.VMEM((8,) + shape, BF)] + reduce_scratch(shape)
 
 
 def rms_parts(v):
@@ -522,7 +506,7 @@
         o = dot(e.astype(BF), v, NN) * share
         e = e * share
         for m in range(n + 1):
-            probs[h, n * (n + 1) // 2 + m] = e[:, 256 * m : 256 * (m + 1)].astype(BF)
+            probs[h, n * (n + 1) // 2 + m] = e[:, 256 * m : 256 * (m + 1)].astype(BF).T
         heads[2 * n : 2 * n + 2, :, HD * h : HD * (h + 1)] = o.reshape(2, T, HD)
 
     def work():
@@ -669,8 +653,8 @@
     out_ref, gx_ref, small_ref, a1, ao, a2, ad,
     down_part, qkv, probs, heads, raw, tab, hid, w1_all, gw2, gwd,
     gatt, delta, gwo_f, gk_f, gv_f, gqkv, part, gw1, gwo,
-    la, sa, lb, sb, h1, b1, l1, h2, b2, l2,
-    h3, b3, l3, h4, b4, l4,
+    la, sa, lb, sb, h1, b1, l1, t1, h2, b2, l2, t2,
+    h3, b3, l3, t3, h4, b4, l4, t4,
     s1, so, gw2_sum, gwd_sum, own_d, sm, smc, sm2, sms, ss, rs, ls,
 ):
     s, c, core, ctx, chips, sibling, goes, comes, stays = places()
@@ -702,10 +686,10 @@
         loads[9].wait()
         yield from reduce_shard(
             net, chips, core, sibling,
-            [(gw2, h3, b3, l3), (gwd, h4, b4, l4)], got_ff,
+            [(gw2, lanes(WCOL2), h3, b3, l3, t3), (gwd, lanes(D), h4, b4, l4, t4)], got_ff,
         )
         yield from move(net, [(gwd_sum, own_d)], comes, stays)
-        yield from gather_peers(net, ctx, [(gw2_sum, at(a2)), (own_d, at(ad))])
+        yield from gather(net, ctx, [(gw2_sum, at(a2), lanes(WCOL2)), (own_d, at(ad), lanes(D))])
 
     def got_out(k, total):
         so[...] = total.astype(BF)
@@ -717,34 +701,33 @@
         for i in range(NS):
             gwo[i % 2, i // 2] = gwo_f[16 * i : 16 * (i + 1)].astype(BF)
         yield from reduce_shard(
-            net, chips, core, sibling, [(gwo, h2, b2, l2)], got_out
+            net, chips, core, sibling, [(gwo, lanes(D), h2, b2, l2, t2)], got_out
         )
         yield from move(net, [(so, ao.at[comes[1]])], comes, stays)
-        yield from gather_peers(net, ctx, [(None, at(ao))])
+        yield from gather(net, ctx, [(None, at(ao), lanes(D))])
 
     def head_grads(i):
         g = dot(ga_all[i], wo_all[...].reshape(QW, D), NT, BF)
         gatt[i] = g
         both = g.astype(F32) * heads[i]
         for h in range(2):
-            delta[h, pl.ds(pl.multiple_of(i * T, T), T)] = jnp.sum(
-                both[:, HD * h : HD * (h + 1)], -1, keepdims=True
-            )
+            d = jnp.sum(both[:, HD * h : HD * (h + 1)], -1, keepdims=True)
+            delta[h, 0:1, pl.ds(pl.multiple_of(i * T, T), T)] = jnp.broadcast_to(d, (T, T)).T[0:1]
 
     def attend_back(h, n, fresh):
         here = slice(2 * n, 2 * n + 2)
         mine = slice(HD * h, HD * (h + 1))
         q = qkv[here, :, mine].reshape(256, HD)
         g = gatt[here, :, mine].reshape(256, HD)
-        d = delta[h, 256 * n : 256 * (n + 1)]
+        d = delta[h, 0:1, 256 * n : 256 * (n + 1)]
         gq = None
         for m in range(n + 1):
             k = qkv[2 * m : 2 * m + 2, :, 2 * HD : 3 * HD].reshape(256, HD)
             v = qkv[2 * m : 2 * m + 2, :, 3 * HD :].reshape(256, HD)
             p = probs[h, n * (n + 1) // 2 + m]
-            gv = dot(p, g, TN)
-            gs = (p.astype(F32) * (dot(g, v, NT) - d)).astype(BF)
-            gk = dot(gs, q, TN)
+            gv = dot(p, g, NN)
+            gs = (p.astype(F32) * (dot(v, g, NT) - d)).astype(BF)
+            gk = dot(gs, q, NN)
             span = slice(256 * m, 256 * (m + 1))
             if fresh:
                 gv_f[span] = gv
@@ -752,7 +735,7 @@
             else:
                 gv_f[span] += gv
                 gk_f[span] += gk
-            x = dot(gs, k, NN)
+            x = dot(gs, k, TN)
             gq = x if gq is None else gq + x
         turn_back(gq * HD**-0.5, here, mine, 0, fresh)
 
@@ -854,13 +837,13 @@
             gw1[1, j] = g[64:128]
 
         yield from reduce_shard(
-            net, chips, core, sibling, [(gw1, h1, b1, l1)], got_shard
+            net, chips, core, sibling, [(gw1, lanes(512), h1, b1, l1, t1)], got_shard
         )
-        yield from gather_peers(net, ctx, [(s1, at(a1))])
+        yield from gather(net, ctx, [(s1, at(a1), lanes(512))])
 
     last = grads()
     tokens = each(by_ctx, la, sa)
-    drive(*tokens, last, *rest, small())
+    drive(*tokens[:2], last, *tokens[2:], last, *rest, small())
 
 
 def assemble_body(
@@ -967,7 +950,7 @@
             pltpu.VMEM((NC, T, 2 * HD), F32), pltpu.VMEM((NC, T, D), BF),
             pltpu.VMEM((NS, 64, WCOL1), BF),
             pltpu.VMEM((2, 8, 64, WCOL2), BF), pltpu.VMEM((2, 8, 24, D), BF),
-            pltpu.VMEM((NC, T, QW), BF), pltpu.VMEM((2, SEQ, 1), F32), pltpu.VMEM((QW, D), F32),
+            pltpu.VMEM((NC, T, QW), BF), pltpu.VMEM((2, 8, SEQ), F32), pltpu.VMEM((QW, D), F32),
             pltpu.VMEM((SEQ, HD), F32), pltpu.VMEM((SEQ, HD), F32), pltpu.VMEM((NC, T, 512), BF),
             pltpu.VMEM((NC, T, D), BF), pltpu.VMEM((2, 8, 64, 512), BF),
             pltpu.VMEM((2, 8, 16, D), BF),

time: 259 us -> 236 us (0.911)
  Pallas kernels: 254 us -> 231 us
    pallas_call x3, Pallas kernels: 250 us -> 227 us  [remote_call(): pl.pallas_call(body, out_shape=[jax.ShapeDtypeStruct(s, d) for s, d, _ in...]
where the time goes in v8:
time: 236 us
  Pallas kernels  231 us (98%)
  local copies, waits for them, and re-layouts  2.57 us (1%)
    pallas_call x3, Pallas kernels, remote_call(): pl.pallas_call(body, out_shape=[jax.ShapeDtypeStruct(s, d) for s, d, _ in...  227 us

profile of v8, /device:TPU:1, one launch (start us, length us, event | category | flops | bytes accessed | tf_op | source)
XLA Modules:
  0.0 235.7 jit_solution(16563795231339955606)
XLA Ops:
  0.7 0.8 maximum_bitcast_fusion
  1.4 0.1 pad.2.clone
  1.5 0.7 maximum_maximum_fusion.gblock
  2.2 63.8 %shard_map.246 = (bf16[8,128,1024]{2,1,0:T(8,128)(2,1)}, bf16[16,64,640]{2,1,0:T(8,128)(2,1)}, bf16[16,16,1024]{2,1,0:T(8,128)(2,1)}, bf16[16,64,768]{2,1,0:T(8,...) custom-call(bf16[128,1024]{1,0:T(8,128)(2,1)} %bitcast.20, ...), custom_call_target="tpu_custom_call" | custom-call | tf_op jit(solution)/shard_map/pallas_call | solution.py:381
  66.0 69.5 %shard_map.247 = (bf16[8,128,1024]{2,1,0:T(8,128)(2,1)}, f32[128,1024]{1,0:T(8,128)}, f32[1,1024]{1,0:T(1,128)}, bf16[2,8,64,768]{3,2,1,0:T(8,128)(2,1)}, bf16[2...) custom-call(bf16[8,128,1024]{2,1,0:T(8,128)(2,1)} %get-tuple-element.50.part, ...), custom_call_target="tpu_custom_call" | custom-call | tf_op jit(solution)/shard_map/pallas_call | solution.py:381
  135.5 93.8 %shard_map.248 = (bf16[128,1024]{1,0:T(8,128)(2,1)}, f32[128,1024]{1,0:T(8,128)}, f32[1,2304]{1,0:T(1,128)}, bf16[8,64,512]{2,1,0:T(8,128)(2,1)}, bf16[8,16,1024...) custom-call(bf16[8,128,1024]{2,1,0:T(8,128)(2,1)} %get-tuple-element.55.ga_all, ...), custom_call_target="tpu_custom_call" | custom-call | tf_op jit(solution)/shard_map/pallas_call | solution.py:381
  229.3 3.9 %shard_map.249 = (bf16[128,1024]{1,0:T(8,128)(2,1)}, f32[128,1024]{1,0:T(8,128)}, f32[64,2048]{1,0:T(8,128)}, f32[64,1024]{1,0:T(8,128)}, f32[64,1024]{1,0:T(8,1...) custom-call(bf16[128,1024]{1,0:T(8,128)(2,1)} %get-tuple-element.71.out_h, ...), custom_call_target="tpu_custom_call" | custom-call | tf_op jit(solution)/shard_map/pallas_call | solution.py:969
  233.3 1.3 fusion.2
  234.5 1.2 fusion.3
  (2 shorter events, 0.0 us)

commit v9 on v8

--- a/solution.py
+++ b/solution.py
@@ -764,8 +764,8 @@
         for n in (3, 2, 1, 0):
             for h in range(2):
                 attend_back(h, n, n == 3 and h == 0)
-            if n:
-                yield
+                if n:
+                    yield
         for m in range(2):
             here = slice(4 * m, 4 * m + 4)
             span = slice(512 * m, 512 * (m + 1))

time: 236 us -> 247 us (1.047)
  Pallas kernels: 231 us -> 242 us
    pallas_call x3, Pallas kernels: 227 us -> 238 us  [remote_call(): pl.pallas_call(body, out_shape=[jax.ShapeDtypeStruct(s, d) for s, d, _ in...]
where the time goes in v9:
time: 247 us
  Pallas kernels  242 us (98%)
  local copies, waits for them, and re-layouts  2.57 us (1%)
    pallas_call x3, Pallas kernels, remote_call(): pl.pallas_call(body, out_shape=[jax.ShapeDtypeStruct(s, d) for s, d, _ in...  238 us

profile of v9, /device:TPU:1, one launch (start us, length us, event | category | flops | bytes accessed | tf_op | source)
XLA Modules:
  0.0 247.1 jit_solution(11948639448461233712)
XLA Ops:
  0.7 0.8 maximum_bitcast_fusion
  1.4 0.1 pad.2.clone
  1.5 0.7 maximum_maximum_fusion.gblock
  2.2 63.8 %shard_map.246 = (bf16[8,128,1024]{2,1,0:T(8,128)(2,1)}, bf16[16,64,640]{2,1,0:T(8,128)(2,1)}, bf16[16,16,1024]{2,1,0:T(8,128)(2,1)}, bf16[16,64,768]{2,1,0:T(8,...) custom-call(bf16[128,1024]{1,0:T(8,128)(2,1)} %bitcast.20, ...), custom_call_target="tpu_custom_call" | custom-call | tf_op jit(solution)/shard_map/pallas_call | solution.py:381
  66.0 69.5 %shard_map.247 = (bf16[8,128,1024]{2,1,0:T(8,128)(2,1)}, f32[128,1024]{1,0:T(8,128)}, f32[1,1024]{1,0:T(1,128)}, bf16[2,8,64,768]{3,2,1,0:T(8,128)(2,1)}, bf16[2...) custom-call(bf16[8,128,1024]{2,1,0:T(8,128)(2,1)} %get-tuple-element.50.part, ...), custom_call_target="tpu_custom_call" | custom-call | tf_op jit(solution)/shard_map/pallas_call | solution.py:381
  135.5 105.2 %shard_map.248 = (bf16[128,1024]{1,0:T(8,128)(2,1)}, f32[128,1024]{1,0:T(8,128)}, f32[1,2304]{1,0:T(1,128)}, bf16[8,64,512]{2,1,0:T(8,128)(2,1)}, bf16[8,16,1024...) custom-call(bf16[8,128,1024]{2,1,0:T(8,128)(2,1)} %get-tuple-element.55.ga_all, ...), custom_call_target="tpu_custom_call" | custom-call | tf_op jit(solution)/shard_map/pallas_call | solution.py:381
  240.7 3.9 %shard_map.249 = (bf16[128,1024]{1,0:T(8,128)(2,1)}, f32[128,1024]{1,0:T(8,128)}, f32[64,2048]{1,0:T(8,128)}, f32[64,1024]{1,0:T(8,128)}, f32[64,1024]{1,0:T(8,1...) custom-call(bf16[128,1024]{1,0:T(8,128)(2,1)} %get-tuple-element.71.out_h, ...), custom_call_target="tpu_custom_call" | custom-call | tf_op jit(solution)/shard_map/pallas_call | solution.py:969
  244.6 1.3 fusion.2
  245.9 1.2 fusion.3
  (2 shorter events, 0.0 us)
